TPU v7x, 512 devices: a whole 4x4x16 slice. The times are simulated.
512 devices in a mesh: dp: 32 (over z, core), seq: 16 (over y, x).
Axes of the slice: x: 4, y: 4, z: 16, core: 2. Of those that a mesh axis runs over, the one named last changes fastest.
Arguments:
- features: bfloat16 [32, 3072, 1024], P('dp', 'seq'), may hold values from -18 to 18
- qkv_weight: bfloat16 [1024, 3072], P('dp'), may hold values from -1 to 1
- cotangent: bfloat16 [32, 3072, 1024], P('dp', 'seq'), may hold values from -6 to 6
- node_order: int32 [32, 3072], P('dp'), may hold values from 0 to 3071, as said below
- blocks: int32 [32, 48, 8], P('dp'), may hold values from 0 to 47, as said below
- counts: int32 [32, 48], P('dp'), may hold values from 1 to 8, as said below
Outputs:
- attended: bfloat16 [32, 3072, 1024], P('dp', 'seq')
- grad_features: bfloat16 [32, 3072, 1024], P('dp', 'seq')
- grad_weight: float32 [1024, 3072], P('dp', 'seq')
Inputs may be any that keep to these rules, and one draw needn't show every extreme that they name: Every row of node_order lists each node of the subgraph once. blocks[g, c, 0] is c, and the 8 entries of a row are distinct clusters; slots at or beyond counts[g, c] are unused. `counts`: every subgraph has a cluster with all 8 slots live.
All inputs are finite; a program needn't handle non-finite values.
Results may differ from a plain program's by a relative error of at most 0.03.
Values may be sent and summed in bfloat16 or wider, within the bound.
No kernel may reach another device: no remote copies, remote signals or barrier semaphores. Data moves between devices by JAX's collectives and lax.ppermute only.
A program may use at most 128 MiB of HBM per device.

v0:
```python
import math

import jax
import jax.numpy as jnp
from jax import lax
from jax.sharding import PartitionSpec as P

HEADS = 16
HD = 64


def attend(query, key_in, value, grad_out, blocks, counts):
    cluster_count, slot_count = blocks.shape
    node_count, head_width = query.shape
    block_rows = node_count // cluster_count
    in_group = math.gcd(cluster_count, 8)
    runs_total = cluster_count // in_group
    score_scale = 1.0 / math.sqrt(head_width)
    key_blocks = key_in.reshape(cluster_count, block_rows, head_width)
    value_blocks = value.reshape(cluster_count, block_rows, head_width)
    inputs_all = (
        query.reshape(runs_total, in_group, block_rows, head_width),
        grad_out.reshape(runs_total, in_group, block_rows, head_width),
        blocks.reshape(runs_total, in_group, slot_count),
        counts.reshape(runs_total, in_group),
    )

    def group_step(totals, inputs_now):
        grad_key, grad_value = totals
        query_block, grad_block, block_ids, live_count = inputs_now
        key_rows = key_blocks[block_ids].reshape(in_group, slot_count * block_rows, head_width)
        value_rows = value_blocks[block_ids].reshape(in_group, slot_count * block_rows, head_width)
        is_live = jnp.repeat(
            jnp.arange(slot_count)[None, :] < live_count[:, None], block_rows, axis=1
        )[:, None, :]
        scores = (
            jnp.einsum("cqe,cke->cqk", query_block, key_rows, preferred_element_type=jnp.float32)
            * score_scale
        )
        scores = jnp.where(is_live, scores, -1e30)
        row_max = jnp.max(scores, axis=-1, keepdims=True)
        raw_weights = jnp.where(is_live, jnp.exp(scores - row_max), 0.0)
        attn_weights = raw_weights / jnp.sum(raw_weights, axis=-1, keepdims=True)
        attn_low = attn_weights.astype(jnp.bfloat16)
        output_blk = jnp.einsum(
            "cqk,cke->cqe", attn_low, value_rows, preferred_element_type=jnp.float32
        ).astype(jnp.bfloat16)
        grad_weights = jnp.einsum(
            "cqe,cke->cqk", grad_block, value_rows, preferred_element_type=jnp.float32
        )
        row_dot = jnp.sum(attn_weights * grad_weights, axis=-1, keepdims=True)
        grad_scores = (attn_weights * (grad_weights - row_dot) * score_scale).astype(jnp.bfloat16)
        grad_query = jnp.einsum(
            "cqk,cke->cqe", grad_scores, key_rows, preferred_element_type=jnp.float32
        ).astype(jnp.bfloat16)
        key_terms = jnp.einsum(
            "cqk,cqe->cke", grad_scores, query_block, preferred_element_type=jnp.float32
        )
        value_terms = jnp.einsum(
            "cqk,cqe->cke", attn_low, grad_block, preferred_element_type=jnp.float32
        )
        grad_key = grad_key.at[block_ids].add(
            key_terms.reshape(in_group, slot_count, block_rows, head_width)
        )
        grad_value = grad_value.at[block_ids].add(
            value_terms.reshape(in_group, slot_count, block_rows, head_width)
        )
        return ((grad_key, grad_value), (output_blk, grad_query))

    empty_sum = jnp.zeros((cluster_count, block_rows, head_width), jnp.float32)
    (grad_key, grad_value), (output_all, grad_query) = lax.scan(
        group_step, (empty_sum, empty_sum), inputs_all
    )
    return (
        output_all.reshape(node_count, head_width),
        grad_query.reshape(node_count, head_width),
        grad_key.reshape(node_count, head_width).astype(jnp.bfloat16),
        grad_value.reshape(node_count, head_width).astype(jnp.bfloat16),
    )


def per_device(features, qkv_weight, cotangent, node_order, blocks, counts):
    local_rows = features.shape[1]
    model_width = features.shape[2]
    heads_local = HEADS // lax.axis_size("seq")
    three_width = 3 * HD
    node_feats = features[0]
    cot_heads = cotangent[0].reshape(local_rows, HEADS, HD)
    weights_all = lax.all_gather(qkv_weight, "dp", axis=0, tiled=True)
    node_all = lax.all_gather(node_feats, "seq", axis=0, tiled=True)
    node_count = node_all.shape[0]
    projected = jnp.dot(node_feats, weights_all, preferred_element_type=jnp.float32).astype(
        jnp.bfloat16
    )
    projected = projected.reshape(local_rows, HEADS, three_width)
    head_qkv, head_cot = (
        lax.all_to_all(projected, "seq", split_axis=1, concat_axis=0, tiled=True),
        lax.all_to_all(cot_heads, "seq", split_axis=1, concat_axis=0, tiled=True),
    )
    graph_order = node_order[0]
    inverse = (
        jnp.zeros((node_count,), jnp.int32)
        .at[graph_order]
        .set(jnp.arange(node_count, dtype=jnp.int32))
    )
    sorted_qkv = head_qkv[graph_order]
    sorted_cot = head_cot[graph_order]
    output_all, grad_query, grad_key, grad_value = jax.vmap(
        attend, in_axes=(1, 1, 1, 1, None, None), out_axes=1
    )(
        sorted_qkv[:, :, :HD],
        sorted_qkv[:, :, HD : 2 * HD],
        sorted_qkv[:, :, 2 * HD :],
        sorted_cot,
        blocks[0],
        counts[0],
    )
    grad_heads = jnp.concatenate([grad_query, grad_key, grad_value], axis=-1)[inverse]
    output_nodes = output_all[inverse]
    output_back, grad_back = (
        lax.all_to_all(output_nodes, "seq", split_axis=0, concat_axis=1, tiled=True),
        lax.all_to_all(grad_heads, "seq", split_axis=0, concat_axis=1, tiled=True),
    )
    attended = output_back.reshape(1, local_rows, model_width)
    grad_local = grad_back.reshape(local_rows, 3 * model_width)
    grad_feats = lax.dot_general(
        grad_local, weights_all, (((1,), (1,)), ((), ())), preferred_element_type=jnp.float32
    )
    grad_features = grad_feats.astype(jnp.bfloat16).reshape(1, local_rows, model_width)
    head_grads = grad_heads.reshape(node_count, heads_local * three_width)
    grad_weight = lax.psum_scatter(
        lax.dot_general(
            node_all, head_grads, (((0,), (0,)), ((), ())), preferred_element_type=jnp.float32
        ).astype(jnp.bfloat16),
        "dp",
        scatter_dimension=0,
        tiled=True,
    ).astype(jnp.float32)
    return (attended, grad_features, grad_weight)


def solution(mesh):
    return jax.shard_map(
        per_device,
        mesh=mesh,
        in_specs=(
            P("dp", "seq", None),
            P("dp", None),
            P("dp", "seq", None),
            P("dp", None),
            P("dp", None, None),
            P("dp", None),
        ),
        out_specs=(P("dp", "seq", None), P("dp", "seq", None), P("dp", "seq")),
        check_vma=False,
    )
```

profile of v0, /device:TPU:1, one launch (start us, length us, event | category | flops | bytes accessed | tf_op | source)
XLA Modules:
  0.0 625.8 jit_solution(6024842970168261089)
XLA Ops:
  9.9 7.6 %all-to-all-start.1 = ((bf16[192,16,64]{0,2,1:T(8,128)(2,1)}), bf16[192,16,64]{0,2,1:T(8,128)(2,1)S(1)}, u32[]{:S(2)}, u32[]{:S(2)}) async-start(bf16[192,16,64]{0,2,1:T(8,128)(2,1)} %bitcast.27), calls=%async_computation.1 | async-start | bytes 1048576 | tf_op jit(solution)/shard_map/all_to_all | solution.py:98
  19.6 73.2 %all-gather.4.cloned.1.call-done = bf16[1024,3072]{1,0:T(8,128)(2,1)} async-done(((bf16[32,3072]{1,0:T(8,128)(2,1)}), bf16[1024,3072]{1,0:T(8,128)(2,1)}) %all-gather.4.cloned.1.call-update) | async-done | bytes 6291472 | tf_op jit(solution)/shard_map/all_gather | solution.py:89
  109.5 12.0 %scatter_custom_fusion.2 = s32[3072]{0:T(1024)S(1)} fusion(s32[3072]{0:T(1024)S(1)} %bitcast.182, s32[3072]{0:T(1024)S(1)} %iota.7, s32[]{:T(128)} %copy.139), kind=kCustom, calls=%fused_computation.71 | custom fusion | bytes 12292 | tf_op jit(solution)/shard_map/scatter | solution.py:104
  121.9 11.4 %gather_fusion.3 = bf16[3072,64]{1,0:T(8,128)(2,1)} fusion(bf16[3072,64]{1,0:T(8,128)(2,1)S(1)} %bitcast.161, s32[3072]{0:T(1024)S(1)} %broadcast_clamp_fusion), kind=kCustom, calls=%fused_computation.3 | custom fusion | bytes 798720 | tf_op jit(solution)/shard_map/gather | solution.py:107
  139.1 11.1 %gather_fusion.2 = bf16[3072,192]{1,0:T(8,128)(2,1)S(1)} fusion(bf16[3072,192]{1,0:T(8,128)(2,1)S(1)} %bitcast.152, s32[3072]{0:T(1024)S(1)} %broadcast_clamp_fusion), kind=kCustom, calls=%fused_computation.2 | custom fusion | bytes 2371584 | tf_op jit(solution)/shard_map/gather | solution.py:106
  152.3 286.4 %while.16 = (s32[]{:T(128)}, f32[1,48,64,64]{3,2,1,0:T(8,128)S(1)}, f32[1,48,64,64]{3,2,1,0:T(8,128)S(1)}, bf16[6,1,8,64,64]{4,3,2,1,0:T(8,128)(2,1)}, bf16[6,1,...) while((s32[]{:T(128)}, f32[1,48,64,64]{3,2,1,0:T(8,128)S(1)}, ...), condition=%wide.region_6.7_spmd, body=%wide.region_0.6_spmd.sunk | while | flops 209000192 | bytes 36499064 | solution.py:71
  175.6 7.0 %scatter_fusion.1 = f32[48,64,64]{2,1,0:T(8,128)S(1)} fusion(f32[48,64,64]{2,1,0:T(8,128)S(1)} %bitcast.155, s32[64]{0:T(128)S(1)} %reshape.343, f32[64,64,64]{2,1,0:T(8,128)} %bitcast.163), kind=kCustom, calls=%fused_computation.7.clone.1 | custom fusion | flops 262144 | bytes 3145984 | tf_op jit(solution)/shard_map/vmap()/while/body/eval_jaxpr/scatter-add | solution.py:65
  182.6 7.0 %fusion.110 = f32[8,512,64]{2,1,0:T(8,128)} fusion(f32[8,64,512]{2,1,0:T(8,128)} %fusion.106, bf16[6,1,8,64,64]{4,3,2,1,0:T(8,128)(2,1)} %get-tuple-element.266, s32[]{:T(128)} %get-tuple-element.247, f32[8,64,512]{2,1,0:T(8,128)} %get-tuple-element.233, f32[8,64]{1,0:T(8,128)S(1)} %get-tuple-element.234), kind=kOutput, calls=%fused_computation.26.clone.1 | convolution fusion | flops 35390464 | bytes 5382656 | tf_op jit(solution)/shard_map/vmap()/while/body/eval_jaxpr/reshape | solution.py:63
  189.6 7.0 %scatter_fusion = f32[48,64,64]{2,1,0:T(8,128)S(1)} fusion(f32[48,64,64]{2,1,0:T(8,128)S(1)} %bitcast.153, s32[64]{0:T(128)S(1)} %reshape.343, f32[64,64,64]{2,1,0:T(8,128)} %bitcast.162), kind=kCustom, calls=%fused_computation.6.clone.1 | custom fusion | flops 262144 | bytes 3145984 | tf_op jit(solution)/shard_map/vmap()/while/body/eval_jaxpr/scatter-add | solution.py:62
  223.3 7.0 %scatter_fusion.1 = f32[48,64,64]{2,1,0:T(8,128)S(1)} fusion(f32[48,64,64]{2,1,0:T(8,128)S(1)} %bitcast.155, s32[64]{0:T(128)S(1)} %reshape.343, f32[64,64,64]{2,1,0:T(8,128)} %bitcast.163), kind=kCustom, calls=%fused_computation.7.clone.1 | custom fusion | flops 262144 | bytes 3145984 | tf_op jit(solution)/shard_map/vmap()/while/body/eval_jaxpr/scatter-add | solution.py:65
  230.3 7.0 %fusion.110 = f32[8,512,64]{2,1,0:T(8,128)} fusion(f32[8,64,512]{2,1,0:T(8,128)} %fusion.106, bf16[6,1,8,64,64]{4,3,2,1,0:T(8,128)(2,1)} %get-tuple-element.266, s32[]{:T(128)} %get-tuple-element.247, f32[8,64,512]{2,1,0:T(8,128)} %get-tuple-element.233, f32[8,64]{1,0:T(8,128)S(1)} %get-tuple-element.234), kind=kOutput, calls=%fused_computation.26.clone.1 | convolution fusion | flops 35390464 | bytes 5382656 | tf_op jit(solution)/shard_map/vmap()/while/body/eval_jaxpr/reshape | solution.py:63
  237.3 7.0 %scatter_fusion = f32[48,64,64]{2,1,0:T(8,128)S(1)} fusion(f32[48,64,64]{2,1,0:T(8,128)S(1)} %bitcast.153, s32[64]{0:T(128)S(1)} %reshape.343, f32[64,64,64]{2,1,0:T(8,128)} %bitcast.162), kind=kCustom, calls=%fused_computation.6.clone.1 | custom fusion | flops 262144 | bytes 3145984 | tf_op jit(solution)/shard_map/vmap()/while/body/eval_jaxpr/scatter-add | solution.py:62
  278.0 7.0 %fusion.110 = f32[8,512,64]{2,1,0:T(8,128)} fusion(f32[8,64,512]{2,1,0:T(8,128)} %fusion.106, bf16[6,1,8,64,64]{4,3,2,1,0:T(8,128)(2,1)} %get-tuple-element.266, s32[]{:T(128)} %get-tuple-element.247, f32[8,64,512]{2,1,0:T(8,128)} %get-tuple-element.233, f32[8,64]{1,0:T(8,128)S(1)} %get-tuple-element.234), kind=kOutput, calls=%fused_computation.26.clone.1 | convolution fusion | flops 35390464 | bytes 5382656 | tf_op jit(solution)/shard_map/vmap()/while/body/eval_jaxpr/reshape | solution.py:63
  318.7 7.0 %scatter_fusion.1 = f32[48,64,64]{2,1,0:T(8,128)S(1)} fusion(f32[48,64,64]{2,1,0:T(8,128)S(1)} %bitcast.155, s32[64]{0:T(128)S(1)} %reshape.343, f32[64,64,64]{2,1,0:T(8,128)} %bitcast.163), kind=kCustom, calls=%fused_computation.7.clone.1 | custom fusion | flops 262144 | bytes 3145984 | tf_op jit(solution)/shard_map/vmap()/while/body/eval_jaxpr/scatter-add | solution.py:65
  325.7 7.0 %fusion.110 = f32[8,512,64]{2,1,0:T(8,128)} fusion(f32[8,64,512]{2,1,0:T(8,128)} %fusion.106, bf16[6,1,8,64,64]{4,3,2,1,0:T(8,128)(2,1)} %get-tuple-element.266, s32[]{:T(128)} %get-tuple-element.247, f32[8,64,512]{2,1,0:T(8,128)} %get-tuple-element.233, f32[8,64]{1,0:T(8,128)S(1)} %get-tuple-element.234), kind=kOutput, calls=%fused_computation.26.clone.1 | convolution fusion | flops 35390464 | bytes 5382656 | tf_op jit(solution)/shard_map/vmap()/while/body/eval_jaxpr/reshape | solution.py:63
  332.7 7.0 %scatter_fusion = f32[48,64,64]{2,1,0:T(8,128)S(1)} fusion(f32[48,64,64]{2,1,0:T(8,128)S(1)} %bitcast.153, s32[64]{0:T(128)S(1)} %reshape.343, f32[64,64,64]{2,1,0:T(8,128)} %bitcast.162), kind=kCustom, calls=%fused_computation.6.clone.1 | custom fusion | flops 262144 | bytes 3145984 | tf_op jit(solution)/shard_map/vmap()/while/body/eval_jaxpr/scatter-add | solution.py:62
  373.4 7.0 %fusion.110 = f32[8,512,64]{2,1,0:T(8,128)} fusion(f32[8,64,512]{2,1,0:T(8,128)} %fusion.106, bf16[6,1,8,64,64]{4,3,2,1,0:T(8,128)(2,1)} %get-tuple-element.266, s32[]{:T(128)} %get-tuple-element.247, f32[8,64,512]{2,1,0:T(8,128)} %get-tuple-element.233, f32[8,64]{1,0:T(8,128)S(1)} %get-tuple-element.234), kind=kOutput, calls=%fused_computation.26.clone.1 | convolution fusion | flops 35390464 | bytes 5382656 | tf_op jit(solution)/shard_map/vmap()/while/body/eval_jaxpr/reshape | solution.py:63
  414.1 7.0 %scatter_fusion.1 = f32[48,64,64]{2,1,0:T(8,128)S(1)} fusion(f32[48,64,64]{2,1,0:T(8,128)S(1)} %bitcast.155, s32[64]{0:T(128)S(1)} %reshape.343, f32[64,64,64]{2,1,0:T(8,128)} %bitcast.163), kind=kCustom, calls=%fused_computation.7.clone.1 | custom fusion | flops 262144 | bytes 3145984 | tf_op jit(solution)/shard_map/vmap()/while/body/eval_jaxpr/scatter-add | solution.py:65
  421.1 7.0 %fusion.110 = f32[8,512,64]{2,1,0:T(8,128)} fusion(f32[8,64,512]{2,1,0:T(8,128)} %fusion.106, bf16[6,1,8,64,64]{4,3,2,1,0:T(8,128)(2,1)} %get-tuple-element.266, s32[]{:T(128)} %get-tuple-element.247, f32[8,64,512]{2,1,0:T(8,128)} %get-tuple-element.233, f32[8,64]{1,0:T(8,128)S(1)} %get-tuple-element.234), kind=kOutput, calls=%fused_computation.26.clone.1 | convolution fusion | flops 35390464 | bytes 5382656 | tf_op jit(solution)/shard_map/vmap()/while/body/eval_jaxpr/reshape | solution.py:63
  428.2 7.0 %scatter_fusion = f32[48,64,64]{2,1,0:T(8,128)S(1)} fusion(f32[48,64,64]{2,1,0:T(8,128)S(1)} %bitcast.153, s32[64]{0:T(128)S(1)} %reshape.343, f32[64,64,64]{2,1,0:T(8,128)} %bitcast.162), kind=kCustom, calls=%fused_computation.6.clone.1 | custom fusion | flops 262144 | bytes 3145984 | tf_op jit(solution)/shard_map/vmap()/while/body/eval_jaxpr/scatter-add | solution.py:62
  440.9 9.2 %gather_fusion.4 = bf16[3072,64]{1,0:T(8,128)(2,1)S(1)} fusion(bf16[3072,64]{1,0:T(8,128)(2,1)S(1)} %bitcast.164, s32[3072]{0:T(1024)S(1)} %fusion.52), kind=kCustom, calls=%fused_computation.4 | custom fusion | bytes 798720 | tf_op jit(solution)/shard_map/gather | solution.py:119
  459.0 11.1 %gather_fusion.5 = bf16[3072,192]{1,0:T(8,128)(2,1)S(1)} fusion(bf16[3072,192]{1,0:T(8,128)(2,1)S(1)} %maximum_bitcast_fusion, s32[3072]{0:T(1024)S(1)} %fusion.52), kind=kCustom, calls=%fused_computation.5 | custom fusion | bytes 2371584 | tf_op jit(solution)/shard_map/gather | solution.py:118
  490.1 100.3 %reduce-scatter.4.cloned.1.call-done = bf16[32,192]{1,0:T(8,128)(2,1)} async-done(((bf16[1024,192]{1,0:T(8,128)(2,1)}), bf16[32,192]{1,0:T(8,128)(2,1)}) %reduce-scatter.4.cloned.1.call-update) | async-done | bytes 12304
  592.0 8.4 %reshape.325 = bf16[3072,1,192]{2,1,0:T(2,128)(2,1)S(1)} reshape(bf16[16,2,18432]{2,1,0:T(2,128)(2,1)} %all-to-all-done.3) | data formatting | bytes 2359296
  (172 shorter events, 269.3 us)
Async XLA Ops:
  7.2 85.6 %copy-start.3 = (bf16[1,192,1024]{2,1,0:T(8,128)(2,1)S(1)}, bf16[1,192,1024]{2,1,0:T(8,128)(2,1)}, u32[]{:S(2)}) copy-start(bf16[1,192,1024]{2,1,0:T(8,128)(2,1)} %param.8) | copy-start | bytes 1179652
  7.2 11.1 %copy-start.5 = (s32[1,48,8]{1,2,0:T(8,128)S(1)}, s32[1,48,8]{1,2,0:T(8,128)}, u32[]{:S(2)}) copy-start(s32[1,48,8]{1,2,0:T(8,128)} %param.12) | copy-start | bytes 4612
  7.2 11.7 %copy-start.6 = (s32[1,48]{1,0:T(1,128)S(1)}, s32[1,48]{1,0:T(1,128)}, u32[]{:S(2)}) copy-start(s32[1,48]{1,0:T(1,128)} %param.13) | copy-start | bytes 580
  7.2 85.6 %all-gather.4.cloned.1.call-start = ((), (), s32[]{:S(2)}) async-start(), calls=%async_computation.5 | async-start | bytes 6488064 | tf_op jit(solution)/shard_map/all_gather | solution.py:89
  9.9 92.9 %all-to-all-start.1 = ((bf16[192,16,64]{0,2,1:T(8,128)(2,1)}), bf16[192,16,64]{0,2,1:T(8,128)(2,1)S(1)}, u32[]{:S(2)}, u32[]{:S(2)}) async-start(bf16[192,16,64]{0,2,1:T(8,128)(2,1)} %bitcast.27), calls=%async_computation.1 | async-start | bytes 1048576 | tf_op jit(solution)/shard_map/all_to_all | solution.py:98
  17.5 463.3 %all-gather.6.cloned.1.call-start = ((), (), s32[]{:S(2)}) async-start(), calls=%async_computation.6 | async-start | bytes 6684672 | tf_op jit(solution)/shard_map/all_gather | solution.py:90
  102.8 6.7 %copy-start.4 = (s32[1,3072]{1,0:T(1,128)S(1)}, s32[1,3072]{1,0:T(1,128)}, u32[]{:S(2)}) copy-start(s32[1,3072]{1,0:T(1,128)} %param.11) | copy-start | bytes 36868
  102.8 36.2 %all-to-all-start = ((bf16[192,16,192]{2,0,1:T(8,128)(2,1)}), bf16[192,16,192]{2,0,1:T(8,128)(2,1)S(1)}, u32[]{:S(2)}, u32[]{:S(2)}) async-start(bf16[192,16,192]{2,0,1:T(8,128)(2,1)} %copy.93), calls=%async_computation | async-start | bytes 3145728 | tf_op jit(solution)/shard_map/all_to_all | solution.py:97
  157.3 1.0 copy-start
  205.1 1.0 copy-start
  252.9 1.0 copy-start
  300.6 1.0 copy-start
  348.3 1.0 copy-start
  396.0 1.0 copy-start
  439.7 1.1 copy-start.1
  450.5 6.6 %copy-start.2 = (bf16[1,48,64,64]{3,2,1,0:T(8,128)(2,1)S(1)}, bf16[1,48,64,64]{3,2,1,0:T(8,128)(2,1)}, u32[]{:S(2)}) copy-start(bf16[1,48,64,64]{3,2,1,0:T(8,128)(2,1)} %convert_element_type.62) | copy-start | bytes 1179652
  453.3 21.0 %all-to-all-start.2 = ((bf16[16,2,6144]{2,1,0:T(2,128)(2,1)}), bf16[16,2,6144]{2,1,0:T(2,128)(2,1)S(1)}, u32[]{:S(2)}, u32[]{:S(2)}) async-start(bf16[16,2,6144]{2,1,0:T(2,128)(2,1)} %reshape.322), calls=%async_computation.2 | async-start | bytes 786432 | tf_op jit(solution)/shard_map/all_to_all | solution.py:121
  474.4 117.6 %all-to-all-start.3 = ((bf16[16,2,18432]{2,1,0:T(2,128)(2,1)}), bf16[16,2,18432]{2,1,0:T(2,128)(2,1)}, u32[]{:S(2)}, u32[]{:S(2)}) async-start(bf16[16,2,18432]{2,1,0:T(2,128)(2,1)} %reshape.324), calls=%async_computation.3 | async-start | bytes 2359296 | tf_op jit(solution)/shard_map/all_to_all | solution.py:122
  480.8 109.7 %reduce-scatter.4.cloned.1.call-start = ((), (), s32[]{:S(2)}) async-start(), calls=%async_computation.7 | async-start | bytes 540672
Sparse Core Ops, SparseCore 0:
  10.2 82.6 all-gather.3
  95.8 83.5 all-gather.5
  486.2 104.1 reduce-scatter.3
where the time goes:
time: 633 us; the launch traced here: 626 us
  waiting for transfers between devices  181 us (29%)
  matrix products  168 us (27%)
  local copies, waits for them, and re-layouts  140 us (22%)
  other arithmetic  99 us (16%)
  starting transfers between devices  24.6 us (4%)
  between operations  14 us (2%)
    unnamed x4, waiting for transfers between devices  102 us
    all_gather x1, waiting for transfers between devices, per_device(): weights_all = lax.all_gather(qkv_weight, 'dp', axis=0, tiled=True)  73.2 us
    reshape x6, matrix products, group_step(): key_terms.reshape(in_group, slot_count, block_rows, head_width)  42.2 us
    scatter-add x6, other arithmetic, group_step(): grad_key.at[block_ids]  42 us
    scatter-add x6, other arithmetic, group_step(): grad_value.at[block_ids]  42 us
    dot_general x6, matrix products, group_step(): jnp.einsum('cqk,cke->cqe', grad_scores, key_rows, preferred_element_type=...  36 us
    reshape x6, matrix products, group_step(): value_terms.reshape(in_group, slot_count, block_rows, head_width)  25.8 us
    dot_general x6, matrix products, group_step(): jnp.einsum('cqk,cke->cqe', attn_low, value_rows, preferred_element_type=j...  21 us
  transfers between devices with their start and end apart: 7, of which 3 were waited for; matrix products, arithmetic and copies ran while one was open for 59% of the time, Pallas kernels for 0%

commit v1 on v0

v1 whole, which is shorter than its diff:
```python
import jax
import jax.numpy as jnp
from jax import lax
from jax.experimental import pallas as pl
from jax.experimental.pallas import tpu as pltpu
from jax.sharding import PartitionSpec as P

HEADS = 16
HD = 64
BF = jnp.bfloat16
F32 = jnp.float32
ROWS = 256


def dot(a, b, ca=1, cb=0):
    return lax.dot_general(a, b, (((ca,), (cb,)), ((), ())), preferred_element_type=F32)


def attend_kernel(
    blocks_ref, counts_ref, feat_ref, w_ref, cot_ref, ocol_ref, orow_ref,
    out_ref, x_ref, kv_ref, a_ref, acc_ref, g_ref,
):
    nodes = feat_ref.shape[0]
    clusters, slots = blocks_ref.shape
    rows = nodes // clusters
    keys = slots * rows
    tiles = nodes // ROWS
    place = (
        lax.broadcasted_iota(jnp.int32, (HD, 4 * HD), 0) + 3 * HD
        == lax.broadcasted_iota(jnp.int32, (HD, 4 * HD), 1)
    ).astype(F32).astype(BF)

    def project(i, carry):
        r = pl.ds(pl.multiple_of(i * ROWS, ROWS), ROWS)
        x = dot(feat_ref[r, :], w_ref[...]) + dot(cot_ref[r, :], place)
        x_ref[r, :] = x.astype(BF)
        return carry

    lax.fori_loop(0, tiles, project, 0, unroll=2)

    first = lax.broadcasted_iota(jnp.int32, (rows, 2 * HD), 1) < HD

    def to_clusters(i, carry):
        r = pl.ds(pl.multiple_of(i * ROWS, ROWS), ROWS)
        pick = ocol_ref[r, :] == lax.broadcasted_iota(jnp.int32, (ROWS, nodes), 1)
        moved = dot(pick.astype(F32).astype(BF), x_ref[...])
        kv_ref[r, :] = moved[:, : 2 * HD].astype(BF)
        for t in range(ROWS // rows):
            qd = moved[t * rows : (t + 1) * rows, 2 * HD :]
            base = pl.multiple_of(i * 2 * ROWS + 2 * rows * t, 2 * rows)
            a_ref[pl.ds(base, rows), :] = jnp.where(first, qd, 0.0).astype(BF)
            a_ref[pl.ds(base + rows, rows), :] = jnp.where(first, 0.0, qd).astype(BF)
        return carry

    lax.fori_loop(0, tiles, to_clusters, 0, unroll=1)

    acc_ref[...] = jnp.zeros_like(acc_ref)
    key_at = lax.broadcasted_iota(jnp.int32, (rows, keys), 1)

    def cluster(c):
        at = [
            pl.ds(pl.multiple_of(blocks_ref[c, j] * rows, rows), rows)
            for j in range(slots)
        ]
        kv = jnp.concatenate([kv_ref[s, :] for s in at], axis=0)
        a = a_ref[pl.ds(pl.multiple_of(c * 2 * rows, 2 * rows), 2 * rows), :]
        both = dot(a, kv, 1, 1)
        score = jnp.where(key_at < counts_ref[c] * rows, both[:rows], -1e30)
        dpw = both[rows:]
        raw = jnp.exp(score - jnp.max(score, axis=1, keepdims=True))
        p = raw * (1.0 / jnp.sum(raw, axis=1, keepdims=True))
        ds = p * (dpw - jnp.sum(p * dpw, axis=1, keepdims=True))
        pd = jnp.concatenate([ds, p], axis=0).astype(BF)
        oq = dot(pd, kv)
        back = dot(pd, a, 0, 0)
        here = pl.ds(pl.multiple_of(c * rows, rows), rows)
        g_ref[here, 2 * HD :] = jnp.where(first, oq[:rows] * 0.125, oq[rows:]).astype(BF)
        return at, back

    def step(i, carry):
        for c in (2 * i, 2 * i + 1):
            at, back = cluster(c)
            new = [
                acc_ref[s, :] + back[j * rows : (j + 1) * rows]
                for j, s in enumerate(at)
            ]
            for s, v in zip(at, new):
                acc_ref[s, :] = v
        return carry

    lax.fori_loop(0, clusters // 2, step, 0)
    g_ref[:, : 2 * HD] = acc_ref[...].astype(BF)

    def to_nodes(i, carry):
        r = pl.ds(pl.multiple_of(i * ROWS, ROWS), ROWS)
        pick = orow_ref[...] == lax.broadcasted_iota(jnp.int32, (ROWS, nodes), 0) + i * ROWS
        out_ref[r, :] = dot(pick.astype(F32).astype(BF), g_ref[...]).astype(BF)
        return carry

    lax.fori_loop(0, tiles, to_nodes, 0, unroll=1)


def attend(feats, w_head, cot, order, blocks, counts):
    nodes = feats.shape[0]
    vmem = pl.BlockSpec(memory_space=pltpu.VMEM)
    smem = pl.BlockSpec(memory_space=pltpu.SMEM)
    return pl.pallas_call(
        attend_kernel,
        name="attend",
        out_shape=jax.ShapeDtypeStruct((nodes, 4 * HD), BF),
        in_specs=[smem, smem] + [vmem] * 5,
        out_specs=vmem,
        scratch_shapes=[
            pltpu.VMEM((nodes, 4 * HD), BF),
            pltpu.VMEM((nodes, 2 * HD), BF),
            pltpu.VMEM((2 * nodes, 2 * HD), BF),
            pltpu.VMEM((nodes, 2 * HD), F32),
            pltpu.VMEM((nodes, 4 * HD), BF),
        ],
        compiler_params=pltpu.CompilerParams(vmem_limit_bytes=50 << 20),
    )(blocks, counts, feats, w_head, cot, order.reshape(nodes, 1), order.reshape(1, nodes))


def finish_kernel(g_ref, w_ref, att_ref, gf_ref, lhs_ref):
    heads = g_ref.shape[0]
    wide = heads * 2 * HD
    first = lax.broadcasted_iota(jnp.int32, (g_ref.shape[1], 2 * HD), 1) < HD
    for h in range(0, heads, 2):
        lhs_ref[:, h * 2 * HD : (h + 1) * 2 * HD] = g_ref[h, :, : 2 * HD]
        lhs_ref[:, (h + 1) * 2 * HD : (h + 2) * 2 * HD] = g_ref[h + 1, :, : 2 * HD]
        even = g_ref[h, :, 2 * HD :].astype(F32)
        odd = g_ref[h + 1, :, 2 * HD :].astype(F32)
        to = slice(h * HD, (h + 2) * HD)
        lhs_ref[:, wide + h * HD : wide + (h + 2) * HD] = jnp.where(
            first, even, pltpu.roll(odd, HD, 1)
        ).astype(BF)
        att_ref[:, to] = jnp.where(first, pltpu.roll(even, HD, 1), odd).astype(BF)
    gf_ref[...] = dot(lhs_ref[...], w_ref[...], 1, 1).astype(BF)


def finish(got, weights):
    rows, width = got.shape[1], weights.shape[0]
    vmem = pl.BlockSpec(memory_space=pltpu.VMEM)
    return pl.pallas_call(
        finish_kernel,
        name="finish",
        out_shape=[
            jax.ShapeDtypeStruct((rows, HEADS * HD), BF),
            jax.ShapeDtypeStruct((rows, width), BF),
        ],
        in_specs=[vmem, vmem],
        out_specs=[vmem, vmem],
        scratch_shapes=[pltpu.VMEM((rows, weights.shape[1]), BF)],
        compiler_params=pltpu.CompilerParams(vmem_limit_bytes=40 << 20),
    )(got, weights)


def per_device(features, qkv_weight, cotangent, node_order, blocks, counts):
    local_rows = features.shape[1]
    model_width = features.shape[2]
    deep = qkv_weight.shape[0]
    feats = features[0]
    head = lax.axis_index("seq")
    own = lax.dynamic_slice(qkv_weight, (0, head * 3 * HD), (deep, 3 * HD))
    own = jnp.concatenate(
        [own[:, HD:], own[:, :HD] * jnp.asarray(0.125, BF), jnp.zeros((deep, HD), BF)],
        axis=1,
    )
    w_head = lax.all_gather(own, "dp", axis=0, tiled=True)
    node_all = lax.all_gather(feats, "seq", axis=0, tiled=True)
    cot = lax.all_to_all(
        cotangent[0].reshape(local_rows, HEADS, HD).transpose(1, 0, 2), "seq", 0, 0, tiled=True
    ).reshape(HEADS * local_rows, HD)
    by_head = qkv_weight.reshape(deep, HEADS, 3 * HD)
    ordered = jnp.concatenate(
        [by_head[:, :, HD:].reshape(deep, -1), by_head[:, :, :HD].reshape(deep, -1)], axis=1
    )
    weights = lax.all_gather(ordered, "dp", axis=0, tiled=True)
    grads = attend(node_all, w_head, cot, node_order[0], blocks[0], counts[0])
    got = lax.all_to_all(grads.reshape(HEADS, local_rows, 4 * HD), "seq", 0, 0, tiled=True)
    part = lax.dot_general(
        node_all, grads[:, : 3 * HD], (((0,), (0,)), ((), ())), preferred_element_type=F32
    ).astype(BF)
    parts = lax.all_to_all(part.reshape(-1, deep, 3 * HD), "dp", 0, 0, tiled=True)
    total = jnp.sum(parts.astype(F32), axis=0)
    grad_weight = jnp.concatenate([total[:, 2 * HD :], total[:, : 2 * HD]], axis=1)
    attended, grad_feats = finish(got, weights)
    return (
        attended.reshape(1, local_rows, model_width),
        grad_feats.reshape(1, local_rows, model_width),
        grad_weight,
    )


def solution(mesh):
    return jax.shard_map(
        per_device,
        mesh=mesh,
        in_specs=(
            P("dp", "seq", None),
            P("dp", None),
            P("dp", "seq", None),
            P("dp", None),
            P("dp", None, None),
            P("dp", None),
        ),
        out_specs=(P("dp", "seq", None), P("dp", "seq", None), P("dp", "seq")),
        check_vma=False,
    )
```

time: 633 us -> 227 us (0.36); the launches traced: 626 us -> 227 us
  matrix products: 168 us -> 4.77 us
  local copies, waits for them, and re-layouts: 140 us -> 9.42 us
  waiting for transfers between devices: 181 us -> 77.3 us
  other arithmetic: 99 us -> 2.27 us
  Pallas kernels: 0 us -> 52.8 us
  blocking collectives: 0 us -> 38.5 us
    unnamed x4 -> x2, waiting for transfers between devices: 102 us -> 0.7 us
    dot_general x27 -> x1, matrix products: 99.9 us -> 4.77 us  [per_device(): lax.dot_general(node_all, grads[:, :3 * HD], (((0,), (0,)), ((), ())), pr...]
    scatter-add x12 -> x0, other arithmetic: 84 us -> none  [the longest x6 42 us: group_step(): grad_key.at[block_ids]]
    gather x17 -> x0, local copies, waits for them, and re-layouts: 77.2 us -> none  [the longest x6 17.2 us: group_step(): key_blocks[block_ids].reshape(in_group, slot_count * block_rows, head_width)]
    reshape x12 -> x0, matrix products: 68 us -> none  [the longest x6 42.2 us: group_step(): key_terms.reshape(in_group, slot_count, block_rows, head_width)]
    pallas_call x0 -> x2, Pallas kernels: none -> 52.8 us  [the longest x1 49.8 us: attend(): pl.pallas_call(attend_kernel, name='attend', out_shape=jax.ShapeDtypeStru...]
    all_gather x2, waiting for transfers between devices: 73.2 us -> 31.8 us  [the longest x1 31.8 us: per_device(): node_all = lax.all_gather(feats, 'seq', axis=0, tiled=True)]
    all_to_all x4 -> x3, waiting for transfers between devices: 5.72 us -> 44.7 us  [the longest x1 27.6 us: per_device(): lax.all_to_all(part.reshape(-1, deep, 3 * HD), 'dp', 0, 0, tiled=True)]
  transfers between devices with their start and end apart: 7 -> 5, of which waited for: 3 -> 3; matrix products, arithmetic and copies ran while one was open for 59% -> 6% of each run, Pallas kernels for 0% -> 23%
where the time goes in v1:
time: 227 us
  waiting for transfers between devices  77.3 us (34%)
  Pallas kernels  52.8 us (23%)
  blocking collectives  38.5 us (17%)
  starting transfers between devices  27.5 us (12%)
  between operations  14.2 us (6%)
  local copies, waits for them, and re-layouts  9.42 us (4%)
  matrix products  4.77 us (2%)
  other arithmetic  2.27 us (1%)
    pallas_call x1, Pallas kernels, attend(): pl.pallas_call(attend_kernel, name='attend', out_shape=jax.ShapeDtypeStru...  49.8 us
    all_gather x1, blocking collectives, per_device(): w_head = lax.all_gather(own, 'dp', axis=0, tiled=True)  38.5 us
    all_gather x1, waiting for transfers between devices, per_device(): node_all = lax.all_gather(feats, 'seq', axis=0, tiled=True)  31.8 us
    all_to_all x1, waiting for transfers between devices, per_device(): lax.all_to_all(part.reshape(-1, deep, 3 * HD), 'dp', 0, 0, tiled=True)  27.6 us
    all_to_all x1, waiting for transfers between devices, per_device(): lax.all_to_all(grads.reshape(HEADS, local_rows, 4 * HD), 'seq', 0, 0, til...  17.1 us
    all_to_all x1, starting transfers between devices, per_device(): lax.all_to_all(part.reshape(-1, deep, 3 * HD), 'dp', 0, 0, tiled=True)  14.9 us
    all_to_all x1, starting transfers between devices, per_device(): lax.all_to_all(cotangent[0].reshape(local_rows, HEADS, HD).transpose(1, 0...  7.58 us
    all_to_all x1, starting transfers between devices, per_device(): lax.all_to_all(grads.reshape(HEADS, local_rows, 4 * HD), 'seq', 0, 0, til...  4.97 us
  transfers between devices with their start and end apart: 5, of which 3 were waited for; matrix products, arithmetic and copies ran while one was open for 6% of the time, Pallas kernels for 23%

profile of v1, /device:TPU:1, one launch (start us, length us, event | category | flops | bytes accessed | tf_op | source)
XLA Modules:
  0.0 226.7 jit_solution(6681347716146347874)
XLA Ops:
  7.2 0.7 all-gather.6.cloned.1.call-update
  8.0 1.3 reshape.32
  9.2 0.1 slice.28
  9.4 0.1 reshape.34
  9.6 0.7 pad_maximum_fusion
  10.3 1.0 copy.12
  11.3 7.6 %all-to-all-start = ((bf16[16,192,64]{1,2,0:T(8,128)(2,1)}), bf16[16,192,64]{1,2,0:T(8,128)(2,1)S(1)}, u32[]{:S(2)}, u32[]{:S(2)}) async-start(bf16[16,192,64]{1,2,0:T(8,128)(2,1)} %bitcast.4), calls=%async_computation | async-start | bytes 1048576 | tf_op jit(solution)/shard_map/all_to_all | solution.py:171
  18.9 1.7 copy.14.ocol_ref
  20.8 0.8 dynamic-slice_multiply_fusion
  21.6 0.8 constant_dynamic-slice_fusion
  22.4 38.5 %all_gather.10.w_ref = bf16[1024,256]{1,0:T(8,128)(2,1)S(1)} all-gather(bf16[32,256]{1,0:T(8,128)(2,1)S(1)} %maximum_maximum_fusion), channel_id=1, replica_groups=mesh['dp'=32,'seq'=16] {'dp'}, dimensions={0}, use_global_device_ids=true | all-gather | bytes 540672 | tf_op jit(solution)/shard_map/all_gather | solution.py:169
  60.8 0.4 copy.13
  61.2 31.8 %all-gather.6.cloned.1.call-done = bf16[1,3072,1024]{2,1,0:T(8,128)(2,1)} async-done(((bf16[1,192,1024]{2,1,0:T(8,128)(2,1)}), bf16[1,3072,1024]{2,1,0:T(8,128)(2,1)}) %all-gather.6.cloned.1.call-update) | async-done | bytes 6291472 | tf_op jit(solution)/shard_map/all_gather | solution.py:170
  93.0 49.8 %attend.1 = bf16[3072,256]{1,0:T(8,128)(2,1)} custom-call(s32[48,8]{1,0:T(8,128)S(1)} %bitcast.21, s32[48]{0:T(128)S(1)} %bitcast.23, bf16[3072,1024]{1,0:T(8,128)(2,1)} %bitcast.24, bf16[1024,256]{1,0:T(8,128)(2,1)S(1)} %all_gather.10.w_ref, bf16[3072,64]{1,0:T(8,128)(2,1)S(1)} %bitcast.20, s32[3072,1]{1,0:T(8,128)} %copy.14.ocol_ref, s32[1,3072]{1,0:T(1,128)S(1)} %copy-done.1), custom_call_target="tpu_custom_call" | custom-call | tf_op jit(solution)/shard_map/attend/pallas_call | solution.py:107
  142.8 5.0 %all-to-all-start.1 = ((bf16[16,192,256]{2,1,0:T(8,128)(2,1)}), bf16[16,192,256]{2,1,0:T(8,128)(2,1)S(1)}, u32[]{:S(2)}, u32[]{:S(2)}) async-start(bf16[16,192,256]{2,1,0:T(8,128)(2,1)} %bitcast.7), calls=%async_computation.1 | async-start | bytes 3145728 | tf_op jit(solution)/shard_map/all_to_all | solution.py:180
  147.8 4.8 %fusion.5 = bf16[1024,192]{0,1:T(8,128)(2,1)S(1)} fusion(bf16[3072,256]{1,0:T(8,128)(2,1)} %attend.1, bf16[1,3072,1024]{2,1,0:T(8,128)(2,1)} %all-gather.6.cloned.1.call-done), kind=kOutput, calls=%fused_computation.3 | convolution fusion | flops 1208156160 | bytes 8257536 | tf_op jit(solution)/shard_map/dot_general | solution.py:181
  152.5 1.0 copy.15
  153.5 17.1 %all-to-all-done.1.g_ref = bf16[16,192,256]{2,1,0:T(8,128)(2,1)S(1)} async-done(((bf16[16,192,256]{2,1,0:T(8,128)(2,1)}), bf16[16,192,256]{2,1,0:T(8,128)(2,1)S(1)}, u32[]{:S(2)}, u32[]{:S(2)}) %all-to-all-start.1) | async-done | bytes 1572896 | tf_op jit(solution)/shard_map/all_to_all | solution.py:180
  170.6 14.9 %all-to-all-start.2 = ((bf16[32,32,192]{2,1,0:T(8,128)(2,1)}), bf16[32,32,192]{2,1,0:T(8,128)(2,1)S(1)}, u32[]{:S(2)}, u32[]{:S(2)}) async-start(bf16[32,32,192]{2,1,0:T(8,128)(2,1)} %bitcast.11), calls=%async_computation.2 | async-start | bytes 1048576 | tf_op jit(solution)/shard_map/all_to_all | solution.py:184
  185.6 2.8 %copy-done = bf16[1024,3072]{1,0:T(8,128)(2,1)S(1)} copy-done((bf16[1024,3072]{1,0:T(8,128)(2,1)S(1)}, bf16[1024,3072]{1,0:T(8,128)(2,1)}, u32[]{:S(2)}) %copy-start) | copy-done | bytes 6291480
  188.3 3.1 %finish.1 = (bf16[192,1024]{1,0:T(8,128)(2,1)}, bf16[192,1024]{1,0:T(8,128)(2,1)}) custom-call(bf16[16,192,256]{2,1,0:T(8,128)(2,1)S(1)} %all-to-all-done.1.g_ref, bf16[1024,3072]{1,0:T(8,128)(2,1)S(1)} %copy-done), custom_call_target="tpu_custom_call" | custom-call | tf_op jit(solution)/shard_map/finish/pallas_call | solution.py:144
  191.4 27.6 %all-to-all-done.2 = bf16[32,32,192]{2,1,0:T(8,128)(2,1)S(1)} async-done(((bf16[32,32,192]{2,1,0:T(8,128)(2,1)}), bf16[32,32,192]{2,1,0:T(8,128)(2,1)S(1)}, u32[]{:S(2)}, u32[]{:S(2)}) %all-to-all-start.2) | async-done | bytes 393248 | tf_op jit(solution)/shard_map/all_to_all | solution.py:184
  219.0 0.1 convert_reduce_fusion
  219.2 0.7 pad_maximum_fusion.1
  (22 shorter events, 0.4 us)
Async XLA Ops:
  7.2 3.1 %copy-start.3 = (bf16[1,192,1024]{2,1,0:T(8,128)(2,1)S(1)}, bf16[1,192,1024]{2,1,0:T(8,128)(2,1)}, u32[]{:S(2)}) copy-start(bf16[1,192,1024]{2,1,0:T(8,128)(2,1)} %param.8) | copy-start | bytes 1179652
  7.2 85.8 %all-gather.6.cloned.1.call-start = ((), (), s32[]{:S(2)}) async-start(), calls=%async_computation.4 | async-start | bytes 6684672 | tf_op jit(solution)/shard_map/all_gather | solution.py:170
  7.9 177.6 %all-gather.4.cloned.1.call-start = ((), (), s32[]{:S(2)}) async-start(), calls=%async_computation.3 | async-start | bytes 6488064 | tf_op jit(solution)/shard_map/all_gather | solution.py:178
  9.4 9.6 %copy-start.1 = (s32[1,3072]{1,0:T(1,128)S(1)}, s32[1,3072]{1,0:T(1,128)}, u32[]{:S(2)}) copy-start(s32[1,3072]{1,0:T(1,128)} %orow_ref.1) | copy-start | bytes 36868
  10.3 10.3 %copy-start.4 = (s32[1,48,8]{1,2,0:T(8,128)S(1)}, s32[1,48,8]{1,2,0:T(8,128)}, u32[]{:S(2)}) copy-start(s32[1,48,8]{1,2,0:T(8,128)} %param.10) | copy-start | bytes 4612
  11.3 49.5 %all-to-all-start = ((bf16[16,192,64]{1,2,0:T(8,128)(2,1)}), bf16[16,192,64]{1,2,0:T(8,128)(2,1)S(1)}, u32[]{:S(2)}, u32[]{:S(2)}) async-start(bf16[16,192,64]{1,2,0:T(8,128)(2,1)} %bitcast.4), calls=%async_computation | async-start | bytes 1048576 | tf_op jit(solution)/shard_map/all_to_all | solution.py:171
  18.9 74.1 %copy-start.2 = (s32[1,48]{1,0:T(1,128)S(1)}, s32[1,48]{1,0:T(1,128)}, u32[]{:S(2)}) copy-start(s32[1,48]{1,0:T(1,128)} %param.11) | copy-start | bytes 580
  142.8 27.9 %all-to-all-start.1 = ((bf16[16,192,256]{2,1,0:T(8,128)(2,1)}), bf16[16,192,256]{2,1,0:T(8,128)(2,1)S(1)}, u32[]{:S(2)}, u32[]{:S(2)}) async-start(bf16[16,192,256]{2,1,0:T(8,128)(2,1)} %bitcast.7), calls=%async_computation.1 | async-start | bytes 3145728 | tf_op jit(solution)/shard_map/all_to_all | solution.py:180
  170.6 48.4 %all-to-all-start.2 = ((bf16[32,32,192]{2,1,0:T(8,128)(2,1)}), bf16[32,32,192]{2,1,0:T(8,128)(2,1)S(1)}, u32[]{:S(2)}, u32[]{:S(2)}) async-start(bf16[32,32,192]{2,1,0:T(8,128)(2,1)} %bitcast.11), calls=%async_computation.2 | async-start | bytes 1048576 | tf_op jit(solution)/shard_map/all_to_all | solution.py:184
  185.6 2.8 %copy-start = (bf16[1024,3072]{1,0:T(8,128)(2,1)S(1)}, bf16[1024,3072]{1,0:T(8,128)(2,1)}, u32[]{:S(2)}) copy-start(bf16[1024,3072]{1,0:T(8,128)(2,1)} %all-gather.4.cloned.1.call-done.w_ref) | copy-start | bytes 18874372
Sparse Core Ops, SparseCore 0:
  11.0 81.9 all-gather.5
  95.7 77.4 all-gather.3

commit v2 on v1

--- a/solution.py
+++ b/solution.py
@@ -9,7 +9,8 @@
 HD = 64
 BF = jnp.bfloat16
 F32 = jnp.float32
-ROWS = 256
+ROWS = 1024
+GROUP = 12
 
 
 def dot(a, b, ca=1, cb=0):
@@ -18,7 +19,7 @@
 
 def attend_kernel(
     blocks_ref, counts_ref, feat_ref, w_ref, cot_ref, ocol_ref, orow_ref,
-    out_ref, x_ref, kv_ref, a_ref, acc_ref, g_ref,
+    out_ref, gw_ref, x_ref, kv_ref, a_ref, acc_ref, g_ref, sum_ref,
 ):
     nodes = feat_ref.shape[0]
     clusters, slots = blocks_ref.shape
@@ -36,7 +37,7 @@
         x_ref[r, :] = x.astype(BF)
         return carry
 
-    lax.fori_loop(0, tiles, project, 0, unroll=2)
+    lax.fori_loop(0, tiles, project, 0)
 
     first = lax.broadcasted_iota(jnp.int32, (rows, 2 * HD), 1) < HD
 
@@ -52,70 +53,84 @@
             a_ref[pl.ds(base + rows, rows), :] = jnp.where(first, 0.0, qd).astype(BF)
         return carry
 
-    lax.fori_loop(0, tiles, to_clusters, 0, unroll=1)
+    lax.fori_loop(0, tiles, to_clusters, 0)
 
     acc_ref[...] = jnp.zeros_like(acc_ref)
     key_at = lax.broadcasted_iota(jnp.int32, (rows, keys), 1)
 
-    def cluster(c):
-        at = [
-            pl.ds(pl.multiple_of(blocks_ref[c, j] * rows, rows), rows)
-            for j in range(slots)
-        ]
-        kv = jnp.concatenate([kv_ref[s, :] for s in at], axis=0)
-        a = a_ref[pl.ds(pl.multiple_of(c * 2 * rows, 2 * rows), 2 * rows), :]
-        both = dot(a, kv, 1, 1)
+    def weigh(both, c):
         score = jnp.where(key_at < counts_ref[c] * rows, both[:rows], -1e30)
         dpw = both[rows:]
         raw = jnp.exp(score - jnp.max(score, axis=1, keepdims=True))
         p = raw * (1.0 / jnp.sum(raw, axis=1, keepdims=True))
         ds = p * (dpw - jnp.sum(p * dpw, axis=1, keepdims=True))
-        pd = jnp.concatenate([ds, p], axis=0).astype(BF)
-        oq = dot(pd, kv)
-        back = dot(pd, a, 0, 0)
-        here = pl.ds(pl.multiple_of(c * rows, rows), rows)
-        g_ref[here, 2 * HD :] = jnp.where(first, oq[:rows] * 0.125, oq[rows:]).astype(BF)
-        return at, back
+        return jnp.concatenate([ds, p], axis=0).astype(BF)
 
     def step(i, carry):
-        for c in (2 * i, 2 * i + 1):
-            at, back = cluster(c)
-            new = [
-                acc_ref[s, :] + back[j * rows : (j + 1) * rows]
-                for j, s in enumerate(at)
-            ]
+        group = [i * GROUP + u for u in range(GROUP)]
+        ats = [
+            [pl.ds(pl.multiple_of(blocks_ref[c, j] * rows, rows), rows) for j in range(slots)]
+            for c in group
+        ]
+        kvs = [jnp.concatenate([kv_ref[s, :] for s in at], axis=0) for at in ats]
+        qds = [a_ref[pl.ds(pl.multiple_of(c * 2 * rows, 2 * rows), 2 * rows), :] for c in group]
+        boths = [dot(a, kv, 1, 1) for a, kv in zip(qds, kvs)]
+        pds = [weigh(b, c) for b, c in zip(boths, group)]
+        oqs = [dot(pd, kv) for pd, kv in zip(pds, kvs)]
+        backs = [dot(pd, a, 0, 0) for pd, a in zip(pds, qds)]
+        for c, oq in zip(group, oqs):
+            here = pl.ds(pl.multiple_of(c * rows, rows), rows)
+            g_ref[here, 2 * HD :] = jnp.where(first, oq[:rows] * 0.125, oq[rows:]).astype(BF)
+        for at, back in zip(ats, backs):
+            new = [acc_ref[s, :] + back[j * rows : (j + 1) * rows] for j, s in enumerate(at)]
             for s, v in zip(at, new):
                 acc_ref[s, :] = v
         return carry
 
-    lax.fori_loop(0, clusters // 2, step, 0)
+    lax.fori_loop(0, clusters // GROUP, step, 0)
     g_ref[:, : 2 * HD] = acc_ref[...].astype(BF)
+
+    sum_ref[...] = jnp.zeros_like(sum_ref)
 
     def to_nodes(i, carry):
         r = pl.ds(pl.multiple_of(i * ROWS, ROWS), ROWS)
         pick = orow_ref[...] == lax.broadcasted_iota(jnp.int32, (ROWS, nodes), 0) + i * ROWS
-        out_ref[r, :] = dot(pick.astype(F32).astype(BF), g_ref[...]).astype(BF)
-        return carry
-
-    lax.fori_loop(0, tiles, to_nodes, 0, unroll=1)
-
-
-def attend(feats, w_head, cot, order, blocks, counts):
-    nodes = feats.shape[0]
+        back = dot(pick.astype(F32).astype(BF), g_ref[...]).astype(BF)
+        out_ref[r, :] = back
+        sum_ref[...] += dot(feat_ref[r, :], back, 0, 0)
+        return carry
+
+    lax.fori_loop(0, tiles, to_nodes, 0)
+    parts, tall, lanes = gw_ref.shape
+    deep = tall * 2 // 3
+    gw_ref[:, :deep, :] = sum_ref[:, :lanes].reshape(parts, deep, lanes).astype(BF)
+    query = sum_ref[:, lanes:].reshape(parts, deep, lanes)
+    low, high = query[:, : deep // 2], query[:, deep // 2 :]
+    left = lax.broadcasted_iota(jnp.int32, low.shape, 2) < HD
+    gw_ref[:, deep:, :] = jnp.where(left, low, pltpu.roll(high, HD, 2)).astype(BF)
+
+
+def attend(feats, w_head, cot, order, blocks, counts, parts):
+    nodes, width = feats.shape
+    tall = width // parts * 3 // 2
     vmem = pl.BlockSpec(memory_space=pltpu.VMEM)
     smem = pl.BlockSpec(memory_space=pltpu.SMEM)
     return pl.pallas_call(
         attend_kernel,
         name="attend",
-        out_shape=jax.ShapeDtypeStruct((nodes, 4 * HD), BF),
+        out_shape=[
+            jax.ShapeDtypeStruct((nodes, 4 * HD), BF),
+            jax.ShapeDtypeStruct((parts, tall, 2 * HD), BF),
+        ],
         in_specs=[smem, smem] + [vmem] * 5,
-        out_specs=vmem,
+        out_specs=[vmem, vmem],
         scratch_shapes=[
             pltpu.VMEM((nodes, 4 * HD), BF),
             pltpu.VMEM((nodes, 2 * HD), BF),
             pltpu.VMEM((2 * nodes, 2 * HD), BF),
             pltpu.VMEM((nodes, 2 * HD), F32),
             pltpu.VMEM((nodes, 4 * HD), BF),
+            pltpu.VMEM((width, 4 * HD), F32),
         ],
         compiler_params=pltpu.CompilerParams(vmem_limit_bytes=50 << 20),
     )(blocks, counts, feats, w_head, cot, order.reshape(nodes, 1), order.reshape(1, nodes))
@@ -155,6 +170,22 @@
     )(got, weights)
 
 
+def reduce_scatter(part, axis):
+    size = lax.axis_size(axis)
+    me = lax.axis_index(axis)
+    bit = 1
+    while bit < size:
+        pairs = part.reshape(-1, 2, *part.shape[1:])
+        mine = lax.rem(me // bit, 2)
+        keep = lax.dynamic_index_in_dim(pairs, mine, 1, keepdims=False)
+        send = lax.dynamic_index_in_dim(pairs, 1 - mine, 1, keepdims=False)
+        came = lax.ppermute(send, axis, [(i, i ^ bit) for i in range(size)])
+        total = keep.astype(F32) + came.astype(F32)
+        part = total.astype(BF)
+        bit *= 2
+    return total[0]
+
+
 def per_device(features, qkv_weight, cotangent, node_order, blocks, counts):
     local_rows = features.shape[1]
     model_width = features.shape[2]
@@ -176,14 +207,13 @@
         [by_head[:, :, HD:].reshape(deep, -1), by_head[:, :, :HD].reshape(deep, -1)], axis=1
     )
     weights = lax.all_gather(ordered, "dp", axis=0, tiled=True)
-    grads = attend(node_all, w_head, cot, node_order[0], blocks[0], counts[0])
+    grads, part = attend(
+        node_all, w_head, cot, node_order[0], blocks[0], counts[0], lax.axis_size("dp")
+    )
     got = lax.all_to_all(grads.reshape(HEADS, local_rows, 4 * HD), "seq", 0, 0, tiled=True)
-    part = lax.dot_general(
-        node_all, grads[:, : 3 * HD], (((0,), (0,)), ((), ())), preferred_element_type=F32
-    ).astype(BF)
-    parts = lax.all_to_all(part.reshape(-1, deep, 3 * HD), "dp", 0, 0, tiled=True)
-    total = jnp.sum(parts.astype(F32), axis=0)
-    grad_weight = jnp.concatenate([total[:, 2 * HD :], total[:, : 2 * HD]], axis=1)
+    total = reduce_scatter(part, "dp")
+    query = jnp.concatenate([total[deep:, :HD], total[deep:, HD:]], axis=0)
+    grad_weight = jnp.concatenate([query, total[:deep]], axis=1)
     attended, grad_feats = finish(got, weights)
     return (
         attended.reshape(1, local_rows, model_width),

time: 227 us -> 189 us (0.83)
  waiting for transfers between devices: 77.3 us -> 49.5 us
  Pallas kernels: 52.8 us -> 32.7 us
  starting transfers between devices: 27.5 us -> 42.2 us
  matrix products: 4.77 us -> 0 us
    ppermute x0 -> x5, starting transfers between devices: none -> 30.4 us  [reduce_scatter(): came = lax.ppermute(send, axis, [(i, i ^ bit) for i in range(size)])]
    all_to_all x1 -> x0, waiting for transfers between devices: 27.6 us -> none  [per_device(): lax.all_to_all(part.reshape(-1, deep, 3 * HD), 'dp', 0, 0, tiled=True)]
    pallas_call x1, Pallas kernels: 49.8 us -> 29.6 us  [attend(): pl.pallas_call(attend_kernel, name='attend', out_shape=[jax.ShapeDtypeStr...]
    all_to_all x1, waiting for transfers between devices: 17.1 us -> 0.01 us  [per_device(): lax.all_to_all(grads.reshape(HEADS, local_rows, 4 * HD), 'seq', 0, 0, til...]
    all_to_all x1 -> x0, starting transfers between devices: 14.9 us -> none  [per_device(): lax.all_to_all(part.reshape(-1, deep, 3 * HD), 'dp', 0, 0, tiled=True)]
    ppermute x0 -> x5, waiting for transfers between devices: none -> 9.13 us  [reduce_scatter(): came = lax.ppermute(send, axis, [(i, i ^ bit) for i in range(size)])]
    all_gather x1, waiting for transfers between devices: 0.02 us -> 7.83 us  [per_device(): weights = lax.all_gather(ordered, 'dp', axis=0, tiled=True)]
    dot_general x1 -> x0, matrix products: 4.77 us -> none  [per_device(): lax.dot_general(node_all, grads[:, :3 * HD], (((0,), (0,)), ((), ())), pr...]
  transfers between devices with their start and end apart: 5 -> 9, of which waited for: 3 -> 6; matrix products, arithmetic and copies ran while one was open for 6% -> 4% of each run, Pallas kernels for 23% -> 16%
where the time goes in v2:
time: 189 us; the launch traced here: 188 us
  waiting for transfers between devices  49.5 us (26%)
  starting transfers between devices  42.2 us (22%)
  blocking collectives  38.5 us (20%)
  Pallas kernels  32.7 us (17%)
  between operations  14.4 us (8%)
  local copies, waits for them, and re-layouts  8.56 us (5%)
  other arithmetic  2.3 us (1%)
    all_gather x1, blocking collectives, per_device(): w_head = lax.all_gather(own, 'dp', axis=0, tiled=True)  38.5 us
    all_gather x1, waiting for transfers between devices, per_device(): node_all = lax.all_gather(feats, 'seq', axis=0, tiled=True)  31.8 us
    ppermute x5, starting transfers between devices, reduce_scatter(): came = lax.ppermute(send, axis, [(i, i ^ bit) for i in range(size)])  30.4 us
    pallas_call x1, Pallas kernels, attend(): pl.pallas_call(attend_kernel, name='attend', out_shape=[jax.ShapeDtypeStr...  29.6 us
    ppermute x5, waiting for transfers between devices, reduce_scatter(): came = lax.ppermute(send, axis, [(i, i ^ bit) for i in range(size)])  9.13 us
    all_gather x1, waiting for transfers between devices, per_device(): weights = lax.all_gather(ordered, 'dp', axis=0, tiled=True)  7.83 us
    all_to_all x1, starting transfers between devices, per_device(): lax.all_to_all(cotangent[0].reshape(local_rows, HEADS, HD).transpose(1, 0...  7.58 us
    all_to_all x1, starting transfers between devices, per_device(): lax.all_to_all(grads.reshape(HEADS, local_rows, 4 * HD), 'seq', 0, 0, til...  4.09 us
  transfers between devices with their start and end apart: 9, of which 6 were waited for; matrix products, arithmetic and copies ran while one was open for 4% of the time, Pallas kernels for 16%

profile of v2, /device:TPU:1, one launch (start us, length us, event | category | flops | bytes accessed | tf_op | source)
XLA Modules:
  0.0 188.0 jit_solution(3101462637764801630)
XLA Ops:
  8.0 1.3 reshape.57
  9.6 0.7 pad_maximum_fusion
  10.3 1.0 copy.20
  11.3 7.6 %all-to-all-start = ((bf16[16,192,64]{1,2,0:T(8,128)(2,1)}), bf16[16,192,64]{1,2,0:T(8,128)(2,1)S(1)}, u32[]{:S(2)}, u32[]{:S(2)}) async-start(bf16[16,192,64]{1,2,0:T(8,128)(2,1)} %bitcast.4), calls=%async_computation | async-start | bytes 1048576 | tf_op jit(solution)/shard_map/all_to_all | solution.py:202
  19.0 1.7 copy.22.ocol_ref
  20.8 0.8 dynamic-slice_multiply_fusion
  21.6 0.8 constant_dynamic-slice_fusion
  22.4 38.5 %all_gather.10.w_ref = bf16[1024,256]{1,0:T(8,128)(2,1)S(1)} all-gather(bf16[32,256]{1,0:T(8,128)(2,1)S(1)} %maximum_maximum_fusion), channel_id=1, replica_groups=mesh['dp'=32,'seq'=16] {'dp'}, dimensions={0}, use_global_device_ids=true | all-gather | bytes 540672 | tf_op jit(solution)/shard_map/all_gather | solution.py:200
  61.2 31.8 %all-gather.6.cloned.1.call-done = bf16[1,3072,1024]{2,1,0:T(8,128)(2,1)} async-done(((bf16[1,192,1024]{2,1,0:T(8,128)(2,1)}), bf16[1,3072,1024]{2,1,0:T(8,128)(2,1)}) %all-gather.6.cloned.1.call-update) | async-done | bytes 6291472 | tf_op jit(solution)/shard_map/all_gather | solution.py:201
  93.0 29.6 %attend.1 = (bf16[3072,256]{1,0:T(8,128)(2,1)}, bf16[32,48,128]{2,1,0:T(8,128)(2,1)S(1)}) custom-call(s32[48,8]{1,0:T(8,128)S(1)} %bitcast.47, s32[48]{0:T(128)S(1)} %bitcast.49, bf16[3072,1024]{1,0:T(8,128)(2,1)} %bitcast.50, bf16[1024,256]{1,0:T(8,128)(2,1)S(1)} %all_gather.10.w_ref, bf16[3072,64]{1,0:T(8,128)(2,1)S(1)} %bitcast.44, ...), custom_call_target="tpu_custom_call" | custom-call | tf_op jit(solution)/shard_map/attend/pallas_call | solution.py:118
  122.7 2.6 %collective-permute-start = (bf16[16,48,128]{2,1,0:T(8,128)(2,1)S(1)}, bf16[16,48,128]{2,1,0:T(8,128)(2,1)S(1)}, u32[]{:S(2)}, u32[]{:S(2)}) collective-permute-start(bf16[16,48,128]{2,1,0:T(8,128)(2,1)S(1)} %dynamic-slice_bitcast_fusion), channel_id=1, source_target_pairs={{0,16},{16,0},{32,48},{48,32},{64,80},{80,64},{96,112},{112,96},{1... | collective-permute-start | bytes 589832 | tf_op jit(solution)/shard_map/ppermute | solution.py:182
  125.3 1.0 collective-permute-done
  126.4 3.2 %collective-permute-start.1 = (bf16[8,48,128]{2,1,0:T(8,128)(2,1)S(1)}, bf16[8,48,128]{2,1,0:T(8,128)(2,1)S(1)}, u32[]{:S(2)}, u32[]{:S(2)}) collective-permute-start(bf16[8,48,128]{2,1,0:T(8,128)(2,1)S(1)} %dynamic-slice_bitcast_fusion.1), channel_id=1, source_target_pairs={{0,32},{16,48},{32,0},{48,16},{64,96},{80,112},{96,64},{112,80},{1... | collective-permute-start | bytes 294920 | tf_op jit(solution)/shard_map/ppermute | solution.py:182
  129.6 4.9 %collective-permute-done.1 = bf16[8,48,128]{2,1,0:T(8,128)(2,1)S(1)} collective-permute-done((bf16[8,48,128]{2,1,0:T(8,128)(2,1)S(1)}, bf16[8,48,128]{2,1,0:T(8,128)(2,1)S(1)}, u32[]{:S(2)}, u32[]{:S(2)}) %collective-permute-start.1) | collective-permute-done | bytes 98336 | tf_op jit(solution)/shard_map/ppermute | solution.py:182
  134.6 4.3 %collective-permute-start.2 = (bf16[4,48,128]{2,1,0:T(8,128)(2,1)S(1)}, bf16[4,48,128]{2,1,0:T(8,128)(2,1)S(1)}, u32[]{:S(2)}, u32[]{:S(2)}) collective-permute-start(bf16[4,48,128]{2,1,0:T(8,128)(2,1)S(1)} %dynamic-slice_bitcast_fusion.2), channel_id=1, source_target_pairs={{0,64},{16,80},{32,96},{48,112},{64,0},{80,16},{96,32},{112,48},{1... | collective-permute-start | bytes 147464 | tf_op jit(solution)/shard_map/ppermute | solution.py:182
  138.9 4.1 %all-to-all-start.1 = ((bf16[16,192,256]{2,1,0:T(8,128)(2,1)}), bf16[16,192,256]{2,1,0:T(8,128)(2,1)S(1)}, u32[]{:S(2)}, u32[]{:S(2)}) async-start(bf16[16,192,256]{2,1,0:T(8,128)(2,1)} %bitcast.7), calls=%async_computation.1 | async-start | bytes 3145728 | tf_op jit(solution)/shard_map/all_to_all | solution.py:213
  143.1 7.4 %collective-permute-start.3 = (bf16[2,48,128]{2,1,0:T(8,128)(2,1)S(1)}, bf16[2,48,128]{2,1,0:T(8,128)(2,1)S(1)}, u32[]{:S(2)}, u32[]{:S(2)}) collective-permute-start(bf16[2,48,128]{2,1,0:T(8,128)(2,1)S(1)} %dynamic-slice_bitcast_fusion.3), channel_id=1, source_target_pairs={{0,128},{16,144},{32,160},{48,176},{64,192},{80,208},{96,224},{112... | collective-permute-start | bytes 73736 | tf_op jit(solution)/shard_map/ppermute | solution.py:182
  150.5 2.0 %collective-permute-done.3 = bf16[2,48,128]{2,1,0:T(8,128)(2,1)S(1)} collective-permute-done((bf16[2,48,128]{2,1,0:T(8,128)(2,1)S(1)}, bf16[2,48,128]{2,1,0:T(8,128)(2,1)S(1)}, u32[]{:S(2)}, u32[]{:S(2)}) %collective-permute-start.3) | collective-permute-done | bytes 24608 | tf_op jit(solution)/shard_map/ppermute | solution.py:182
  152.6 13.0 %collective-permute-start.4 = (bf16[1,48,128]{2,1,0:T(8,128)(2,1)S(1)}, bf16[1,48,128]{2,1,0:T(8,128)(2,1)S(1)}, u32[]{:S(2)}, u32[]{:S(2)}) collective-permute-start(bf16[1,48,128]{2,1,0:T(8,128)(2,1)S(1)} %constant_dynamic-slice_fusion.1), channel_id=1, source_target_pairs={{0,256},{16,272},{32,288},{48,304},{64,320},{80,336},{96,352},{112... | collective-permute-start | bytes 36872 | tf_op jit(solution)/shard_map/ppermute | solution.py:182
  165.5 1.2 collective-permute-done.4
  166.8 0.7 pad_maximum_fusion.1
  167.5 7.8 %all-gather.4.cloned.1.call-done.w_ref = bf16[1024,3072]{1,0:T(8,128)(2,1)} async-done(((bf16[32,3072]{1,0:T(8,128)(2,1)}), bf16[1024,3072]{1,0:T(8,128)(2,1)}) %all-gather.4.cloned.1.call-update) | async-done | bytes 6291472 | tf_op jit(solution)/shard_map/all_gather | solution.py:209
  175.3 2.8 %copy-done = bf16[1024,3072]{1,0:T(8,128)(2,1)S(1)} copy-done((bf16[1024,3072]{1,0:T(8,128)(2,1)S(1)}, bf16[1024,3072]{1,0:T(8,128)(2,1)}, u32[]{:S(2)}) %copy-start) | copy-done | bytes 6291480
  178.1 3.1 %finish.1 = (bf16[192,1024]{1,0:T(8,128)(2,1)}, bf16[192,1024]{1,0:T(8,128)(2,1)}) custom-call(bf16[16,192,256]{2,1,0:T(8,128)(2,1)S(1)} %all-to-all-done.1.g_ref, bf16[1024,3072]{1,0:T(8,128)(2,1)S(1)} %copy-done), custom_call_target="tpu_custom_call" | custom-call | tf_op jit(solution)/shard_map/finish/pallas_call | solution.py:159
  (37 shorter events, 1.9 us)
Async XLA Ops:
  7.2 3.1 %copy-start.3 = (bf16[1,192,1024]{2,1,0:T(8,128)(2,1)S(1)}, bf16[1,192,1024]{2,1,0:T(8,128)(2,1)}, u32[]{:S(2)}) copy-start(bf16[1,192,1024]{2,1,0:T(8,128)(2,1)} %param.8) | copy-start | bytes 1179652
  7.2 85.8 %all-gather.6.cloned.1.call-start = ((), (), s32[]{:S(2)}) async-start(), calls=%async_computation.3 | async-start | bytes 6684672 | tf_op jit(solution)/shard_map/all_gather | solution.py:201
  7.9 167.4 %all-gather.4.cloned.1.call-start = ((), (), s32[]{:S(2)}) async-start(), calls=%async_computation.2 | async-start | bytes 6488064 | tf_op jit(solution)/shard_map/all_gather | solution.py:209
  9.4 9.6 %copy-start.4 = (s32[1,48,8]{1,2,0:T(8,128)S(1)}, s32[1,48,8]{1,2,0:T(8,128)}, u32[]{:S(2)}) copy-start(s32[1,48,8]{1,2,0:T(8,128)} %param.10) | copy-start | bytes 4612
  9.4 9.6 %copy-start.1 = (s32[1,3072]{1,0:T(1,128)S(1)}, s32[1,3072]{1,0:T(1,128)}, u32[]{:S(2)}) copy-start(s32[1,3072]{1,0:T(1,128)} %orow_ref.1) | copy-start | bytes 36868
  11.3 49.5 %all-to-all-start = ((bf16[16,192,64]{1,2,0:T(8,128)(2,1)}), bf16[16,192,64]{1,2,0:T(8,128)(2,1)S(1)}, u32[]{:S(2)}, u32[]{:S(2)}) async-start(bf16[16,192,64]{1,2,0:T(8,128)(2,1)} %bitcast.4), calls=%async_computation | async-start | bytes 1048576 | tf_op jit(solution)/shard_map/all_to_all | solution.py:202
  19.0 74.0 %copy-start.2 = (s32[1,48]{1,0:T(1,128)S(1)}, s32[1,48]{1,0:T(1,128)}, u32[]{:S(2)}) copy-start(s32[1,48]{1,0:T(1,128)} %param.11) | copy-start | bytes 580
  122.7 3.6 %collective-permute-start = (bf16[16,48,128]{2,1,0:T(8,128)(2,1)S(1)}, bf16[16,48,128]{2,1,0:T(8,128)(2,1)S(1)}, u32[]{:S(2)}, u32[]{:S(2)}) collective-permute-start(bf16[16,48,128]{2,1,0:T(8,128)(2,1)S(1)} %dynamic-slice_bitcast_fusion), channel_id=1, source_target_pairs={{0,16},{16,0},{32,48},{48,32},{64,80},{80,64},{96,112},{112,96},{1... | collective-permute-start | bytes 589832 | tf_op jit(solution)/shard_map/ppermute | solution.py:182
  126.4 8.2 %collective-permute-start.1 = (bf16[8,48,128]{2,1,0:T(8,128)(2,1)S(1)}, bf16[8,48,128]{2,1,0:T(8,128)(2,1)S(1)}, u32[]{:S(2)}, u32[]{:S(2)}) collective-permute-start(bf16[8,48,128]{2,1,0:T(8,128)(2,1)S(1)} %dynamic-slice_bitcast_fusion.1), channel_id=1, source_target_pairs={{0,32},{16,48},{32,0},{48,16},{64,96},{80,112},{96,64},{112,80},{1... | collective-permute-start | bytes 294920 | tf_op jit(solution)/shard_map/ppermute | solution.py:182
  134.6 8.4 %collective-permute-start.2 = (bf16[4,48,128]{2,1,0:T(8,128)(2,1)S(1)}, bf16[4,48,128]{2,1,0:T(8,128)(2,1)S(1)}, u32[]{:S(2)}, u32[]{:S(2)}) collective-permute-start(bf16[4,48,128]{2,1,0:T(8,128)(2,1)S(1)} %dynamic-slice_bitcast_fusion.2), channel_id=1, source_target_pairs={{0,64},{16,80},{32,96},{48,112},{64,0},{80,16},{96,32},{112,48},{1... | collective-permute-start | bytes 147464 | tf_op jit(solution)/shard_map/ppermute | solution.py:182
  138.9 36.4 %all-to-all-start.1 = ((bf16[16,192,256]{2,1,0:T(8,128)(2,1)}), bf16[16,192,256]{2,1,0:T(8,128)(2,1)S(1)}, u32[]{:S(2)}, u32[]{:S(2)}) async-start(bf16[16,192,256]{2,1,0:T(8,128)(2,1)} %bitcast.7), calls=%async_computation.1 | async-start | bytes 3145728 | tf_op jit(solution)/shard_map/all_to_all | solution.py:213
  143.1 9.5 %collective-permute-start.3 = (bf16[2,48,128]{2,1,0:T(8,128)(2,1)S(1)}, bf16[2,48,128]{2,1,0:T(8,128)(2,1)S(1)}, u32[]{:S(2)}, u32[]{:S(2)}) collective-permute-start(bf16[2,48,128]{2,1,0:T(8,128)(2,1)S(1)} %dynamic-slice_bitcast_fusion.3), channel_id=1, source_target_pairs={{0,128},{16,144},{32,160},{48,176},{64,192},{80,208},{96,224},{112... | collective-permute-start | bytes 73736 | tf_op jit(solution)/shard_map/ppermute | solution.py:182
  152.6 14.2 %collective-permute-start.4 = (bf16[1,48,128]{2,1,0:T(8,128)(2,1)S(1)}, bf16[1,48,128]{2,1,0:T(8,128)(2,1)S(1)}, u32[]{:S(2)}, u32[]{:S(2)}) collective-permute-start(bf16[1,48,128]{2,1,0:T(8,128)(2,1)S(1)} %constant_dynamic-slice_fusion.1), channel_id=1, source_target_pairs={{0,256},{16,272},{32,288},{48,304},{64,320},{80,336},{96,352},{112... | collective-permute-start | bytes 36872 | tf_op jit(solution)/shard_map/ppermute | solution.py:182
  175.3 2.8 %copy-start = (bf16[1024,3072]{1,0:T(8,128)(2,1)S(1)}, bf16[1024,3072]{1,0:T(8,128)(2,1)}, u32[]{:S(2)}) copy-start(bf16[1024,3072]{1,0:T(8,128)(2,1)} %all-gather.4.cloned.1.call-done.w_ref) | copy-start | bytes 18874372
Sparse Core Ops, SparseCore 0:
  11.0 81.9 all-gather.5
  95.7 79.5 all-gather.3

commit v3 on v2

--- a/solution.py
+++ b/solution.py
@@ -11,6 +11,16 @@
 F32 = jnp.float32
 ROWS = 1024
 GROUP = 12
+SIDE = 4
+HOPS = (
+    ((0, 0), (0, 1)), ((0, 0), (0, -1)), ((0, 0), (1, 0)), ((0, 0), (-1, 0)),
+    ((1, 0), (0, 1)), ((-1, 0), (0, -1)), ((0, -1), (1, 0)), ((0, 1), (-1, 0)),
+    ((0, 1), (0, 1)), ((1, -1), (0, -1)), ((1, 0), (1, 0)), ((-1, 1), (-1, 0)),
+    ((2, 1), (0, 1)), ((-1, -1), (0, -1)), ((1, -1), (1, 0)),
+)
+
+
+SECOND = 4
 
 
 def dot(a, b, ca=1, cb=0):
@@ -18,32 +28,53 @@
 
 
 def attend_kernel(
-    blocks_ref, counts_ref, feat_ref, w_ref, cot_ref, ocol_ref, orow_ref,
-    out_ref, gw_ref, x_ref, kv_ref, a_ref, acc_ref, g_ref, sum_ref,
+    blocks_ref, counts_ref, owner_ref, ids_ref, w_ref, cot_ref, ocol_ref, orow_ref, *refs
 ):
+    members = owner_ref.shape[0]
+    parts_refs, refs = refs[:members], refs[members:]
+    (out_ref, gw_ref, feat_ref, wide_ref, x_ref, kv_ref, a_ref, acc_ref, g_ref, sum_ref, sem) = refs
     nodes = feat_ref.shape[0]
     clusters, slots = blocks_ref.shape
     rows = nodes // clusters
     keys = slots * rows
     tiles = nodes // ROWS
+    local = nodes // members
+    loads = [
+        pltpu.make_async_copy(part, feat_ref.at[pl.ds(k * local, local), :], sem.at[k])
+        for k, part in enumerate(parts_refs)
+    ]
+    for load in loads:
+        load.start()
+
+    parts, tall, lanes = w_ref.shape
+    deep = tall * 2 // 3
+    width = parts * deep
+    wide_ref[:, :lanes] = w_ref[:, :deep, :].reshape(width, lanes)
+    packed = w_ref[:, deep:, :].astype(F32)
+    left = lax.broadcasted_iota(jnp.int32, packed.shape, 2) < HD
+    query = [jnp.where(left, packed, 0.0), jnp.where(left, pltpu.roll(packed, HD, 2), 0.0)]
+    wide_ref[:, lanes:] = jnp.concatenate(query, axis=1).reshape(width, lanes).astype(BF)
     place = (
         lax.broadcasted_iota(jnp.int32, (HD, 4 * HD), 0) + 3 * HD
         == lax.broadcasted_iota(jnp.int32, (HD, 4 * HD), 1)
     ).astype(F32).astype(BF)
 
-    def project(i, carry):
-        r = pl.ds(pl.multiple_of(i * ROWS, ROWS), ROWS)
-        x = dot(feat_ref[r, :], w_ref[...]) + dot(cot_ref[r, :], place)
-        x_ref[r, :] = x.astype(BF)
-        return carry
-
-    lax.fori_loop(0, tiles, project, 0)
+    def at_owner(k):
+        return pl.ds(pl.multiple_of(owner_ref[k] * local, local), local)
+
+    batch = 4
+    for b in range(0, members, batch):
+        for load in loads[b : b + batch]:
+            load.wait()
+        r = slice(b * local, (b + batch) * local)
+        cot = jnp.concatenate([cot_ref[at_owner(b + k), :] for k in range(batch)], axis=0)
+        x_ref[r, :] = (dot(feat_ref[r, :], wide_ref[...]) + dot(cot, place)).astype(BF)
 
     first = lax.broadcasted_iota(jnp.int32, (rows, 2 * HD), 1) < HD
 
     def to_clusters(i, carry):
         r = pl.ds(pl.multiple_of(i * ROWS, ROWS), ROWS)
-        pick = ocol_ref[r, :] == lax.broadcasted_iota(jnp.int32, (ROWS, nodes), 1)
+        pick = ocol_ref[r, :] == ids_ref[...]
         moved = dot(pick.astype(F32).astype(BF), x_ref[...])
         kv_ref[r, :] = moved[:, : 2 * HD].astype(BF)
         for t in range(ROWS // rows):
@@ -92,27 +123,33 @@
 
     sum_ref[...] = jnp.zeros_like(sum_ref)
 
+    half = members // 2
+    here = lax.broadcasted_iota(jnp.int32, (local, nodes), 0)
+
     def to_nodes(i, carry):
-        r = pl.ds(pl.multiple_of(i * ROWS, ROWS), ROWS)
-        pick = orow_ref[...] == lax.broadcasted_iota(jnp.int32, (ROWS, nodes), 0) + i * ROWS
-        back = dot(pick.astype(F32).astype(BF), g_ref[...]).astype(BF)
-        out_ref[r, :] = back
+        picks = [
+            (orow_ref[...] == here + owner_ref[i * half + k] * local).astype(F32).astype(BF)
+            for k in range(half)
+        ]
+        back = dot(jnp.concatenate(picks, axis=0), g_ref[...]).astype(BF)
+        for k in range(half):
+            out_ref[at_owner(i * half + k), :] = back[k * local : (k + 1) * local]
+        r = pl.ds(pl.multiple_of(i * half * local, half * local), half * local)
         sum_ref[...] += dot(feat_ref[r, :], back, 0, 0)
         return carry
 
-    lax.fori_loop(0, tiles, to_nodes, 0)
-    parts, tall, lanes = gw_ref.shape
-    deep = tall * 2 // 3
+    lax.fori_loop(0, 2, to_nodes, 0)
     gw_ref[:, :deep, :] = sum_ref[:, :lanes].reshape(parts, deep, lanes).astype(BF)
     query = sum_ref[:, lanes:].reshape(parts, deep, lanes)
     low, high = query[:, : deep // 2], query[:, deep // 2 :]
-    left = lax.broadcasted_iota(jnp.int32, low.shape, 2) < HD
     gw_ref[:, deep:, :] = jnp.where(left, low, pltpu.roll(high, HD, 2)).astype(BF)
 
 
-def attend(feats, w_head, cot, order, blocks, counts, parts):
-    nodes, width = feats.shape
-    tall = width // parts * 3 // 2
+def attend(blocks_of, owner, w_head, cot, order, blocks, counts):
+    local, width = blocks_of[0].shape
+    nodes = len(blocks_of) * local
+    parts, tall, lanes = w_head.shape
+    ids = (owner[:, None] * local + jnp.arange(local, dtype=jnp.int32)).reshape(1, nodes)
     vmem = pl.BlockSpec(memory_space=pltpu.VMEM)
     smem = pl.BlockSpec(memory_space=pltpu.SMEM)
     return pl.pallas_call(
@@ -120,20 +157,26 @@
         name="attend",
         out_shape=[
             jax.ShapeDtypeStruct((nodes, 4 * HD), BF),
-            jax.ShapeDtypeStruct((parts, tall, 2 * HD), BF),
+            jax.ShapeDtypeStruct((parts, tall, lanes), BF),
         ],
-        in_specs=[smem, smem] + [vmem] * 5,
+        in_specs=[smem] * 3 + [vmem] * 5 + [pl.BlockSpec(memory_space=pl.ANY)] * len(blocks_of),
         out_specs=[vmem, vmem],
         scratch_shapes=[
+            pltpu.VMEM((nodes, width), BF),
+            pltpu.VMEM((width, 4 * HD), BF),
             pltpu.VMEM((nodes, 4 * HD), BF),
             pltpu.VMEM((nodes, 2 * HD), BF),
             pltpu.VMEM((2 * nodes, 2 * HD), BF),
             pltpu.VMEM((nodes, 2 * HD), F32),
             pltpu.VMEM((nodes, 4 * HD), BF),
             pltpu.VMEM((width, 4 * HD), F32),
+            pltpu.SemaphoreType.DMA((len(blocks_of),)),
         ],
-        compiler_params=pltpu.CompilerParams(vmem_limit_bytes=50 << 20),
-    )(blocks, counts, feats, w_head, cot, order.reshape(nodes, 1), order.reshape(1, nodes))
+        compiler_params=pltpu.CompilerParams(vmem_limit_bytes=52 << 20),
+    )(
+        blocks, counts, owner, ids, w_head, cot,
+        order.reshape(nodes, 1), order.reshape(1, nodes), *blocks_of,
+    )
 
 
 def finish_kernel(g_ref, w_ref, att_ref, gf_ref, lhs_ref):
@@ -186,6 +229,22 @@
     return total[0]
 
 
+def gather_round(block, axis):
+    y, x = lax.axis_index(axis) // SIDE, lax.rem(lax.axis_index(axis), SIDE)
+    held = {(0, 0): block}
+    for (hy, hx), (dy, dx) in HOPS:
+        pairs = [
+            ((r + dy) % SIDE * SIDE + (c + dx) % SIDE, r * SIDE + c)
+            for r in range(SIDE)
+            for c in range(SIDE)
+        ]
+        source = held[hy % SIDE, hx % SIDE]
+        held[(hy + dy) % SIDE, (hx + dx) % SIDE] = lax.ppermute(source, axis, pairs)
+    places = jnp.asarray(list(held), jnp.int32)
+    owner = lax.rem(places[:, 0] + y, SIDE) * SIDE + lax.rem(places[:, 1] + x, SIDE)
+    return list(held.values()), owner.astype(jnp.int32)
+
+
 def per_device(features, qkv_weight, cotangent, node_order, blocks, counts):
     local_rows = features.shape[1]
     model_width = features.shape[2]
@@ -193,23 +252,22 @@
     feats = features[0]
     head = lax.axis_index("seq")
     own = lax.dynamic_slice(qkv_weight, (0, head * 3 * HD), (deep, 3 * HD))
-    own = jnp.concatenate(
-        [own[:, HD:], own[:, :HD] * jnp.asarray(0.125, BF), jnp.zeros((deep, HD), BF)],
-        axis=1,
-    )
-    w_head = lax.all_gather(own, "dp", axis=0, tiled=True)
-    node_all = lax.all_gather(feats, "seq", axis=0, tiled=True)
+    query = own[:, :HD] * jnp.asarray(0.125, BF)
+    query = jnp.concatenate([query[: deep // 2], query[deep // 2 :]], axis=1)
+    own = jnp.concatenate([own[:, HD:], query], axis=0)
+    copies = jnp.broadcast_to(own[None], (lax.axis_size("dp"), *own.shape))
+    blocks_of, owner = gather_round(feats, "seq")
     cot = lax.all_to_all(
         cotangent[0].reshape(local_rows, HEADS, HD).transpose(1, 0, 2), "seq", 0, 0, tiled=True
     ).reshape(HEADS * local_rows, HD)
+    copies, _ = lax.optimization_barrier((copies, blocks_of[SECOND]))
+    w_head = lax.all_to_all(copies, "dp", 0, 0, tiled=True)
     by_head = qkv_weight.reshape(deep, HEADS, 3 * HD)
     ordered = jnp.concatenate(
         [by_head[:, :, HD:].reshape(deep, -1), by_head[:, :, :HD].reshape(deep, -1)], axis=1
     )
     weights = lax.all_gather(ordered, "dp", axis=0, tiled=True)
-    grads, part = attend(
-        node_all, w_head, cot, node_order[0], blocks[0], counts[0], lax.axis_size("dp")
-    )
+    grads, part = attend(blocks_of, owner, w_head, cot, node_order[0], blocks[0], counts[0])
     got = lax.all_to_all(grads.reshape(HEADS, local_rows, 4 * HD), "seq", 0, 0, tiled=True)
     total = reduce_scatter(part, "dp")
     query = jnp.concatenate([total[deep:, :HD], total[deep:, HD:]], axis=0)

time: 189 us -> 197 us (1.042)
  the two profiles are of different devices: /device:TPU:1 before, /device:TPU:2 now
where the time goes in v3:
time: 197 us; the launch traced here: 195 us
  starting transfers between devices  110 us (56%)
  Pallas kernels  34.7 us (18%)
  waiting for transfers between devices  23.6 us (12%)
  between operations  14.7 us (7%)
  local copies, waits for them, and re-layouts  10.3 us (5%)
  other arithmetic  2.49 us (1%)
    ppermute x15, starting transfers between devices, gather_round(): held[(hy + dy) % SIDE, (hx + dx) % SIDE] = lax.ppermute(source, axis, pairs)  55.1 us
    pallas_call x1, Pallas kernels, attend(): pl.pallas_call(attend_kernel, name='attend', out_shape=[jax.ShapeDtypeStr...  31.7 us
    ppermute x5, starting transfers between devices, reduce_scatter(): came = lax.ppermute(send, axis, [(i, i ^ bit) for i in range(size)])  27 us
    all_to_all x1, starting transfers between devices, per_device(): w_head = lax.all_to_all(copies, 'dp', 0, 0, tiled=True)  13.7 us
    ppermute x5, waiting for transfers between devices, reduce_scatter(): came = lax.ppermute(send, axis, [(i, i ^ bit) for i in range(size)])  11.2 us
    all_to_all x1, starting transfers between devices, per_device(): lax.all_to_all(grads.reshape(HEADS, local_rows, 4 * HD), 'seq', 0, 0, til...  7.81 us
    all_to_all x1, waiting for transfers between devices, per_device(): lax.all_to_all(cotangent[0].reshape(local_rows, HEADS, HD).transpose(1, 0...  6.21 us
    ppermute x15, waiting for transfers between devices, gather_round(): held[(hy + dy) % SIDE, (hx + dx) % SIDE] = lax.ppermute(source, axis, pairs)  6.17 us
  transfers between devices with their start and end apart: 24, of which 7 were waited for; matrix products, arithmetic and copies ran while one was open for 4% of the time, Pallas kernels for 16%

profile of v3, /device:TPU:2, one launch (start us, length us, event | category | flops | bytes accessed | tf_op | source)
XLA Modules:
  0.0 195.5 jit_solution(17826055936049663745)
XLA Ops:
  9.6 3.6 %collective-permute-start = (bf16[192,1024]{1,0:T(8,128)(2,1)S(1)}, bf16[192,1024]{1,0:T(8,128)(2,1)S(1)}, u32[]{:S(2)}, u32[]{:S(2)}) collective-permute-start(bf16[192,1024]{1,0:T(8,128)(2,1)S(1)} %bitcast.72), channel_id=1, source_target_pairs={{12,0},{13,1},{14,2},{15,3},{0,4},{1,5},{2,6},{3,7},{4,8},{5,9},{6... | collective-permute-start | bytes 1179656 | tf_op jit(solution)/shard_map/ppermute | solution.py:242
  13.3 6.3 %collective-permute-start.1 = (bf16[192,1024]{1,0:T(8,128)(2,1)S(1)}, bf16[192,1024]{1,0:T(8,128)(2,1)S(1)}, u32[]{:S(2)}, u32[]{:S(2)}) collective-permute-start(bf16[192,1024]{1,0:T(8,128)(2,1)S(1)} %bitcast.73), channel_id=1, source_target_pairs={{1,0},{2,1},{3,2},{0,3},{5,4},{6,5},{7,6},{4,7},{9,8},{10,9},{11,1... | collective-permute-start | bytes 1179656 | tf_op jit(solution)/shard_map/ppermute | solution.py:242
  20.5 6.0 %all-to-all-start.1 = ((bf16[16,192,64]{1,2,0:T(8,128)(2,1)}), bf16[16,192,64]{1,2,0:T(8,128)(2,1)S(1)}, u32[]{:S(2)}, u32[]{:S(2)}) async-start(bf16[16,192,64]{1,2,0:T(8,128)(2,1)} %bitcast.7), calls=%async_computation.1 | async-start | bytes 1048576 | tf_op jit(solution)/shard_map/all_to_all | solution.py:260
  29.1 6.2 %all-to-all-done.1 = bf16[16,192,64]{1,2,0:T(8,128)(2,1)S(1)} async-done(((bf16[16,192,64]{1,2,0:T(8,128)(2,1)}), bf16[16,192,64]{1,2,0:T(8,128)(2,1)S(1)}, u32[]{:S(2)}, u32[]{:S(2)}) %all-to-all-start.1) | async-done | bytes 393248 | tf_op jit(solution)/shard_map/all_to_all | solution.py:260
  35.3 13.7 %all-to-all-start = ((bf16[32,48,128]{2,1,0:T(8,128)(2,1)}), bf16[32,48,128]{2,1,0:T(8,128)(2,1)S(1)}, u32[]{:S(2)}, u32[]{:S(2)}) async-start(bf16[32,48,128]{2,1,0:T(8,128)(2,1)} %broadcast_in_dim.2), calls=%async_computation | async-start | bytes 786432 | tf_op jit(solution)/shard_map/all_to_all | solution.py:264
  51.5 3.2 %collective-permute-start.3 = (bf16[192,1024]{1,0:T(8,128)(2,1)S(1)}, bf16[192,1024]{1,0:T(8,128)(2,1)S(1)}, u32[]{:S(2)}, u32[]{:S(2)}) collective-permute-start(bf16[192,1024]{1,0:T(8,128)(2,1)S(1)} %bitcast.75), channel_id=1, source_target_pairs={{4,0},{5,1},{6,2},{7,3},{8,4},{9,5},{10,6},{11,7},{12,8},{13,9},{1... | collective-permute-start | bytes 1179656 | tf_op jit(solution)/shard_map/ppermute | solution.py:242
  57.4 5.0 %collective-permute-start.5 = (bf16[192,1024]{1,0:T(8,128)(2,1)S(1)}, bf16[192,1024]{1,0:T(8,128)(2,1)}, u32[]{:S(2)}, u32[]{:S(2)}) collective-permute-start(bf16[192,1024]{1,0:T(8,128)(2,1)S(1)} %collective-permute-done.refs_4_), channel_id=1, source_target_pairs={{3,0},{0,1},{1,2},{2,3},{7,4},{4,5},{5,6},{6,7},{11,8},{8,9},{9,10... | collective-permute-start | bytes 1179656 | tf_op jit(solution)/shard_map/ppermute | solution.py:242
  62.9 4.0 %collective-permute-start.6 = (bf16[192,1024]{1,0:T(8,128)(2,1)S(1)}, bf16[192,1024]{1,0:T(8,128)(2,1)}, u32[]{:S(2)}, u32[]{:S(2)}) collective-permute-start(bf16[192,1024]{1,0:T(8,128)(2,1)S(1)} %collective-permute-done.2.refs_2_), channel_id=1, source_target_pairs={{4,0},{5,1},{6,2},{7,3},{8,4},{9,5},{10,6},{11,7},{12,8},{13,9},{1... | collective-permute-start | bytes 1179656 | tf_op jit(solution)/shard_map/ppermute | solution.py:242
  69.1 3.5 %collective-permute-start.4 = (bf16[192,1024]{1,0:T(8,128)(2,1)S(1)}, bf16[192,1024]{1,0:T(8,128)(2,1)}, u32[]{:S(2)}, u32[]{:S(2)}) collective-permute-start(bf16[192,1024]{1,0:T(8,128)(2,1)S(1)} %collective-permute-done.3.refs_3_), channel_id=1, source_target_pairs={{1,0},{2,1},{3,2},{0,3},{5,4},{6,5},{7,6},{4,7},{9,8},{10,9},{11,1... | collective-permute-start | bytes 1179656 | tf_op jit(solution)/shard_map/ppermute | solution.py:242
  72.6 3.3 %collective-permute-start.11 = (bf16[192,1024]{1,0:T(8,128)(2,1)S(1)}, bf16[192,1024]{1,0:T(8,128)(2,1)}, u32[]{:S(2)}, u32[]{:S(2)}) collective-permute-start(bf16[192,1024]{1,0:T(8,128)(2,1)S(1)} %collective-permute-done.7.refs_8_), channel_id=1, source_target_pairs={{12,0},{13,1},{14,2},{15,3},{0,4},{1,5},{2,6},{3,7},{4,8},{5,9},{6... | collective-permute-start | bytes 1179656 | tf_op jit(solution)/shard_map/ppermute | solution.py:242
  75.9 3.6 %collective-permute-start.8 = (bf16[192,1024]{1,0:T(8,128)(2,1)S(1)}, bf16[192,1024]{1,0:T(8,128)(2,1)}, u32[]{:S(2)}, u32[]{:S(2)}) collective-permute-start(bf16[192,1024]{1,0:T(8,128)(2,1)S(1)} %collective-permute-done.1.refs_1_), channel_id=1, source_target_pairs={{1,0},{2,1},{3,2},{0,3},{5,4},{6,5},{7,6},{4,7},{9,8},{10,9},{11,1... | collective-permute-start | bytes 1179656 | tf_op jit(solution)/shard_map/ppermute | solution.py:242
  79.6 4.3 %collective-permute-start.14 = (bf16[192,1024]{1,0:T(8,128)(2,1)}, bf16[192,1024]{1,0:T(8,128)(2,1)}, u32[]{:S(2)}, u32[]{:S(2)}) collective-permute-start(bf16[192,1024]{1,0:T(8,128)(2,1)} %collective-permute-done.6.refs_7_), channel_id=1, source_target_pairs={{4,0},{5,1},{6,2},{7,3},{8,4},{9,5},{10,6},{11,7},{12,8},{13,9},{1... | collective-permute-start | bytes 1179656 | tf_op jit(solution)/shard_map/ppermute | solution.py:242
  83.9 3.7 %collective-permute-start.9 = (bf16[192,1024]{1,0:T(8,128)(2,1)}, bf16[192,1024]{1,0:T(8,128)(2,1)}, u32[]{:S(2)}, u32[]{:S(2)}) collective-permute-start(bf16[192,1024]{1,0:T(8,128)(2,1)} %collective-permute-done.6.refs_7_), channel_id=1, source_target_pairs={{3,0},{0,1},{1,2},{2,3},{7,4},{4,5},{5,6},{6,7},{11,8},{8,9},{9,10... | collective-permute-start | bytes 1179656 | tf_op jit(solution)/shard_map/ppermute | solution.py:242
  87.7 5.2 %collective-permute-start.13 = (bf16[192,1024]{1,0:T(8,128)(2,1)}, bf16[192,1024]{1,0:T(8,128)(2,1)}, u32[]{:S(2)}, u32[]{:S(2)}) collective-permute-start(bf16[192,1024]{1,0:T(8,128)(2,1)} %collective-permute-done.5.refs_6_), channel_id=1, source_target_pairs={{3,0},{0,1},{1,2},{2,3},{7,4},{4,5},{5,6},{6,7},{11,8},{8,9},{9,10... | collective-permute-start | bytes 1179656 | tf_op jit(solution)/shard_map/ppermute | solution.py:242
  98.2 5.7 %collective-permute-done.13.refs_14_ = bf16[192,1024]{1,0:T(8,128)(2,1)} collective-permute-done((bf16[192,1024]{1,0:T(8,128)(2,1)}, bf16[192,1024]{1,0:T(8,128)(2,1)}, u32[]{:S(2)}, u32[]{:S(2)}) %collective-permute-start.13) | collective-permute-done | bytes 393248 | tf_op jit(solution)/shard_map/ppermute | solution.py:242
  103.9 31.7 %attend.1 = (bf16[3072,256]{1,0:T(8,128)(2,1)}, bf16[32,48,128]{2,1,0:T(8,128)(2,1)S(1)}) custom-call(s32[48,8]{1,0:T(8,128)S(1)} %bitcast.79, s32[48]{0:T(128)S(1)} %bitcast.81, s32[16]{0:T(128)S(1)} %fusion.6.owner_ref, s32[1,3072]{1,0:T(1,128)S(1)} %add.126.ids_ref, bf16[32,48,128]{2,1,0:T(8,128)(2,1)S(1)} %all-to-all-done.w_ref, ...), custom_call_target="tpu_custom_call" | custom-call | tf_op jit(solution)/shard_map/attend/pallas_call | solution.py:155
  139.0 3.3 %collective-permute-start.16 = (bf16[8,48,128]{2,1,0:T(8,128)(2,1)S(1)}, bf16[8,48,128]{2,1,0:T(8,128)(2,1)S(1)}, u32[]{:S(2)}, u32[]{:S(2)}) collective-permute-start(bf16[8,48,128]{2,1,0:T(8,128)(2,1)S(1)} %dynamic-slice_bitcast_fusion.1), channel_id=1, source_target_pairs={{0,32},{16,48},{32,0},{48,16},{64,96},{80,112},{96,64},{112,80},{1... | collective-permute-start | bytes 294920 | tf_op jit(solution)/shard_map/ppermute | solution.py:225
  142.4 3.4 %collective-permute-done.16 = bf16[8,48,128]{2,1,0:T(8,128)(2,1)S(1)} collective-permute-done((bf16[8,48,128]{2,1,0:T(8,128)(2,1)S(1)}, bf16[8,48,128]{2,1,0:T(8,128)(2,1)S(1)}, u32[]{:S(2)}, u32[]{:S(2)}) %collective-permute-start.16) | collective-permute-done | bytes 98336 | tf_op jit(solution)/shard_map/ppermute | solution.py:225
  145.8 4.2 %collective-permute-start.17 = (bf16[4,48,128]{2,1,0:T(8,128)(2,1)S(1)}, bf16[4,48,128]{2,1,0:T(8,128)(2,1)S(1)}, u32[]{:S(2)}, u32[]{:S(2)}) collective-permute-start(bf16[4,48,128]{2,1,0:T(8,128)(2,1)S(1)} %dynamic-slice_bitcast_fusion.2), channel_id=1, source_target_pairs={{0,64},{16,80},{32,96},{48,112},{64,0},{80,16},{96,32},{112,48},{1... | collective-permute-start | bytes 147464 | tf_op jit(solution)/shard_map/ppermute | solution.py:225
  150.0 7.8 %all-to-all-start.2 = ((bf16[16,192,256]{2,1,0:T(8,128)(2,1)}), bf16[16,192,256]{2,1,0:T(8,128)(2,1)S(1)}, u32[]{:S(2)}, u32[]{:S(2)}) async-start(bf16[16,192,256]{2,1,0:T(8,128)(2,1)} %bitcast.10), calls=%async_computation.2 | async-start | bytes 3145728 | tf_op jit(solution)/shard_map/all_to_all | solution.py:271
  157.9 7.3 %collective-permute-start.18 = (bf16[2,48,128]{2,1,0:T(8,128)(2,1)S(1)}, bf16[2,48,128]{2,1,0:T(8,128)(2,1)S(1)}, u32[]{:S(2)}, u32[]{:S(2)}) collective-permute-start(bf16[2,48,128]{2,1,0:T(8,128)(2,1)S(1)} %dynamic-slice_bitcast_fusion.3), channel_id=1, source_target_pairs={{0,128},{16,144},{32,160},{48,176},{64,192},{80,208},{96,224},{112... | collective-permute-start | bytes 73736 | tf_op jit(solution)/shard_map/ppermute | solution.py:225
  167.6 10.3 %collective-permute-start.19 = (bf16[1,48,128]{2,1,0:T(8,128)(2,1)S(1)}, bf16[1,48,128]{2,1,0:T(8,128)(2,1)S(1)}, u32[]{:S(2)}, u32[]{:S(2)}) collective-permute-start(bf16[1,48,128]{2,1,0:T(8,128)(2,1)S(1)} %constant_dynamic-slice_fusion.1), channel_id=1, source_target_pairs={{0,256},{16,272},{32,288},{48,304},{64,320},{80,336},{96,352},{112... | collective-permute-start | bytes 36872 | tf_op jit(solution)/shard_map/ppermute | solution.py:225
  177.9 4.1 %collective-permute-done.19 = bf16[1,48,128]{2,1,0:T(8,128)(2,1)S(1)} collective-permute-done((bf16[1,48,128]{2,1,0:T(8,128)(2,1)S(1)}, bf16[1,48,128]{2,1,0:T(8,128)(2,1)S(1)}, u32[]{:S(2)}, u32[]{:S(2)}) %collective-permute-start.19) | collective-permute-done | bytes 12320 | tf_op jit(solution)/shard_map/ppermute | solution.py:225
  185.6 3.1 %finish.1 = (bf16[192,1024]{1,0:T(8,128)(2,1)}, bf16[192,1024]{1,0:T(8,128)(2,1)}) custom-call(bf16[16,192,256]{2,1,0:T(8,128)(2,1)S(1)} %all-to-all-done.2.g_ref, bf16[1024,3072]{1,0:T(8,128)(2,1)S(1)} %copy-done), custom_call_target="tpu_custom_call" | custom-call | tf_op jit(solution)/shard_map/finish/pallas_call | solution.py:202
  (81 shorter events, 28.3 us)
Async XLA Ops:
  7.2 175.6 %all-gather.2.cloned.1.call-start = ((), (), s32[]{:S(2)}) async-start(), calls=%async_computation.3 | async-start | bytes 6488064 | tf_op jit(solution)/shard_map/all_gather | solution.py:269
  9.6 18.6 %collective-permute-start = (bf16[192,1024]{1,0:T(8,128)(2,1)S(1)}, bf16[192,1024]{1,0:T(8,128)(2,1)S(1)}, u32[]{:S(2)}, u32[]{:S(2)}) collective-permute-start(bf16[192,1024]{1,0:T(8,128)(2,1)S(1)} %bitcast.72), channel_id=1, source_target_pairs={{12,0},{13,1},{14,2},{15,3},{0,4},{1,5},{2,6},{3,7},{4,8},{5,9},{6... | collective-permute-start | bytes 1179656 | tf_op jit(solution)/shard_map/ppermute | solution.py:242
  13.3 41.5 %collective-permute-start.1 = (bf16[192,1024]{1,0:T(8,128)(2,1)S(1)}, bf16[192,1024]{1,0:T(8,128)(2,1)S(1)}, u32[]{:S(2)}, u32[]{:S(2)}) collective-permute-start(bf16[192,1024]{1,0:T(8,128)(2,1)S(1)} %bitcast.73), channel_id=1, source_target_pairs={{1,0},{2,1},{3,2},{0,3},{5,4},{6,5},{7,6},{4,7},{9,8},{10,9},{11,1... | collective-permute-start | bytes 1179656 | tf_op jit(solution)/shard_map/ppermute | solution.py:242
  20.5 14.8 %all-to-all-start.1 = ((bf16[16,192,64]{1,2,0:T(8,128)(2,1)}), bf16[16,192,64]{1,2,0:T(8,128)(2,1)S(1)}, u32[]{:S(2)}, u32[]{:S(2)}) async-start(bf16[16,192,64]{1,2,0:T(8,128)(2,1)} %bitcast.7), calls=%async_computation.1 | async-start | bytes 1048576 | tf_op jit(solution)/shard_map/all_to_all | solution.py:260
  35.3 68.5 %all-to-all-start = ((bf16[32,48,128]{2,1,0:T(8,128)(2,1)}), bf16[32,48,128]{2,1,0:T(8,128)(2,1)S(1)}, u32[]{:S(2)}, u32[]{:S(2)}) async-start(bf16[32,48,128]{2,1,0:T(8,128)(2,1)} %broadcast_in_dim.2), calls=%async_computation | async-start | bytes 786432 | tf_op jit(solution)/shard_map/all_to_all | solution.py:264
  49.1 13.8 %collective-permute-start.2 = (bf16[192,1024]{1,0:T(8,128)(2,1)S(1)}, bf16[192,1024]{1,0:T(8,128)(2,1)S(1)}, u32[]{:S(2)}, u32[]{:S(2)}) collective-permute-start(bf16[192,1024]{1,0:T(8,128)(2,1)S(1)} %bitcast.74), channel_id=1, source_target_pairs={{3,0},{0,1},{1,2},{2,3},{7,4},{4,5},{5,6},{6,7},{11,8},{8,9},{9,10... | collective-permute-start | bytes 1179656 | tf_op jit(solution)/shard_map/ppermute | solution.py:242
  51.5 15.4 %collective-permute-start.3 = (bf16[192,1024]{1,0:T(8,128)(2,1)S(1)}, bf16[192,1024]{1,0:T(8,128)(2,1)S(1)}, u32[]{:S(2)}, u32[]{:S(2)}) collective-permute-start(bf16[192,1024]{1,0:T(8,128)(2,1)S(1)} %bitcast.75), channel_id=1, source_target_pairs={{4,0},{5,1},{6,2},{7,3},{8,4},{9,5},{10,6},{11,7},{12,8},{13,9},{1... | collective-permute-start | bytes 1179656 | tf_op jit(solution)/shard_map/ppermute | solution.py:242
  54.8 17.8 %collective-permute-start.7 = (bf16[192,1024]{1,0:T(8,128)(2,1)S(1)}, bf16[192,1024]{1,0:T(8,128)(2,1)S(1)}, u32[]{:S(2)}, u32[]{:S(2)}) collective-permute-start(bf16[192,1024]{1,0:T(8,128)(2,1)S(1)} %collective-permute-done.1.refs_1_), channel_id=1, source_target_pairs={{12,0},{13,1},{14,2},{15,3},{0,4},{1,5},{2,6},{3,7},{4,8},{5,9},{6... | collective-permute-start | bytes 1179656 | tf_op jit(solution)/shard_map/ppermute | solution.py:242
  57.4 18.5 %collective-permute-start.5 = (bf16[192,1024]{1,0:T(8,128)(2,1)S(1)}, bf16[192,1024]{1,0:T(8,128)(2,1)}, u32[]{:S(2)}, u32[]{:S(2)}) collective-permute-start(bf16[192,1024]{1,0:T(8,128)(2,1)S(1)} %collective-permute-done.refs_4_), channel_id=1, source_target_pairs={{3,0},{0,1},{1,2},{2,3},{7,4},{4,5},{5,6},{6,7},{11,8},{8,9},{9,10... | collective-permute-start | bytes 1179656 | tf_op jit(solution)/shard_map/ppermute | solution.py:242
  62.9 16.7 %collective-permute-start.6 = (bf16[192,1024]{1,0:T(8,128)(2,1)S(1)}, bf16[192,1024]{1,0:T(8,128)(2,1)}, u32[]{:S(2)}, u32[]{:S(2)}) collective-permute-start(bf16[192,1024]{1,0:T(8,128)(2,1)S(1)} %collective-permute-done.2.refs_2_), channel_id=1, source_target_pairs={{4,0},{5,1},{6,2},{7,3},{8,4},{9,5},{10,6},{11,7},{12,8},{13,9},{1... | collective-permute-start | bytes 1179656 | tf_op jit(solution)/shard_map/ppermute | solution.py:242
  67.0 17.0 %collective-permute-start.10 = (bf16[192,1024]{1,0:T(8,128)(2,1)S(1)}, bf16[192,1024]{1,0:T(8,128)(2,1)}, u32[]{:S(2)}, u32[]{:S(2)}) collective-permute-start(bf16[192,1024]{1,0:T(8,128)(2,1)S(1)} %collective-permute-done.3.refs_3_), channel_id=1, source_target_pairs={{4,0},{5,1},{6,2},{7,3},{8,4},{9,5},{10,6},{11,7},{12,8},{13,9},{1... | collective-permute-start | bytes 1179656 | tf_op jit(solution)/shard_map/ppermute | solution.py:242
  69.1 18.6 %collective-permute-start.4 = (bf16[192,1024]{1,0:T(8,128)(2,1)S(1)}, bf16[192,1024]{1,0:T(8,128)(2,1)}, u32[]{:S(2)}, u32[]{:S(2)}) collective-permute-start(bf16[192,1024]{1,0:T(8,128)(2,1)S(1)} %collective-permute-done.3.refs_3_), channel_id=1, source_target_pairs={{1,0},{2,1},{3,2},{0,3},{5,4},{6,5},{7,6},{4,7},{9,8},{10,9},{11,1... | collective-permute-start | bytes 1179656 | tf_op jit(solution)/shard_map/ppermute | solution.py:242
  72.6 20.3 %collective-permute-start.11 = (bf16[192,1024]{1,0:T(8,128)(2,1)S(1)}, bf16[192,1024]{1,0:T(8,128)(2,1)}, u32[]{:S(2)}, u32[]{:S(2)}) collective-permute-start(bf16[192,1024]{1,0:T(8,128)(2,1)S(1)} %collective-permute-done.7.refs_8_), channel_id=1, source_target_pairs={{12,0},{13,1},{14,2},{15,3},{0,4},{1,5},{2,6},{3,7},{4,8},{5,9},{6... | collective-permute-start | bytes 1179656 | tf_op jit(solution)/shard_map/ppermute | solution.py:242
  75.9 22.2 %collective-permute-start.8 = (bf16[192,1024]{1,0:T(8,128)(2,1)S(1)}, bf16[192,1024]{1,0:T(8,128)(2,1)}, u32[]{:S(2)}, u32[]{:S(2)}) collective-permute-start(bf16[192,1024]{1,0:T(8,128)(2,1)S(1)} %collective-permute-done.1.refs_1_), channel_id=1, source_target_pairs={{1,0},{2,1},{3,2},{0,3},{5,4},{6,5},{7,6},{4,7},{9,8},{10,9},{11,1... | collective-permute-start | bytes 1179656 | tf_op jit(solution)/shard_map/ppermute | solution.py:242
  79.6 24.2 %collective-permute-start.14 = (bf16[192,1024]{1,0:T(8,128)(2,1)}, bf16[192,1024]{1,0:T(8,128)(2,1)}, u32[]{:S(2)}, u32[]{:S(2)}) collective-permute-start(bf16[192,1024]{1,0:T(8,128)(2,1)} %collective-permute-done.6.refs_7_), channel_id=1, source_target_pairs={{4,0},{5,1},{6,2},{7,3},{8,4},{9,5},{10,6},{11,7},{12,8},{13,9},{1... | collective-permute-start | bytes 1179656 | tf_op jit(solution)/shard_map/ppermute | solution.py:242
  83.9 19.9 %collective-permute-start.9 = (bf16[192,1024]{1,0:T(8,128)(2,1)}, bf16[192,1024]{1,0:T(8,128)(2,1)}, u32[]{:S(2)}, u32[]{:S(2)}) collective-permute-start(bf16[192,1024]{1,0:T(8,128)(2,1)} %collective-permute-done.6.refs_7_), channel_id=1, source_target_pairs={{3,0},{0,1},{1,2},{2,3},{7,4},{4,5},{5,6},{6,7},{11,8},{8,9},{9,10... | collective-permute-start | bytes 1179656 | tf_op jit(solution)/shard_map/ppermute | solution.py:242
  87.7 16.1 %collective-permute-start.13 = (bf16[192,1024]{1,0:T(8,128)(2,1)}, bf16[192,1024]{1,0:T(8,128)(2,1)}, u32[]{:S(2)}, u32[]{:S(2)}) collective-permute-start(bf16[192,1024]{1,0:T(8,128)(2,1)} %collective-permute-done.5.refs_6_), channel_id=1, source_target_pairs={{3,0},{0,1},{1,2},{2,3},{7,4},{4,5},{5,6},{6,7},{11,8},{8,9},{9,10... | collective-permute-start | bytes 1179656 | tf_op jit(solution)/shard_map/ppermute | solution.py:242
  92.9 11.0 %collective-permute-start.12 = (bf16[192,1024]{1,0:T(8,128)(2,1)}, bf16[192,1024]{1,0:T(8,128)(2,1)}, u32[]{:S(2)}, u32[]{:S(2)}) collective-permute-start(bf16[192,1024]{1,0:T(8,128)(2,1)} %collective-permute-done.11.refs_12_), channel_id=1, source_target_pairs={{1,0},{2,1},{3,2},{0,3},{5,4},{6,5},{7,6},{4,7},{9,8},{10,9},{11,1... | collective-permute-start | bytes 1179656 | tf_op jit(solution)/shard_map/ppermute | solution.py:242
  135.6 3.3 %collective-permute-start.15 = (bf16[16,48,128]{2,1,0:T(8,128)(2,1)S(1)}, bf16[16,48,128]{2,1,0:T(8,128)(2,1)S(1)}, u32[]{:S(2)}, u32[]{:S(2)}) collective-permute-start(bf16[16,48,128]{2,1,0:T(8,128)(2,1)S(1)} %dynamic-slice_bitcast_fusion), channel_id=1, source_target_pairs={{0,16},{16,0},{32,48},{48,32},{64,80},{80,64},{96,112},{112,96},{1... | collective-permute-start | bytes 589832 | tf_op jit(solution)/shard_map/ppermute | solution.py:225
  139.0 6.7 %collective-permute-start.16 = (bf16[8,48,128]{2,1,0:T(8,128)(2,1)S(1)}, bf16[8,48,128]{2,1,0:T(8,128)(2,1)S(1)}, u32[]{:S(2)}, u32[]{:S(2)}) collective-permute-start(bf16[8,48,128]{2,1,0:T(8,128)(2,1)S(1)} %dynamic-slice_bitcast_fusion.1), channel_id=1, source_target_pairs={{0,32},{16,48},{32,0},{48,16},{64,96},{80,112},{96,64},{112,80},{1... | collective-permute-start | bytes 294920 | tf_op jit(solution)/shard_map/ppermute | solution.py:225
  145.8 12.0 %collective-permute-start.17 = (bf16[4,48,128]{2,1,0:T(8,128)(2,1)S(1)}, bf16[4,48,128]{2,1,0:T(8,128)(2,1)S(1)}, u32[]{:S(2)}, u32[]{:S(2)}) collective-permute-start(bf16[4,48,128]{2,1,0:T(8,128)(2,1)S(1)} %dynamic-slice_bitcast_fusion.2), channel_id=1, source_target_pairs={{0,64},{16,80},{32,96},{48,112},{64,0},{80,16},{96,32},{112,48},{1... | collective-permute-start | bytes 147464 | tf_op jit(solution)/shard_map/ppermute | solution.py:225
  150.0 32.8 %all-to-all-start.2 = ((bf16[16,192,256]{2,1,0:T(8,128)(2,1)}), bf16[16,192,256]{2,1,0:T(8,128)(2,1)S(1)}, u32[]{:S(2)}, u32[]{:S(2)}) async-start(bf16[16,192,256]{2,1,0:T(8,128)(2,1)} %bitcast.10), calls=%async_computation.2 | async-start | bytes 3145728 | tf_op jit(solution)/shard_map/all_to_all | solution.py:271
  157.9 9.6 %collective-permute-start.18 = (bf16[2,48,128]{2,1,0:T(8,128)(2,1)S(1)}, bf16[2,48,128]{2,1,0:T(8,128)(2,1)S(1)}, u32[]{:S(2)}, u32[]{:S(2)}) collective-permute-start(bf16[2,48,128]{2,1,0:T(8,128)(2,1)S(1)} %dynamic-slice_bitcast_fusion.3), channel_id=1, source_target_pairs={{0,128},{16,144},{32,160},{48,176},{64,192},{80,208},{96,224},{112... | collective-permute-start | bytes 73736 | tf_op jit(solution)/shard_map/ppermute | solution.py:225
  167.6 14.4 %collective-permute-start.19 = (bf16[1,48,128]{2,1,0:T(8,128)(2,1)S(1)}, bf16[1,48,128]{2,1,0:T(8,128)(2,1)S(1)}, u32[]{:S(2)}, u32[]{:S(2)}) collective-permute-start(bf16[1,48,128]{2,1,0:T(8,128)(2,1)S(1)} %constant_dynamic-slice_fusion.1), channel_id=1, source_target_pairs={{0,256},{16,272},{32,288},{48,304},{64,320},{80,336},{96,352},{112... | collective-permute-start | bytes 36872 | tf_op jit(solution)/shard_map/ppermute | solution.py:225
  (11 other events, 499.0 us)
Sparse Core Ops, SparseCore 0:
  10.1 94.7 all-gather.1

commit v4 on v3

--- a/solution.py
+++ b/solution.py
@@ -20,19 +20,16 @@
 )
 
 
-SECOND = 4
-
-
 def dot(a, b, ca=1, cb=0):
     return lax.dot_general(a, b, (((ca,), (cb,)), ((), ())), preferred_element_type=F32)
 
 
 def attend_kernel(
-    blocks_ref, counts_ref, owner_ref, ids_ref, w_ref, cot_ref, ocol_ref, orow_ref, *refs
+    blocks_ref, counts_ref, owner_ref, head_ref, ids_ref, cot_ref, ocol_ref, orow_ref, w_ref, *refs
 ):
     members = owner_ref.shape[0]
     parts_refs, refs = refs[:members], refs[members:]
-    (out_ref, gw_ref, feat_ref, wide_ref, x_ref, kv_ref, a_ref, acc_ref, g_ref, sum_ref, sem) = refs
+    (out_ref, gw_ref, feat_ref, wide_ref, pair_ref, x_ref, kv_ref, a_ref, acc_ref, g_ref, sum_ref, sem) = refs
     nodes = feat_ref.shape[0]
     clusters, slots = blocks_ref.shape
     rows = nodes // clusters
@@ -43,17 +40,25 @@
         pltpu.make_async_copy(part, feat_ref.at[pl.ds(k * local, local), :], sem.at[k])
         for k, part in enumerate(parts_refs)
     ]
-    for load in loads:
+    parts, tall, lanes = gw_ref.shape
+    deep = tall * 2 // 3
+    head = head_ref[0]
+    key_at = pl.multiple_of(head * lanes, lanes)
+    query_at = pl.multiple_of((HEADS + head // 2) * lanes, lanes)
+    weigh_in = [
+        pltpu.make_async_copy(
+            w_ref.at[:, pl.ds(key_at, lanes)], wide_ref.at[:, pl.ds(0, lanes)], sem.at[members]
+        ),
+        pltpu.make_async_copy(w_ref.at[:, pl.ds(query_at, lanes)], pair_ref, sem.at[members + 1]),
+    ]
+    for load in weigh_in + loads:
         load.start()
-
-    parts, tall, lanes = w_ref.shape
-    deep = tall * 2 // 3
-    width = parts * deep
-    wide_ref[:, :lanes] = w_ref[:, :deep, :].reshape(width, lanes)
-    packed = w_ref[:, deep:, :].astype(F32)
-    left = lax.broadcasted_iota(jnp.int32, packed.shape, 2) < HD
-    query = [jnp.where(left, packed, 0.0), jnp.where(left, pltpu.roll(packed, HD, 2), 0.0)]
-    wide_ref[:, lanes:] = jnp.concatenate(query, axis=1).reshape(width, lanes).astype(BF)
+    for load in weigh_in:
+        load.wait()
+    two = pair_ref[...].astype(F32)
+    mine = jnp.where(lax.rem(head, 2) == 0, two, pltpu.roll(two, HD, 1))
+    left = lax.broadcasted_iota(jnp.int32, two.shape, 1) < HD
+    wide_ref[:, lanes:] = jnp.where(left, mine * 0.125, 0.0).astype(BF)
     place = (
         lax.broadcasted_iota(jnp.int32, (HD, 4 * HD), 0) + 3 * HD
         == lax.broadcasted_iota(jnp.int32, (HD, 4 * HD), 1)
@@ -87,10 +92,10 @@
     lax.fori_loop(0, tiles, to_clusters, 0)
 
     acc_ref[...] = jnp.zeros_like(acc_ref)
-    key_at = lax.broadcasted_iota(jnp.int32, (rows, keys), 1)
+    place_of = lax.broadcasted_iota(jnp.int32, (rows, keys), 1)
 
     def weigh(both, c):
-        score = jnp.where(key_at < counts_ref[c] * rows, both[:rows], -1e30)
+        score = jnp.where(place_of < counts_ref[c] * rows, both[:rows], -1e30)
         dpw = both[rows:]
         raw = jnp.exp(score - jnp.max(score, axis=1, keepdims=True))
         p = raw * (1.0 / jnp.sum(raw, axis=1, keepdims=True))
@@ -142,13 +147,14 @@
     gw_ref[:, :deep, :] = sum_ref[:, :lanes].reshape(parts, deep, lanes).astype(BF)
     query = sum_ref[:, lanes:].reshape(parts, deep, lanes)
     low, high = query[:, : deep // 2], query[:, deep // 2 :]
+    left = lax.broadcasted_iota(jnp.int32, low.shape, 2) < HD
     gw_ref[:, deep:, :] = jnp.where(left, low, pltpu.roll(high, HD, 2)).astype(BF)
 
 
-def attend(blocks_of, owner, w_head, cot, order, blocks, counts):
+def attend(blocks_of, owner, head, weights, cot, order, blocks, counts, parts):
     local, width = blocks_of[0].shape
     nodes = len(blocks_of) * local
-    parts, tall, lanes = w_head.shape
+    tall, lanes = width // parts * 3 // 2, 2 * HD
     ids = (owner[:, None] * local + jnp.arange(local, dtype=jnp.int32)).reshape(1, nodes)
     vmem = pl.BlockSpec(memory_space=pltpu.VMEM)
     smem = pl.BlockSpec(memory_space=pltpu.SMEM)
@@ -159,27 +165,39 @@
             jax.ShapeDtypeStruct((nodes, 4 * HD), BF),
             jax.ShapeDtypeStruct((parts, tall, lanes), BF),
         ],
-        in_specs=[smem] * 3 + [vmem] * 5 + [pl.BlockSpec(memory_space=pl.ANY)] * len(blocks_of),
+        in_specs=[smem] * 4
+        + [vmem] * 4
+        + [pl.BlockSpec(memory_space=pl.ANY)] * (1 + len(blocks_of)),
         out_specs=[vmem, vmem],
         scratch_shapes=[
             pltpu.VMEM((nodes, width), BF),
             pltpu.VMEM((width, 4 * HD), BF),
+            pltpu.VMEM((width, 2 * HD), BF),
             pltpu.VMEM((nodes, 4 * HD), BF),
             pltpu.VMEM((nodes, 2 * HD), BF),
             pltpu.VMEM((2 * nodes, 2 * HD), BF),
             pltpu.VMEM((nodes, 2 * HD), F32),
             pltpu.VMEM((nodes, 4 * HD), BF),
             pltpu.VMEM((width, 4 * HD), F32),
-            pltpu.SemaphoreType.DMA((len(blocks_of),)),
+            pltpu.SemaphoreType.DMA((len(blocks_of) + 2,)),
         ],
         compiler_params=pltpu.CompilerParams(vmem_limit_bytes=52 << 20),
     )(
-        blocks, counts, owner, ids, w_head, cot,
-        order.reshape(nodes, 1), order.reshape(1, nodes), *blocks_of,
-    )
-
-
-def finish_kernel(g_ref, w_ref, att_ref, gf_ref, lhs_ref):
+        blocks, counts, owner, head.reshape(1), ids, cot,
+        order.reshape(nodes, 1), order.reshape(1, nodes), weights, *blocks_of,
+    )
+
+
+def finish_kernel(g_ref, w_ref, att_ref, gf_ref, lhs_ref, have_ref, sem):
+    bands = sem.shape[0]
+    band = w_ref.shape[0] // bands
+    cuts = [slice(i * band, (i + 1) * band) for i in range(bands)]
+    loads = [
+        pltpu.make_async_copy(w_ref.at[cut, :], have_ref.at[cut, :], sem.at[i])
+        for i, cut in enumerate(cuts)
+    ]
+    for load in loads:
+        load.start()
     heads = g_ref.shape[0]
     wide = heads * 2 * HD
     first = lax.broadcasted_iota(jnp.int32, (g_ref.shape[1], 2 * HD), 1) < HD
@@ -193,7 +211,9 @@
             first, even, pltpu.roll(odd, HD, 1)
         ).astype(BF)
         att_ref[:, to] = jnp.where(first, pltpu.roll(even, HD, 1), odd).astype(BF)
-    gf_ref[...] = dot(lhs_ref[...], w_ref[...], 1, 1).astype(BF)
+    for cut, load in zip(cuts, loads):
+        load.wait()
+        gf_ref[:, cut] = dot(lhs_ref[...], have_ref[cut, :], 1, 1).astype(BF)
 
 
 def finish(got, weights):
@@ -206,9 +226,13 @@
             jax.ShapeDtypeStruct((rows, HEADS * HD), BF),
             jax.ShapeDtypeStruct((rows, width), BF),
         ],
-        in_specs=[vmem, vmem],
+        in_specs=[vmem, pl.BlockSpec(memory_space=pl.ANY)],
         out_specs=[vmem, vmem],
-        scratch_shapes=[pltpu.VMEM((rows, weights.shape[1]), BF)],
+        scratch_shapes=[
+            pltpu.VMEM((rows, weights.shape[1]), BF),
+            pltpu.VMEM(weights.shape, BF),
+            pltpu.SemaphoreType.DMA((4,)),
+        ],
         compiler_params=pltpu.CompilerParams(vmem_limit_bytes=40 << 20),
     )(got, weights)
 
@@ -251,23 +275,25 @@
     deep = qkv_weight.shape[0]
     feats = features[0]
     head = lax.axis_index("seq")
-    own = lax.dynamic_slice(qkv_weight, (0, head * 3 * HD), (deep, 3 * HD))
-    query = own[:, :HD] * jnp.asarray(0.125, BF)
-    query = jnp.concatenate([query[: deep // 2], query[deep // 2 :]], axis=1)
-    own = jnp.concatenate([own[:, HD:], query], axis=0)
-    copies = jnp.broadcast_to(own[None], (lax.axis_size("dp"), *own.shape))
+    by_head = qkv_weight.reshape(deep, HEADS, 3 * HD)
+    ordered = jnp.concatenate(
+        [by_head[:, :, HD:].reshape(deep, -1), by_head[:, :, :HD].reshape(deep, -1)], axis=1
+    )
+    size = lax.axis_size("dp")
+    core = lax.rem(lax.axis_index("dp"), 2)
+    other = lax.ppermute(ordered, "dp", [(i, i ^ 1) for i in range(size)])
+    chip = jnp.where(
+        core == 0, jnp.stack([ordered, other]), jnp.stack([other, ordered])
+    ).reshape(2 * deep, -1)
+    groups = [list(range(c, size, 2)) for c in range(2)]
+    weights = lax.all_gather(chip, "dp", axis=0, tiled=True, axis_index_groups=groups)
     blocks_of, owner = gather_round(feats, "seq")
     cot = lax.all_to_all(
         cotangent[0].reshape(local_rows, HEADS, HD).transpose(1, 0, 2), "seq", 0, 0, tiled=True
     ).reshape(HEADS * local_rows, HD)
-    copies, _ = lax.optimization_barrier((copies, blocks_of[SECOND]))
-    w_head = lax.all_to_all(copies, "dp", 0, 0, tiled=True)
-    by_head = qkv_weight.reshape(deep, HEADS, 3 * HD)
-    ordered = jnp.concatenate(
-        [by_head[:, :, HD:].reshape(deep, -1), by_head[:, :, :HD].reshape(deep, -1)], axis=1
-    )
-    weights = lax.all_gather(ordered, "dp", axis=0, tiled=True)
-    grads, part = attend(blocks_of, owner, w_head, cot, node_order[0], blocks[0], counts[0])
+    grads, part = attend(
+        blocks_of, owner, head, weights, cot, node_order[0], blocks[0], counts[0], size
+    )
     got = lax.all_to_all(grads.reshape(HEADS, local_rows, 4 * HD), "seq", 0, 0, tiled=True)
     total = reduce_scatter(part, "dp")
     query = jnp.concatenate([total[deep:, :HD], total[deep:, HD:]], axis=0)

time: 197 us -> 197 us (level)
  the two profiles are of different devices: /device:TPU:2 before, /device:TPU:34 now
where the time goes in v4:
time: 197 us
  starting transfers between devices  89.4 us (45%)
  waiting for transfers between devices  45.1 us (23%)
  Pallas kernels  37 us (19%)
  between operations  14.7 us (7%)
  local copies, waits for them, and re-layouts  8.7 us (4%)
    ppermute x15, starting transfers between devices, gather_round(): held[(hy + dy) % SIDE, (hx + dx) % SIDE] = lax.ppermute(source, axis, pairs)  50.1 us
    pallas_call x1, Pallas kernels, attend(): pl.pallas_call(attend_kernel, name='attend', out_shape=[jax.ShapeDtypeStr...  31.3 us
    all_gather x1, waiting for transfers between devices, per_device(): lax.all_gather(chip, 'dp', axis=0, tiled=True, axis_index_groups=groups)  23.1 us
    ppermute x5, starting transfers between devices, reduce_scatter(): came = lax.ppermute(send, axis, [(i, i ^ bit) for i in range(size)])  23 us
    ppermute x5, waiting for transfers between devices, reduce_scatter(): came = lax.ppermute(send, axis, [(i, i ^ bit) for i in range(size)])  15.9 us
    all_to_all x1, starting transfers between devices, per_device(): lax.all_to_all(cotangent[0].reshape(local_rows, HEADS, HD).transpose(1, 0...  7.25 us
    all_to_all x1, starting transfers between devices, per_device(): lax.all_to_all(grads.reshape(HEADS, local_rows, 4 * HD), 'seq', 0, 0, til...  7.17 us
    pallas_call x1, Pallas kernels, finish(): pl.pallas_call(finish_kernel, name='finish', out_shape=[jax.ShapeDtypeStr...  5.72 us
  transfers between devices with their start and end apart: 24, of which 9 were waited for; matrix products, arithmetic and copies ran while one was open for 3% of the time, Pallas kernels for 0%

profile of v4, /device:TPU:34, one launch (start us, length us, event | category | flops | bytes accessed | tf_op | source)
XLA Modules:
  0.0 196.5 jit_solution(16427805887987635406)
XLA Ops:
  15.5 3.4 %collective-permute-start.2 = (bf16[192,1024]{1,0:T(8,128)(2,1)S(1)}, bf16[192,1024]{1,0:T(8,128)(2,1)S(1)}, u32[]{:S(2)}, u32[]{:S(2)}) collective-permute-start(bf16[192,1024]{1,0:T(8,128)(2,1)S(1)} %bitcast.78), channel_id=1, source_target_pairs={{3,0},{0,1},{1,2},{2,3},{7,4},{4,5},{5,6},{6,7},{11,8},{8,9},{9,10... | collective-permute-start | bytes 1179656 | tf_op jit(solution)/shard_map/ppermute | solution.py:266
  18.9 3.5 %collective-permute-start.4 = (bf16[192,1024]{1,0:T(8,128)(2,1)S(1)}, bf16[192,1024]{1,0:T(8,128)(2,1)S(1)}, u32[]{:S(2)}, u32[]{:S(2)}) collective-permute-start(bf16[192,1024]{1,0:T(8,128)(2,1)S(1)} %bitcast.79), channel_id=1, source_target_pairs={{12,0},{13,1},{14,2},{15,3},{0,4},{1,5},{2,6},{3,7},{4,8},{5,9},{6... | collective-permute-start | bytes 1179656 | tf_op jit(solution)/shard_map/ppermute | solution.py:266
  22.4 3.6 %collective-permute-start.3 = (bf16[192,1024]{1,0:T(8,128)(2,1)S(1)}, bf16[192,1024]{1,0:T(8,128)(2,1)S(1)}, u32[]{:S(2)}, u32[]{:S(2)}) collective-permute-start(bf16[192,1024]{1,0:T(8,128)(2,1)S(1)} %bitcast.80), channel_id=1, source_target_pairs={{4,0},{5,1},{6,2},{7,3},{8,4},{9,5},{10,6},{11,7},{12,8},{13,9},{1... | collective-permute-start | bytes 1179656 | tf_op jit(solution)/shard_map/ppermute | solution.py:266
  26.1 3.5 %collective-permute-start.8 = (bf16[192,1024]{1,0:T(8,128)(2,1)S(1)}, bf16[192,1024]{1,0:T(8,128)(2,1)S(1)}, u32[]{:S(2)}, u32[]{:S(2)}) collective-permute-start(bf16[192,1024]{1,0:T(8,128)(2,1)S(1)} %collective-permute-done.1.refs_1_), channel_id=1, source_target_pairs={{12,0},{13,1},{14,2},{15,3},{0,4},{1,5},{2,6},{3,7},{4,8},{5,9},{6... | collective-permute-start | bytes 1179656 | tf_op jit(solution)/shard_map/ppermute | solution.py:266
  29.6 4.6 %collective-permute-start.7 = (bf16[192,1024]{1,0:T(8,128)(2,1)S(1)}, bf16[192,1024]{1,0:T(8,128)(2,1)S(1)}, u32[]{:S(2)}, u32[]{:S(2)}) collective-permute-start(bf16[192,1024]{1,0:T(8,128)(2,1)S(1)} %collective-permute-done.2.refs_2_), channel_id=1, source_target_pairs={{4,0},{5,1},{6,2},{7,3},{8,4},{9,5},{10,6},{11,7},{12,8},{13,9},{1... | collective-permute-start | bytes 1179656 | tf_op jit(solution)/shard_map/ppermute | solution.py:266
  34.2 3.2 %collective-permute-start.6 = (bf16[192,1024]{1,0:T(8,128)(2,1)S(1)}, bf16[192,1024]{1,0:T(8,128)(2,1)}, u32[]{:S(2)}, u32[]{:S(2)}) collective-permute-start(bf16[192,1024]{1,0:T(8,128)(2,1)S(1)} %collective-permute-done.4.refs_4_), channel_id=1, source_target_pairs={{3,0},{0,1},{1,2},{2,3},{7,4},{4,5},{5,6},{6,7},{11,8},{8,9},{9,10... | collective-permute-start | bytes 1179656 | tf_op jit(solution)/shard_map/ppermute | solution.py:266
  37.5 3.7 %collective-permute-start.11 = (bf16[192,1024]{1,0:T(8,128)(2,1)S(1)}, bf16[192,1024]{1,0:T(8,128)(2,1)}, u32[]{:S(2)}, u32[]{:S(2)}) collective-permute-start(bf16[192,1024]{1,0:T(8,128)(2,1)S(1)} %collective-permute-done.3.refs_3_), channel_id=1, source_target_pairs={{4,0},{5,1},{6,2},{7,3},{8,4},{9,5},{10,6},{11,7},{12,8},{13,9},{1... | collective-permute-start | bytes 1179656 | tf_op jit(solution)/shard_map/ppermute | solution.py:266
  43.7 3.2 %collective-permute-start.12 = (bf16[192,1024]{1,0:T(8,128)(2,1)S(1)}, bf16[192,1024]{1,0:T(8,128)(2,1)}, u32[]{:S(2)}, u32[]{:S(2)}) collective-permute-start(bf16[192,1024]{1,0:T(8,128)(2,1)S(1)} %collective-permute-done.8.refs_8_), channel_id=1, source_target_pairs={{12,0},{13,1},{14,2},{15,3},{0,4},{1,5},{2,6},{3,7},{4,8},{5,9},{6... | collective-permute-start | bytes 1179656 | tf_op jit(solution)/shard_map/ppermute | solution.py:266
  48.0 7.2 %all-to-all-start = ((bf16[16,192,64]{1,2,0:T(8,128)(2,1)}), bf16[16,192,64]{1,2,0:T(8,128)(2,1)S(1)}, u32[]{:S(2)}, u32[]{:S(2)}) async-start(bf16[16,192,64]{1,2,0:T(8,128)(2,1)} %bitcast.7), calls=%async_computation | async-start | bytes 1048576 | tf_op jit(solution)/shard_map/all_to_all | solution.py:291
  57.4 3.8 %collective-permute-start.10 = (bf16[192,1024]{1,0:T(8,128)(2,1)S(1)}, bf16[192,1024]{1,0:T(8,128)(2,1)}, u32[]{:S(2)}, u32[]{:S(2)}) collective-permute-start(bf16[192,1024]{1,0:T(8,128)(2,1)S(1)} %collective-permute-done.7.refs_7_), channel_id=1, source_target_pairs={{3,0},{0,1},{1,2},{2,3},{7,4},{4,5},{5,6},{6,7},{11,8},{8,9},{9,10... | collective-permute-start | bytes 1179656 | tf_op jit(solution)/shard_map/ppermute | solution.py:266
  61.2 4.6 %collective-permute-start.15 = (bf16[192,1024]{1,0:T(8,128)(2,1)S(1)}, bf16[192,1024]{1,0:T(8,128)(2,1)}, u32[]{:S(2)}, u32[]{:S(2)}) collective-permute-start(bf16[192,1024]{1,0:T(8,128)(2,1)S(1)} %collective-permute-done.7.refs_7_), channel_id=1, source_target_pairs={{4,0},{5,1},{6,2},{7,3},{8,4},{9,5},{10,6},{11,7},{12,8},{13,9},{1... | collective-permute-start | bytes 1179656 | tf_op jit(solution)/shard_map/ppermute | solution.py:266
  65.8 3.4 %collective-permute-start.14 = (bf16[192,1024]{1,0:T(8,128)(2,1)}, bf16[192,1024]{1,0:T(8,128)(2,1)}, u32[]{:S(2)}, u32[]{:S(2)}) collective-permute-start(bf16[192,1024]{1,0:T(8,128)(2,1)} %collective-permute-done.6.refs_6_), channel_id=1, source_target_pairs={{3,0},{0,1},{1,2},{2,3},{7,4},{4,5},{5,6},{6,7},{11,8},{8,9},{9,10... | collective-permute-start | bytes 1179656 | tf_op jit(solution)/shard_map/ppermute | solution.py:266
  76.8 2.8 %collective-permute-done.13.refs_13_ = bf16[192,1024]{1,0:T(8,128)(2,1)} collective-permute-done((bf16[192,1024]{1,0:T(8,128)(2,1)}, bf16[192,1024]{1,0:T(8,128)(2,1)}, u32[]{:S(2)}, u32[]{:S(2)}) %collective-permute-start.13) | collective-permute-done | bytes 393248 | tf_op jit(solution)/shard_map/ppermute | solution.py:266
  79.6 23.1 %all-gather.2.cloned.1.call-done.w_ref = bf16[1024,3072]{1,0:T(8,128)(2,1)} async-done(((bf16[64,3072]{1,0:T(8,128)(2,1)}), bf16[1024,3072]{1,0:T(8,128)(2,1)}) %all-gather.2.cloned.1.call-update) | async-done | bytes 6291472 | tf_op jit(solution)/shard_map/all_gather | solution.py:289
  102.6 31.3 %attend.1 = (bf16[3072,256]{1,0:T(8,128)(2,1)}, bf16[32,48,128]{2,1,0:T(8,128)(2,1)S(1)}) custom-call(s32[48,8]{1,0:T(8,128)S(1)} %bitcast.82, s32[48]{0:T(128)S(1)} %bitcast.84, s32[16]{0:T(128)S(1)} %fusion.6.owner_ref, s32[1]{0:T(128)} %bitcast.4.head_ref, s32[1,3072]{1,0:T(1,128)S(1)} %add.123.ids_ref, bf16[3072,64]{1,0:T(8,128)(2,1)} %bitcast.85, ...), custom_call_target="tpu_custom_call" | custom-call | tf_op jit(solution)/shard_map/attend/pallas_call | solution.py:161
  137.4 3.3 %collective-permute-start.17 = (bf16[8,48,128]{2,1,0:T(8,128)(2,1)S(1)}, bf16[8,48,128]{2,1,0:T(8,128)(2,1)S(1)}, u32[]{:S(2)}, u32[]{:S(2)}) collective-permute-start(bf16[8,48,128]{2,1,0:T(8,128)(2,1)S(1)} %dynamic-slice_bitcast_fusion.1), channel_id=1, source_target_pairs={{0,32},{16,48},{32,0},{48,16},{64,96},{80,112},{96,64},{112,80},{1... | collective-permute-start | bytes 294920 | tf_op jit(solution)/shard_map/ppermute | solution.py:249
  140.7 3.4 %collective-permute-done.17 = bf16[8,48,128]{2,1,0:T(8,128)(2,1)S(1)} collective-permute-done((bf16[8,48,128]{2,1,0:T(8,128)(2,1)S(1)}, bf16[8,48,128]{2,1,0:T(8,128)(2,1)S(1)}, u32[]{:S(2)}, u32[]{:S(2)}) %collective-permute-start.17) | collective-permute-done | bytes 98336 | tf_op jit(solution)/shard_map/ppermute | solution.py:249
  144.1 4.4 %collective-permute-start.18 = (bf16[4,48,128]{2,1,0:T(8,128)(2,1)S(1)}, bf16[4,48,128]{2,1,0:T(8,128)(2,1)S(1)}, u32[]{:S(2)}, u32[]{:S(2)}) collective-permute-start(bf16[4,48,128]{2,1,0:T(8,128)(2,1)S(1)} %dynamic-slice_bitcast_fusion.2), channel_id=1, source_target_pairs={{0,64},{16,80},{32,96},{48,112},{64,0},{80,16},{96,32},{112,48},{1... | collective-permute-start | bytes 147464 | tf_op jit(solution)/shard_map/ppermute | solution.py:249
  148.5 7.2 %all-to-all-start.1 = ((bf16[16,192,256]{2,1,0:T(8,128)(2,1)}), bf16[16,192,256]{2,1,0:T(8,128)(2,1)S(1)}, u32[]{:S(2)}, u32[]{:S(2)}) async-start(bf16[16,192,256]{2,1,0:T(8,128)(2,1)} %bitcast.14), calls=%async_computation.1 | async-start | bytes 3145728 | tf_op jit(solution)/shard_map/all_to_all | solution.py:297
  155.8 6.1 %collective-permute-start.19 = (bf16[2,48,128]{2,1,0:T(8,128)(2,1)S(1)}, bf16[2,48,128]{2,1,0:T(8,128)(2,1)S(1)}, u32[]{:S(2)}, u32[]{:S(2)}) collective-permute-start(bf16[2,48,128]{2,1,0:T(8,128)(2,1)S(1)} %dynamic-slice_bitcast_fusion.3), channel_id=1, source_target_pairs={{0,128},{16,144},{32,160},{48,176},{64,192},{80,208},{96,224},{112... | collective-permute-start | bytes 73736 | tf_op jit(solution)/shard_map/ppermute | solution.py:249
  161.9 3.9 %collective-permute-done.19 = bf16[2,48,128]{2,1,0:T(8,128)(2,1)S(1)} collective-permute-done((bf16[2,48,128]{2,1,0:T(8,128)(2,1)S(1)}, bf16[2,48,128]{2,1,0:T(8,128)(2,1)S(1)}, u32[]{:S(2)}, u32[]{:S(2)}) %collective-permute-start.19) | collective-permute-done | bytes 24608 | tf_op jit(solution)/shard_map/ppermute | solution.py:249
  165.8 7.3 %collective-permute-start.20 = (bf16[1,48,128]{2,1,0:T(8,128)(2,1)S(1)}, bf16[1,48,128]{2,1,0:T(8,128)(2,1)S(1)}, u32[]{:S(2)}, u32[]{:S(2)}) collective-permute-start(bf16[1,48,128]{2,1,0:T(8,128)(2,1)S(1)} %constant_dynamic-slice_fusion), channel_id=1, source_target_pairs={{0,256},{16,272},{32,288},{48,304},{64,320},{80,336},{96,352},{112... | collective-permute-start | bytes 36872 | tf_op jit(solution)/shard_map/ppermute | solution.py:249
  173.1 7.2 %collective-permute-done.20 = bf16[1,48,128]{2,1,0:T(8,128)(2,1)S(1)} collective-permute-done((bf16[1,48,128]{2,1,0:T(8,128)(2,1)S(1)}, bf16[1,48,128]{2,1,0:T(8,128)(2,1)S(1)}, u32[]{:S(2)}, u32[]{:S(2)}) %collective-permute-start.20) | collective-permute-done | bytes 12320 | tf_op jit(solution)/shard_map/ppermute | solution.py:249
  183.9 5.7 %finish.1 = (bf16[192,1024]{1,0:T(8,128)(2,1)}, bf16[192,1024]{1,0:T(8,128)(2,1)}) custom-call(bf16[16,192,256]{2,1,0:T(8,128)(2,1)S(1)} %all-to-all-done.1.g_ref, bf16[1024,3072]{1,0:T(8,128)(2,1)S(1)} %copy-done), custom_call_target="tpu_custom_call" | custom-call | tf_op jit(solution)/shard_map/finish/pallas_call | solution.py:222
  (77 shorter events, 28.6 us)
Async XLA Ops:
  7.2 95.5 %all-gather.2.cloned.1.call-start = ((), (), s32[]{:S(2)}) async-start(), calls=%async_computation.2 | async-start | bytes 6684672 | tf_op jit(solution)/shard_map/all_gather | solution.py:289
  8.9 3.3 %collective-permute-start = (bf16[32,3072]{1,0:T(8,128)(2,1)S(1)}, bf16[32,3072]{1,0:T(8,128)(2,1)S(1)}, u32[]{:S(2)}, u32[]{:S(2)}) collective-permute-start(bf16[32,3072]{1,0:T(8,128)(2,1)S(1)} %constant_dynamic-update-slice_fusion), channel_id=1, source_target_pairs={{0,16},{16,0},{32,48},{48,32},{64,80},{80,64},{96,112},{112,96},{1... | collective-permute-start | bytes 589832 | tf_op jit(solution)/shard_map/ppermute | solution.py:284
  13.1 13.1 %collective-permute-start.1 = (bf16[192,1024]{1,0:T(8,128)(2,1)S(1)}, bf16[192,1024]{1,0:T(8,128)(2,1)S(1)}, u32[]{:S(2)}, u32[]{:S(2)}) collective-permute-start(bf16[192,1024]{1,0:T(8,128)(2,1)S(1)} %bitcast.77), channel_id=1, source_target_pairs={{1,0},{2,1},{3,2},{0,3},{5,4},{6,5},{7,6},{4,7},{9,8},{10,9},{11,1... | collective-permute-start | bytes 1179656 | tf_op jit(solution)/shard_map/ppermute | solution.py:266
  15.5 14.1 %collective-permute-start.2 = (bf16[192,1024]{1,0:T(8,128)(2,1)S(1)}, bf16[192,1024]{1,0:T(8,128)(2,1)S(1)}, u32[]{:S(2)}, u32[]{:S(2)}) collective-permute-start(bf16[192,1024]{1,0:T(8,128)(2,1)S(1)} %bitcast.78), channel_id=1, source_target_pairs={{3,0},{0,1},{1,2},{2,3},{7,4},{4,5},{5,6},{6,7},{11,8},{8,9},{9,10... | collective-permute-start | bytes 1179656 | tf_op jit(solution)/shard_map/ppermute | solution.py:266
  18.9 15.3 %collective-permute-start.4 = (bf16[192,1024]{1,0:T(8,128)(2,1)S(1)}, bf16[192,1024]{1,0:T(8,128)(2,1)S(1)}, u32[]{:S(2)}, u32[]{:S(2)}) collective-permute-start(bf16[192,1024]{1,0:T(8,128)(2,1)S(1)} %bitcast.79), channel_id=1, source_target_pairs={{12,0},{13,1},{14,2},{15,3},{0,4},{1,5},{2,6},{3,7},{4,8},{5,9},{6... | collective-permute-start | bytes 1179656 | tf_op jit(solution)/shard_map/ppermute | solution.py:266
  22.4 15.0 %collective-permute-start.3 = (bf16[192,1024]{1,0:T(8,128)(2,1)S(1)}, bf16[192,1024]{1,0:T(8,128)(2,1)S(1)}, u32[]{:S(2)}, u32[]{:S(2)}) collective-permute-start(bf16[192,1024]{1,0:T(8,128)(2,1)S(1)} %bitcast.80), channel_id=1, source_target_pairs={{4,0},{5,1},{6,2},{7,3},{8,4},{9,5},{10,6},{11,7},{12,8},{13,9},{1... | collective-permute-start | bytes 1179656 | tf_op jit(solution)/shard_map/ppermute | solution.py:266
  26.1 17.6 %collective-permute-start.8 = (bf16[192,1024]{1,0:T(8,128)(2,1)S(1)}, bf16[192,1024]{1,0:T(8,128)(2,1)S(1)}, u32[]{:S(2)}, u32[]{:S(2)}) collective-permute-start(bf16[192,1024]{1,0:T(8,128)(2,1)S(1)} %collective-permute-done.1.refs_1_), channel_id=1, source_target_pairs={{12,0},{13,1},{14,2},{15,3},{0,4},{1,5},{2,6},{3,7},{4,8},{5,9},{6... | collective-permute-start | bytes 1179656 | tf_op jit(solution)/shard_map/ppermute | solution.py:266
  29.6 25.7 %collective-permute-start.7 = (bf16[192,1024]{1,0:T(8,128)(2,1)S(1)}, bf16[192,1024]{1,0:T(8,128)(2,1)S(1)}, u32[]{:S(2)}, u32[]{:S(2)}) collective-permute-start(bf16[192,1024]{1,0:T(8,128)(2,1)S(1)} %collective-permute-done.2.refs_2_), channel_id=1, source_target_pairs={{4,0},{5,1},{6,2},{7,3},{8,4},{9,5},{10,6},{11,7},{12,8},{13,9},{1... | collective-permute-start | bytes 1179656 | tf_op jit(solution)/shard_map/ppermute | solution.py:266
  34.2 23.1 %collective-permute-start.6 = (bf16[192,1024]{1,0:T(8,128)(2,1)S(1)}, bf16[192,1024]{1,0:T(8,128)(2,1)}, u32[]{:S(2)}, u32[]{:S(2)}) collective-permute-start(bf16[192,1024]{1,0:T(8,128)(2,1)S(1)} %collective-permute-done.4.refs_4_), channel_id=1, source_target_pairs={{3,0},{0,1},{1,2},{2,3},{7,4},{4,5},{5,6},{6,7},{11,8},{8,9},{9,10... | collective-permute-start | bytes 1179656 | tf_op jit(solution)/shard_map/ppermute | solution.py:266
  37.5 23.7 %collective-permute-start.11 = (bf16[192,1024]{1,0:T(8,128)(2,1)S(1)}, bf16[192,1024]{1,0:T(8,128)(2,1)}, u32[]{:S(2)}, u32[]{:S(2)}) collective-permute-start(bf16[192,1024]{1,0:T(8,128)(2,1)S(1)} %collective-permute-done.3.refs_3_), channel_id=1, source_target_pairs={{4,0},{5,1},{6,2},{7,3},{8,4},{9,5},{10,6},{11,7},{12,8},{13,9},{1... | collective-permute-start | bytes 1179656 | tf_op jit(solution)/shard_map/ppermute | solution.py:266
  41.2 24.6 %collective-permute-start.5 = (bf16[192,1024]{1,0:T(8,128)(2,1)S(1)}, bf16[192,1024]{1,0:T(8,128)(2,1)}, u32[]{:S(2)}, u32[]{:S(2)}) collective-permute-start(bf16[192,1024]{1,0:T(8,128)(2,1)S(1)} %collective-permute-done.3.refs_3_), channel_id=1, source_target_pairs={{1,0},{2,1},{3,2},{0,3},{5,4},{6,5},{7,6},{4,7},{9,8},{10,9},{11,1... | collective-permute-start | bytes 1179656 | tf_op jit(solution)/shard_map/ppermute | solution.py:266
  43.7 25.5 %collective-permute-start.12 = (bf16[192,1024]{1,0:T(8,128)(2,1)S(1)}, bf16[192,1024]{1,0:T(8,128)(2,1)}, u32[]{:S(2)}, u32[]{:S(2)}) collective-permute-start(bf16[192,1024]{1,0:T(8,128)(2,1)S(1)} %collective-permute-done.8.refs_8_), channel_id=1, source_target_pairs={{12,0},{13,1},{14,2},{15,3},{0,4},{1,5},{2,6},{3,7},{4,8},{5,9},{6... | collective-permute-start | bytes 1179656 | tf_op jit(solution)/shard_map/ppermute | solution.py:266
  48.0 25.8 %all-to-all-start = ((bf16[16,192,64]{1,2,0:T(8,128)(2,1)}), bf16[16,192,64]{1,2,0:T(8,128)(2,1)S(1)}, u32[]{:S(2)}, u32[]{:S(2)}) async-start(bf16[16,192,64]{1,2,0:T(8,128)(2,1)} %bitcast.7), calls=%async_computation | async-start | bytes 1048576 | tf_op jit(solution)/shard_map/all_to_all | solution.py:291
  55.3 19.7 %collective-permute-start.9 = (bf16[192,1024]{1,0:T(8,128)(2,1)S(1)}, bf16[192,1024]{1,0:T(8,128)(2,1)}, u32[]{:S(2)}, u32[]{:S(2)}) collective-permute-start(bf16[192,1024]{1,0:T(8,128)(2,1)S(1)} %collective-permute-done.1.refs_1_), channel_id=1, source_target_pairs={{1,0},{2,1},{3,2},{0,3},{5,4},{6,5},{7,6},{4,7},{9,8},{10,9},{11,1... | collective-permute-start | bytes 1179656 | tf_op jit(solution)/shard_map/ppermute | solution.py:266
  57.4 17.7 %collective-permute-start.10 = (bf16[192,1024]{1,0:T(8,128)(2,1)S(1)}, bf16[192,1024]{1,0:T(8,128)(2,1)}, u32[]{:S(2)}, u32[]{:S(2)}) collective-permute-start(bf16[192,1024]{1,0:T(8,128)(2,1)S(1)} %collective-permute-done.7.refs_7_), channel_id=1, source_target_pairs={{3,0},{0,1},{1,2},{2,3},{7,4},{4,5},{5,6},{6,7},{11,8},{8,9},{9,10... | collective-permute-start | bytes 1179656 | tf_op jit(solution)/shard_map/ppermute | solution.py:266
  61.2 13.8 %collective-permute-start.15 = (bf16[192,1024]{1,0:T(8,128)(2,1)S(1)}, bf16[192,1024]{1,0:T(8,128)(2,1)}, u32[]{:S(2)}, u32[]{:S(2)}) collective-permute-start(bf16[192,1024]{1,0:T(8,128)(2,1)S(1)} %collective-permute-done.7.refs_7_), channel_id=1, source_target_pairs={{4,0},{5,1},{6,2},{7,3},{8,4},{9,5},{10,6},{11,7},{12,8},{13,9},{1... | collective-permute-start | bytes 1179656 | tf_op jit(solution)/shard_map/ppermute | solution.py:266
  65.8 10.9 %collective-permute-start.14 = (bf16[192,1024]{1,0:T(8,128)(2,1)}, bf16[192,1024]{1,0:T(8,128)(2,1)}, u32[]{:S(2)}, u32[]{:S(2)}) collective-permute-start(bf16[192,1024]{1,0:T(8,128)(2,1)} %collective-permute-done.6.refs_6_), channel_id=1, source_target_pairs={{3,0},{0,1},{1,2},{2,3},{7,4},{4,5},{5,6},{6,7},{11,8},{8,9},{9,10... | collective-permute-start | bytes 1179656 | tf_op jit(solution)/shard_map/ppermute | solution.py:266
  69.2 10.4 %collective-permute-start.13 = (bf16[192,1024]{1,0:T(8,128)(2,1)}, bf16[192,1024]{1,0:T(8,128)(2,1)}, u32[]{:S(2)}, u32[]{:S(2)}) collective-permute-start(bf16[192,1024]{1,0:T(8,128)(2,1)} %collective-permute-done.12.refs_12_), channel_id=1, source_target_pairs={{1,0},{2,1},{3,2},{0,3},{5,4},{6,5},{7,6},{4,7},{9,8},{10,9},{11,1... | collective-permute-start | bytes 1179656 | tf_op jit(solution)/shard_map/ppermute | solution.py:266
  133.9 3.3 %collective-permute-start.16 = (bf16[16,48,128]{2,1,0:T(8,128)(2,1)S(1)}, bf16[16,48,128]{2,1,0:T(8,128)(2,1)S(1)}, u32[]{:S(2)}, u32[]{:S(2)}) collective-permute-start(bf16[16,48,128]{2,1,0:T(8,128)(2,1)S(1)} %dynamic-slice_bitcast_fusion), channel_id=1, source_target_pairs={{0,16},{16,0},{32,48},{48,32},{64,80},{80,64},{96,112},{112,96},{1... | collective-permute-start | bytes 589832 | tf_op jit(solution)/shard_map/ppermute | solution.py:249
  137.4 6.7 %collective-permute-start.17 = (bf16[8,48,128]{2,1,0:T(8,128)(2,1)S(1)}, bf16[8,48,128]{2,1,0:T(8,128)(2,1)S(1)}, u32[]{:S(2)}, u32[]{:S(2)}) collective-permute-start(bf16[8,48,128]{2,1,0:T(8,128)(2,1)S(1)} %dynamic-slice_bitcast_fusion.1), channel_id=1, source_target_pairs={{0,32},{16,48},{32,0},{48,16},{64,96},{80,112},{96,64},{112,80},{1... | collective-permute-start | bytes 294920 | tf_op jit(solution)/shard_map/ppermute | solution.py:249
  144.1 11.6 %collective-permute-start.18 = (bf16[4,48,128]{2,1,0:T(8,128)(2,1)S(1)}, bf16[4,48,128]{2,1,0:T(8,128)(2,1)S(1)}, u32[]{:S(2)}, u32[]{:S(2)}) collective-permute-start(bf16[4,48,128]{2,1,0:T(8,128)(2,1)S(1)} %dynamic-slice_bitcast_fusion.2), channel_id=1, source_target_pairs={{0,64},{16,80},{32,96},{48,112},{64,0},{80,16},{96,32},{112,48},{1... | collective-permute-start | bytes 147464 | tf_op jit(solution)/shard_map/ppermute | solution.py:249
  148.5 32.6 %all-to-all-start.1 = ((bf16[16,192,256]{2,1,0:T(8,128)(2,1)}), bf16[16,192,256]{2,1,0:T(8,128)(2,1)S(1)}, u32[]{:S(2)}, u32[]{:S(2)}) async-start(bf16[16,192,256]{2,1,0:T(8,128)(2,1)} %bitcast.14), calls=%async_computation.1 | async-start | bytes 3145728 | tf_op jit(solution)/shard_map/all_to_all | solution.py:297
  155.8 10.0 %collective-permute-start.19 = (bf16[2,48,128]{2,1,0:T(8,128)(2,1)S(1)}, bf16[2,48,128]{2,1,0:T(8,128)(2,1)S(1)}, u32[]{:S(2)}, u32[]{:S(2)}) collective-permute-start(bf16[2,48,128]{2,1,0:T(8,128)(2,1)S(1)} %dynamic-slice_bitcast_fusion.3), channel_id=1, source_target_pairs={{0,128},{16,144},{32,160},{48,176},{64,192},{80,208},{96,224},{112... | collective-permute-start | bytes 73736 | tf_op jit(solution)/shard_map/ppermute | solution.py:249
  165.8 14.6 %collective-permute-start.20 = (bf16[1,48,128]{2,1,0:T(8,128)(2,1)S(1)}, bf16[1,48,128]{2,1,0:T(8,128)(2,1)S(1)}, u32[]{:S(2)}, u32[]{:S(2)}) collective-permute-start(bf16[1,48,128]{2,1,0:T(8,128)(2,1)S(1)} %constant_dynamic-slice_fusion), channel_id=1, source_target_pairs={{0,256},{16,272},{32,288},{48,304},{64,320},{80,336},{96,352},{112... | collective-permute-start | bytes 36872 | tf_op jit(solution)/shard_map/ppermute | solution.py:249
  (11 other events, 384.3 us)
Sparse Core Ops, SparseCore 0:
  13.2 89.4 all-gather.1

commit v5 on v3

--- a/solution.py
+++ b/solution.py
@@ -18,9 +18,6 @@
     ((0, 1), (0, 1)), ((1, -1), (0, -1)), ((1, 0), (1, 0)), ((-1, 1), (-1, 0)),
     ((2, 1), (0, 1)), ((-1, -1), (0, -1)), ((1, -1), (1, 0)),
 )
-
-
-SECOND = 4
 
 
 def dot(a, b, ca=1, cb=0):
@@ -46,14 +43,13 @@
     for load in loads:
         load.start()
 
-    parts, tall, lanes = w_ref.shape
+    chips, tall, lanes = w_ref.shape
     deep = tall * 2 // 3
-    width = parts * deep
-    wide_ref[:, :lanes] = w_ref[:, :deep, :].reshape(width, lanes)
+    wide_ref[:, :lanes] = w_ref[:, :deep, :].reshape(chips * deep, lanes)
     packed = w_ref[:, deep:, :].astype(F32)
     left = lax.broadcasted_iota(jnp.int32, packed.shape, 2) < HD
     query = [jnp.where(left, packed, 0.0), jnp.where(left, pltpu.roll(packed, HD, 2), 0.0)]
-    wide_ref[:, lanes:] = jnp.concatenate(query, axis=1).reshape(width, lanes).astype(BF)
+    wide_ref[:, lanes:] = jnp.concatenate(query, axis=1).reshape(chips * deep, lanes).astype(BF)
     place = (
         lax.broadcasted_iota(jnp.int32, (HD, 4 * HD), 0) + 3 * HD
         == lax.broadcasted_iota(jnp.int32, (HD, 4 * HD), 1)
@@ -87,10 +83,10 @@
     lax.fori_loop(0, tiles, to_clusters, 0)
 
     acc_ref[...] = jnp.zeros_like(acc_ref)
-    key_at = lax.broadcasted_iota(jnp.int32, (rows, keys), 1)
+    place_of = lax.broadcasted_iota(jnp.int32, (rows, keys), 1)
 
     def weigh(both, c):
-        score = jnp.where(key_at < counts_ref[c] * rows, both[:rows], -1e30)
+        score = jnp.where(place_of < counts_ref[c] * rows, both[:rows], -1e30)
         dpw = both[rows:]
         raw = jnp.exp(score - jnp.max(score, axis=1, keepdims=True))
         p = raw * (1.0 / jnp.sum(raw, axis=1, keepdims=True))
@@ -139,16 +135,19 @@
         return carry
 
     lax.fori_loop(0, 2, to_nodes, 0)
+    parts, tall, lanes = gw_ref.shape
+    deep = tall * 2 // 3
     gw_ref[:, :deep, :] = sum_ref[:, :lanes].reshape(parts, deep, lanes).astype(BF)
     query = sum_ref[:, lanes:].reshape(parts, deep, lanes)
     low, high = query[:, : deep // 2], query[:, deep // 2 :]
+    left = lax.broadcasted_iota(jnp.int32, low.shape, 2) < HD
     gw_ref[:, deep:, :] = jnp.where(left, low, pltpu.roll(high, HD, 2)).astype(BF)
 
 
-def attend(blocks_of, owner, w_head, cot, order, blocks, counts):
+def attend(blocks_of, owner, w_head, cot, order, blocks, counts, parts):
     local, width = blocks_of[0].shape
     nodes = len(blocks_of) * local
-    parts, tall, lanes = w_head.shape
+    tall, lanes = width // parts * 3 // 2, 2 * HD
     ids = (owner[:, None] * local + jnp.arange(local, dtype=jnp.int32)).reshape(1, nodes)
     vmem = pl.BlockSpec(memory_space=pltpu.VMEM)
     smem = pl.BlockSpec(memory_space=pltpu.SMEM)
@@ -213,7 +212,7 @@
     )(got, weights)
 
 
-def reduce_scatter(part, axis):
+def reduce_scatter(part, axis, got, weights):
     size = lax.axis_size(axis)
     me = lax.axis_index(axis)
     bit = 1
@@ -222,11 +221,15 @@
         mine = lax.rem(me // bit, 2)
         keep = lax.dynamic_index_in_dim(pairs, mine, 1, keepdims=False)
         send = lax.dynamic_index_in_dim(pairs, 1 - mine, 1, keepdims=False)
+        if 2 * bit == size:
+            send, got = lax.optimization_barrier((send, got))
         came = lax.ppermute(send, axis, [(i, i ^ bit) for i in range(size)])
+        if 2 * bit == size:
+            came, *done = lax.optimization_barrier((came, *finish(got, weights)))
         total = keep.astype(F32) + came.astype(F32)
         part = total.astype(BF)
         bit *= 2
-    return total[0]
+    return total[0], done
 
 
 def gather_round(block, axis):
@@ -251,28 +254,37 @@
     deep = qkv_weight.shape[0]
     feats = features[0]
     head = lax.axis_index("seq")
-    own = lax.dynamic_slice(qkv_weight, (0, head * 3 * HD), (deep, 3 * HD))
-    query = own[:, :HD] * jnp.asarray(0.125, BF)
-    query = jnp.concatenate([query[: deep // 2], query[deep // 2 :]], axis=1)
-    own = jnp.concatenate([own[:, HD:], query], axis=0)
-    copies = jnp.broadcast_to(own[None], (lax.axis_size("dp"), *own.shape))
-    blocks_of, owner = gather_round(feats, "seq")
-    cot = lax.all_to_all(
-        cotangent[0].reshape(local_rows, HEADS, HD).transpose(1, 0, 2), "seq", 0, 0, tiled=True
-    ).reshape(HEADS * local_rows, HD)
-    copies, _ = lax.optimization_barrier((copies, blocks_of[SECOND]))
-    w_head = lax.all_to_all(copies, "dp", 0, 0, tiled=True)
     by_head = qkv_weight.reshape(deep, HEADS, 3 * HD)
     ordered = jnp.concatenate(
         [by_head[:, :, HD:].reshape(deep, -1), by_head[:, :, :HD].reshape(deep, -1)], axis=1
     )
-    weights = lax.all_gather(ordered, "dp", axis=0, tiled=True)
-    grads, part = attend(blocks_of, owner, w_head, cot, node_order[0], blocks[0], counts[0])
+    size = lax.axis_size("dp")
+    core = lax.rem(lax.axis_index("dp"), 2)
+    other = lax.ppermute(ordered, "dp", [(i, i ^ 1) for i in range(size)])
+    chip = jnp.where(
+        core == 0, jnp.stack([ordered, other]), jnp.stack([other, ordered])
+    ).reshape(2 * deep, -1)
+    groups = [list(range(c, size, 2)) for c in range(2)]
+    weights = lax.all_gather(chip, "dp", axis=0, tiled=True, axis_index_groups=groups)
+    own = lax.dynamic_slice(chip, (0, head * 2 * HD), (2 * deep, 2 * HD))
+    query = lax.dynamic_slice(chip, (0, (2 * HEADS + head) * HD), (2 * deep, HD))
+    query = query * jnp.asarray(0.125, BF)
+    own = jnp.concatenate(
+        [own, jnp.concatenate([query[:deep], query[deep:]], axis=1)], axis=0
+    )
+    copies = jnp.broadcast_to(own[None], (size // 2, *own.shape))
+    w_head = lax.all_to_all(copies, "dp", 0, 0, tiled=True, axis_index_groups=groups)
+    blocks_of, owner = gather_round(feats, "seq")
+    by_owner = cotangent[0].reshape(local_rows, HEADS, HD).transpose(1, 0, 2)
+    by_owner, w_head = lax.optimization_barrier((by_owner, w_head))
+    cot = lax.all_to_all(by_owner, "seq", 0, 0, tiled=True).reshape(HEADS * local_rows, HD)
+    grads, part = attend(
+        blocks_of, owner, w_head, cot, node_order[0], blocks[0], counts[0], size
+    )
     got = lax.all_to_all(grads.reshape(HEADS, local_rows, 4 * HD), "seq", 0, 0, tiled=True)
-    total = reduce_scatter(part, "dp")
+    total, (attended, grad_feats) = reduce_scatter(part, "dp", got, weights)
     query = jnp.concatenate([total[deep:, :HD], total[deep:, HD:]], axis=0)
     grad_weight = jnp.concatenate([query, total[:deep]], axis=1)
-    attended, grad_feats = finish(got, weights)
     return (
         attended.reshape(1, local_rows, model_width),
         grad_feats.reshape(1, local_rows, model_width),

time: 197 us -> 190 us (0.964)
  the two profiles are of different devices: /device:TPU:2 before, /device:TPU:1 now
where the time goes in v5:
time: 190 us; the launch traced here: 189 us
  starting transfers between devices  108 us (57%)
  Pallas kernels  34.7 us (18%)
  waiting for transfers between devices  18.5 us (10%)
  between operations  14.7 us (8%)
  local copies, waits for them, and re-layouts  10.1 us (5%)
  other arithmetic  2.59 us (1%)
    ppermute x15, starting transfers between devices, gather_round(): held[(hy + dy) % SIDE, (hx + dx) % SIDE] = lax.ppermute(source, axis, pairs)  49.1 us
    ppermute x5, starting transfers between devices, reduce_scatter(): came = lax.ppermute(send, axis, [(i, i ^ bit) for i in range(size)])  31.9 us
    pallas_call x1, Pallas kernels, attend(): pl.pallas_call(attend_kernel, name='attend', out_shape=[jax.ShapeDtypeStr...  31.7 us
    all_to_all x1, starting transfers between devices, per_device(): lax.all_to_all(copies, 'dp', 0, 0, tiled=True, axis_index_groups=groups)  9.54 us
    ppermute x1, starting transfers between devices, per_device(): other = lax.ppermute(ordered, 'dp', [(i, i ^ 1) for i in range(size)])  8.92 us
    ppermute x15, waiting for transfers between devices, gather_round(): held[(hy + dy) % SIDE, (hx + dx) % SIDE] = lax.ppermute(source, axis, pairs)  6.67 us
    ppermute x5, waiting for transfers between devices, reduce_scatter(): came = lax.ppermute(send, axis, [(i, i ^ bit) for i in range(size)])  6.35 us
    all_to_all x1, starting transfers between devices, per_device(): lax.all_to_all(grads.reshape(HEADS, local_rows, 4 * HD), 'seq', 0, 0, til...  4.91 us
  transfers between devices with their start and end apart: 25, of which 7 were waited for; matrix products, arithmetic and copies ran while one was open for 4% of the time, Pallas kernels for 18%

profile of v5, /device:TPU:1, one launch (start us, length us, event | category | flops | bytes accessed | tf_op | source)
XLA Modules:
  0.0 188.7 jit_solution(12721000152240408333)
XLA Ops:
  8.8 8.9 %collective-permute-start = (bf16[32,3072]{1,0:T(8,128)(2,1)S(1)}, bf16[32,3072]{1,0:T(8,128)(2,1)S(1)}, u32[]{:S(2)}, u32[]{:S(2)}) collective-permute-start(bf16[32,3072]{1,0:T(8,128)(2,1)S(1)} %constant_dynamic-update-slice_fusion), channel_id=1, source_target_pairs={{0,16},{16,0},{32,48},{48,32},{64,80},{80,64},{96,112},{112,96},{1... | collective-permute-start | bytes 589832 | tf_op jit(solution)/shard_map/ppermute | solution.py:263
  22.0 9.5 %all-to-all-start = ((bf16[16,96,128]{2,1,0:T(8,128)(2,1)}), bf16[16,96,128]{2,1,0:T(8,128)(2,1)S(1)}, u32[]{:S(2)}, u32[]{:S(2)}) async-start(bf16[16,96,128]{2,1,0:T(8,128)(2,1)} %broadcast_in_dim.2), calls=%async_computation | async-start | bytes 786432 | tf_op jit(solution)/shard_map/all_to_all | solution.py:276
  31.6 4.4 %collective-permute-start.1 = (bf16[192,1024]{1,0:T(8,128)(2,1)S(1)}, bf16[192,1024]{1,0:T(8,128)(2,1)S(1)}, u32[]{:S(2)}, u32[]{:S(2)}) collective-permute-start(bf16[192,1024]{1,0:T(8,128)(2,1)S(1)} %bitcast.74), channel_id=1, source_target_pairs={{1,0},{2,1},{3,2},{0,3},{5,4},{6,5},{7,6},{4,7},{9,8},{10,9},{11,1... | collective-permute-start | bytes 1179656 | tf_op jit(solution)/shard_map/ppermute | solution.py:245
  37.9 3.2 %collective-permute-start.4 = (bf16[192,1024]{1,0:T(8,128)(2,1)S(1)}, bf16[192,1024]{1,0:T(8,128)(2,1)S(1)}, u32[]{:S(2)}, u32[]{:S(2)}) collective-permute-start(bf16[192,1024]{1,0:T(8,128)(2,1)S(1)} %bitcast.76), channel_id=1, source_target_pairs={{12,0},{13,1},{14,2},{15,3},{0,4},{1,5},{2,6},{3,7},{4,8},{5,9},{6... | collective-permute-start | bytes 1179656 | tf_op jit(solution)/shard_map/ppermute | solution.py:245
  41.1 3.4 %collective-permute-start.3 = (bf16[192,1024]{1,0:T(8,128)(2,1)S(1)}, bf16[192,1024]{1,0:T(8,128)(2,1)S(1)}, u32[]{:S(2)}, u32[]{:S(2)}) collective-permute-start(bf16[192,1024]{1,0:T(8,128)(2,1)S(1)} %bitcast.77), channel_id=1, source_target_pairs={{4,0},{5,1},{6,2},{7,3},{8,4},{9,5},{10,6},{11,7},{12,8},{13,9},{1... | collective-permute-start | bytes 1179656 | tf_op jit(solution)/shard_map/ppermute | solution.py:245
  48.9 4.6 %collective-permute-start.7 = (bf16[192,1024]{1,0:T(8,128)(2,1)S(1)}, bf16[192,1024]{1,0:T(8,128)(2,1)}, u32[]{:S(2)}, u32[]{:S(2)}) collective-permute-start(bf16[192,1024]{1,0:T(8,128)(2,1)S(1)} %collective-permute-done.2.refs_2_), channel_id=1, source_target_pairs={{4,0},{5,1},{6,2},{7,3},{8,4},{9,5},{10,6},{11,7},{12,8},{13,9},{1... | collective-permute-start | bytes 1179656 | tf_op jit(solution)/shard_map/ppermute | solution.py:245
  57.9 4.6 %collective-permute-start.5 = (bf16[192,1024]{1,0:T(8,128)(2,1)S(1)}, bf16[192,1024]{1,0:T(8,128)(2,1)}, u32[]{:S(2)}, u32[]{:S(2)}) collective-permute-start(bf16[192,1024]{1,0:T(8,128)(2,1)S(1)} %collective-permute-done.3.refs_3_), channel_id=1, source_target_pairs={{1,0},{2,1},{3,2},{0,3},{5,4},{6,5},{7,6},{4,7},{9,8},{10,9},{11,1... | collective-permute-start | bytes 1179656 | tf_op jit(solution)/shard_map/ppermute | solution.py:245
  62.5 2.9 %collective-permute-start.12 = (bf16[192,1024]{1,0:T(8,128)(2,1)S(1)}, bf16[192,1024]{1,0:T(8,128)(2,1)}, u32[]{:S(2)}, u32[]{:S(2)}) collective-permute-start(bf16[192,1024]{1,0:T(8,128)(2,1)S(1)} %collective-permute-done.8.refs_8_), channel_id=1, source_target_pairs={{12,0},{13,1},{14,2},{15,3},{0,4},{1,5},{2,6},{3,7},{4,8},{5,9},{6... | collective-permute-start | bytes 1179656 | tf_op jit(solution)/shard_map/ppermute | solution.py:245
  66.5 3.6 %all-to-all-start.1 = ((bf16[16,192,64]{1,2,0:T(8,128)(2,1)}), bf16[16,192,64]{1,2,0:T(8,128)(2,1)S(1)}, u32[]{:S(2)}, u32[]{:S(2)}) async-start(bf16[16,192,64]{1,2,0:T(8,128)(2,1)} %bitcast.6), calls=%async_computation.1 | async-start | bytes 1048576 | tf_op jit(solution)/shard_map/all_to_all | solution.py:280
  70.1 4.4 %collective-permute-start.9 = (bf16[192,1024]{1,0:T(8,128)(2,1)S(1)}, bf16[192,1024]{1,0:T(8,128)(2,1)}, u32[]{:S(2)}, u32[]{:S(2)}) collective-permute-start(bf16[192,1024]{1,0:T(8,128)(2,1)S(1)} %collective-permute-done.1.refs_1_), channel_id=1, source_target_pairs={{1,0},{2,1},{3,2},{0,3},{5,4},{6,5},{7,6},{4,7},{9,8},{10,9},{11,1... | collective-permute-start | bytes 1179656 | tf_op jit(solution)/shard_map/ppermute | solution.py:245
  76.4 4.4 %collective-permute-start.15 = (bf16[192,1024]{1,0:T(8,128)(2,1)}, bf16[192,1024]{1,0:T(8,128)(2,1)}, u32[]{:S(2)}, u32[]{:S(2)}) collective-permute-start(bf16[192,1024]{1,0:T(8,128)(2,1)} %collective-permute-done.7.refs_7_), channel_id=1, source_target_pairs={{4,0},{5,1},{6,2},{7,3},{8,4},{9,5},{10,6},{11,7},{12,8},{13,9},{1... | collective-permute-start | bytes 1179656 | tf_op jit(solution)/shard_map/ppermute | solution.py:245
  83.0 4.5 %collective-permute-start.13 = (bf16[192,1024]{1,0:T(8,128)(2,1)}, bf16[192,1024]{1,0:T(8,128)(2,1)}, u32[]{:S(2)}, u32[]{:S(2)}) collective-permute-start(bf16[192,1024]{1,0:T(8,128)(2,1)} %collective-permute-done.12.refs_12_), channel_id=1, source_target_pairs={{1,0},{2,1},{3,2},{0,3},{5,4},{6,5},{7,6},{4,7},{9,8},{10,9},{11,1... | collective-permute-start | bytes 1179656 | tf_op jit(solution)/shard_map/ppermute | solution.py:245
  90.7 4.7 %collective-permute-done.14.refs_14_ = bf16[192,1024]{1,0:T(8,128)(2,1)} collective-permute-done((bf16[192,1024]{1,0:T(8,128)(2,1)}, bf16[192,1024]{1,0:T(8,128)(2,1)}, u32[]{:S(2)}, u32[]{:S(2)}) %collective-permute-start.14) | collective-permute-done | bytes 393248 | tf_op jit(solution)/shard_map/ppermute | solution.py:245
  95.4 31.7 %attend.1 = (bf16[3072,256]{1,0:T(8,128)(2,1)}, bf16[32,48,128]{2,1,0:T(8,128)(2,1)S(1)}) custom-call(s32[48,8]{1,0:T(8,128)S(1)} %bitcast.81, s32[48]{0:T(128)S(1)} %bitcast.83, s32[16]{0:T(128)S(1)} %fusion.6.owner_ref, s32[1,3072]{1,0:T(1,128)S(1)} %add.129.ids_ref, bf16[16,96,128]{2,1,0:T(8,128)(2,1)S(1)} %all-to-all-done.w_ref, ...), custom_call_target="tpu_custom_call" | custom-call | tf_op jit(solution)/shard_map/attend/pallas_call | solution.py:154
  127.2 5.0 %collective-permute-start.16 = (bf16[16,48,128]{2,1,0:T(8,128)(2,1)S(1)}, bf16[16,48,128]{2,1,0:T(8,128)(2,1)S(1)}, u32[]{:S(2)}, u32[]{:S(2)}) collective-permute-start(bf16[16,48,128]{2,1,0:T(8,128)(2,1)S(1)} %dynamic-slice_bitcast_fusion), channel_id=1, source_target_pairs={{0,16},{16,0},{32,48},{48,32},{64,80},{80,64},{96,112},{112,96},{1... | collective-permute-start | bytes 589832 | tf_op jit(solution)/shard_map/ppermute | solution.py:226
  132.3 4.9 %all-to-all-start.2 = ((bf16[16,192,256]{2,1,0:T(8,128)(2,1)}), bf16[16,192,256]{2,1,0:T(8,128)(2,1)S(1)}, u32[]{:S(2)}, u32[]{:S(2)}) async-start(bf16[16,192,256]{2,1,0:T(8,128)(2,1)} %bitcast.88), calls=%async_computation.2 | async-start | bytes 3145728 | tf_op jit(solution)/shard_map/all_to_all | solution.py:284
  137.3 3.6 %collective-permute-start.17 = (bf16[8,48,128]{2,1,0:T(8,128)(2,1)S(1)}, bf16[8,48,128]{2,1,0:T(8,128)(2,1)S(1)}, u32[]{:S(2)}, u32[]{:S(2)}) collective-permute-start(bf16[8,48,128]{2,1,0:T(8,128)(2,1)S(1)} %dynamic-slice_bitcast_fusion.1), channel_id=1, source_target_pairs={{0,32},{16,48},{32,0},{48,16},{64,96},{80,112},{96,64},{112,80},{1... | collective-permute-start | bytes 294920 | tf_op jit(solution)/shard_map/ppermute | solution.py:226
  140.9 2.9 %collective-permute-done.17 = bf16[8,48,128]{2,1,0:T(8,128)(2,1)S(1)} collective-permute-done((bf16[8,48,128]{2,1,0:T(8,128)(2,1)S(1)}, bf16[8,48,128]{2,1,0:T(8,128)(2,1)S(1)}, u32[]{:S(2)}, u32[]{:S(2)}) %collective-permute-start.17) | collective-permute-done | bytes 98336 | tf_op jit(solution)/shard_map/ppermute | solution.py:226
  143.9 4.0 %collective-permute-start.18 = (bf16[4,48,128]{2,1,0:T(8,128)(2,1)S(1)}, bf16[4,48,128]{2,1,0:T(8,128)(2,1)S(1)}, u32[]{:S(2)}, u32[]{:S(2)}) collective-permute-start(bf16[4,48,128]{2,1,0:T(8,128)(2,1)S(1)} %dynamic-slice_bitcast_fusion.2), channel_id=1, source_target_pairs={{0,64},{16,80},{32,96},{48,112},{64,0},{80,16},{96,32},{112,48},{1... | collective-permute-start | bytes 147464 | tf_op jit(solution)/shard_map/ppermute | solution.py:226
  149.9 7.0 %collective-permute-start.19 = (bf16[2,48,128]{2,1,0:T(8,128)(2,1)S(1)}, bf16[2,48,128]{2,1,0:T(8,128)(2,1)S(1)}, u32[]{:S(2)}, u32[]{:S(2)}) collective-permute-start(bf16[2,48,128]{2,1,0:T(8,128)(2,1)S(1)} %dynamic-slice_bitcast_fusion.3), channel_id=1, source_target_pairs={{0,128},{16,144},{32,160},{48,176},{64,192},{80,208},{96,224},{112... | collective-permute-start | bytes 73736 | tf_op jit(solution)/shard_map/ppermute | solution.py:226
  158.4 4.4 %all-to-all-done.2.g_ref = bf16[16,192,256]{2,1,0:T(8,128)(2,1)S(1)} async-done(((bf16[16,192,256]{2,1,0:T(8,128)(2,1)}), bf16[16,192,256]{2,1,0:T(8,128)(2,1)S(1)}, u32[]{:S(2)}, u32[]{:S(2)}) %all-to-all-start.2) | async-done | bytes 1572896 | tf_op jit(solution)/shard_map/all_to_all | solution.py:284
  162.9 12.3 %collective-permute-start.20 = (bf16[1,48,128]{2,1,0:T(8,128)(2,1)S(1)}, bf16[1,48,128]{2,1,0:T(8,128)(2,1)S(1)}, u32[]{:S(2)}, u32[]{:S(2)}) collective-permute-start(bf16[1,48,128]{2,1,0:T(8,128)(2,1)S(1)} %constant_dynamic-slice_fusion), channel_id=1, source_target_pairs={{0,256},{16,272},{32,288},{48,304},{64,320},{80,336},{96,352},{112... | collective-permute-start | bytes 36872 | tf_op jit(solution)/shard_map/ppermute | solution.py:226
  175.3 2.8 %copy-done = bf16[1024,3072]{1,0:T(8,128)(2,1)S(1)} copy-done((bf16[1024,3072]{1,0:T(8,128)(2,1)S(1)}, bf16[1024,3072]{1,0:T(8,128)(2,1)}, u32[]{:S(2)}) %copy-start) | copy-done | bytes 6291480
  178.0 3.1 %finish.1 = (bf16[192,1024]{1,0:T(8,128)(2,1)}, bf16[192,1024]{1,0:T(8,128)(2,1)}) custom-call(bf16[16,192,256]{2,1,0:T(8,128)(2,1)S(1)} %all-to-all-done.2.g_ref, bf16[1024,3072]{1,0:T(8,128)(2,1)S(1)} %copy-done), custom_call_target="tpu_custom_call" | custom-call | tf_op jit(solution)/shard_map/finish/pallas_call | solution.py:201
  (84 shorter events, 29.2 us)
Async XLA Ops:
  7.2 168.1 %all-gather.2.cloned.1.call-start = ((), (), s32[]{:S(2)}) async-start(), calls=%async_computation.3 | async-start | bytes 6684672 | tf_op jit(solution)/shard_map/all_gather | solution.py:268
  8.8 10.0 %collective-permute-start = (bf16[32,3072]{1,0:T(8,128)(2,1)S(1)}, bf16[32,3072]{1,0:T(8,128)(2,1)S(1)}, u32[]{:S(2)}, u32[]{:S(2)}) collective-permute-start(bf16[32,3072]{1,0:T(8,128)(2,1)S(1)} %constant_dynamic-update-slice_fusion), channel_id=1, source_target_pairs={{0,16},{16,0},{32,48},{48,32},{64,80},{80,64},{96,112},{112,96},{1... | collective-permute-start | bytes 589832 | tf_op jit(solution)/shard_map/ppermute | solution.py:263
  22.0 44.4 %all-to-all-start = ((bf16[16,96,128]{2,1,0:T(8,128)(2,1)}), bf16[16,96,128]{2,1,0:T(8,128)(2,1)S(1)}, u32[]{:S(2)}, u32[]{:S(2)}) async-start(bf16[16,96,128]{2,1,0:T(8,128)(2,1)} %broadcast_in_dim.2), calls=%async_computation | async-start | bytes 786432 | tf_op jit(solution)/shard_map/all_to_all | solution.py:276
  31.6 12.9 %collective-permute-start.1 = (bf16[192,1024]{1,0:T(8,128)(2,1)S(1)}, bf16[192,1024]{1,0:T(8,128)(2,1)S(1)}, u32[]{:S(2)}, u32[]{:S(2)}) collective-permute-start(bf16[192,1024]{1,0:T(8,128)(2,1)S(1)} %bitcast.74), channel_id=1, source_target_pairs={{1,0},{2,1},{3,2},{0,3},{5,4},{6,5},{7,6},{4,7},{9,8},{10,9},{11,1... | collective-permute-start | bytes 1179656 | tf_op jit(solution)/shard_map/ppermute | solution.py:245
  36.0 12.9 %collective-permute-start.2 = (bf16[192,1024]{1,0:T(8,128)(2,1)S(1)}, bf16[192,1024]{1,0:T(8,128)(2,1)S(1)}, u32[]{:S(2)}, u32[]{:S(2)}) collective-permute-start(bf16[192,1024]{1,0:T(8,128)(2,1)S(1)} %bitcast.75), channel_id=1, source_target_pairs={{3,0},{0,1},{1,2},{2,3},{7,4},{4,5},{5,6},{6,7},{11,8},{8,9},{9,10... | collective-permute-start | bytes 1179656 | tf_op jit(solution)/shard_map/ppermute | solution.py:245
  37.9 15.6 %collective-permute-start.4 = (bf16[192,1024]{1,0:T(8,128)(2,1)S(1)}, bf16[192,1024]{1,0:T(8,128)(2,1)S(1)}, u32[]{:S(2)}, u32[]{:S(2)}) collective-permute-start(bf16[192,1024]{1,0:T(8,128)(2,1)S(1)} %bitcast.76), channel_id=1, source_target_pairs={{12,0},{13,1},{14,2},{15,3},{0,4},{1,5},{2,6},{3,7},{4,8},{5,9},{6... | collective-permute-start | bytes 1179656 | tf_op jit(solution)/shard_map/ppermute | solution.py:245
  41.1 14.4 %collective-permute-start.3 = (bf16[192,1024]{1,0:T(8,128)(2,1)S(1)}, bf16[192,1024]{1,0:T(8,128)(2,1)S(1)}, u32[]{:S(2)}, u32[]{:S(2)}) collective-permute-start(bf16[192,1024]{1,0:T(8,128)(2,1)S(1)} %bitcast.77), channel_id=1, source_target_pairs={{4,0},{5,1},{6,2},{7,3},{8,4},{9,5},{10,6},{11,7},{12,8},{13,9},{1... | collective-permute-start | bytes 1179656 | tf_op jit(solution)/shard_map/ppermute | solution.py:245
  44.5 18.0 %collective-permute-start.8 = (bf16[192,1024]{1,0:T(8,128)(2,1)S(1)}, bf16[192,1024]{1,0:T(8,128)(2,1)S(1)}, u32[]{:S(2)}, u32[]{:S(2)}) collective-permute-start(bf16[192,1024]{1,0:T(8,128)(2,1)S(1)} %collective-permute-done.1.refs_1_), channel_id=1, source_target_pairs={{12,0},{13,1},{14,2},{15,3},{0,4},{1,5},{2,6},{3,7},{4,8},{5,9},{6... | collective-permute-start | bytes 1179656 | tf_op jit(solution)/shard_map/ppermute | solution.py:245
  48.9 21.2 %collective-permute-start.7 = (bf16[192,1024]{1,0:T(8,128)(2,1)S(1)}, bf16[192,1024]{1,0:T(8,128)(2,1)}, u32[]{:S(2)}, u32[]{:S(2)}) collective-permute-start(bf16[192,1024]{1,0:T(8,128)(2,1)S(1)} %collective-permute-done.2.refs_2_), channel_id=1, source_target_pairs={{4,0},{5,1},{6,2},{7,3},{8,4},{9,5},{10,6},{11,7},{12,8},{13,9},{1... | collective-permute-start | bytes 1179656 | tf_op jit(solution)/shard_map/ppermute | solution.py:245
  53.5 20.9 %collective-permute-start.6 = (bf16[192,1024]{1,0:T(8,128)(2,1)S(1)}, bf16[192,1024]{1,0:T(8,128)(2,1)}, u32[]{:S(2)}, u32[]{:S(2)}) collective-permute-start(bf16[192,1024]{1,0:T(8,128)(2,1)S(1)} %collective-permute-done.4.refs_4_), channel_id=1, source_target_pairs={{3,0},{0,1},{1,2},{2,3},{7,4},{4,5},{5,6},{6,7},{11,8},{8,9},{9,10... | collective-permute-start | bytes 1179656 | tf_op jit(solution)/shard_map/ppermute | solution.py:245
  55.5 20.9 %collective-permute-start.11 = (bf16[192,1024]{1,0:T(8,128)(2,1)S(1)}, bf16[192,1024]{1,0:T(8,128)(2,1)}, u32[]{:S(2)}, u32[]{:S(2)}) collective-permute-start(bf16[192,1024]{1,0:T(8,128)(2,1)S(1)} %collective-permute-done.3.refs_3_), channel_id=1, source_target_pairs={{4,0},{5,1},{6,2},{7,3},{8,4},{9,5},{10,6},{11,7},{12,8},{13,9},{1... | collective-permute-start | bytes 1179656 | tf_op jit(solution)/shard_map/ppermute | solution.py:245
  57.9 22.9 %collective-permute-start.5 = (bf16[192,1024]{1,0:T(8,128)(2,1)S(1)}, bf16[192,1024]{1,0:T(8,128)(2,1)}, u32[]{:S(2)}, u32[]{:S(2)}) collective-permute-start(bf16[192,1024]{1,0:T(8,128)(2,1)S(1)} %collective-permute-done.3.refs_3_), channel_id=1, source_target_pairs={{1,0},{2,1},{3,2},{0,3},{5,4},{6,5},{7,6},{4,7},{9,8},{10,9},{11,1... | collective-permute-start | bytes 1179656 | tf_op jit(solution)/shard_map/ppermute | solution.py:245
  62.5 20.5 %collective-permute-start.12 = (bf16[192,1024]{1,0:T(8,128)(2,1)S(1)}, bf16[192,1024]{1,0:T(8,128)(2,1)}, u32[]{:S(2)}, u32[]{:S(2)}) collective-permute-start(bf16[192,1024]{1,0:T(8,128)(2,1)S(1)} %collective-permute-done.8.refs_8_), channel_id=1, source_target_pairs={{12,0},{13,1},{14,2},{15,3},{0,4},{1,5},{2,6},{3,7},{4,8},{5,9},{6... | collective-permute-start | bytes 1179656 | tf_op jit(solution)/shard_map/ppermute | solution.py:245
  66.5 23.0 %all-to-all-start.1 = ((bf16[16,192,64]{1,2,0:T(8,128)(2,1)}), bf16[16,192,64]{1,2,0:T(8,128)(2,1)S(1)}, u32[]{:S(2)}, u32[]{:S(2)}) async-start(bf16[16,192,64]{1,2,0:T(8,128)(2,1)} %bitcast.6), calls=%async_computation.1 | async-start | bytes 1048576 | tf_op jit(solution)/shard_map/all_to_all | solution.py:280
  70.1 20.6 %collective-permute-start.9 = (bf16[192,1024]{1,0:T(8,128)(2,1)S(1)}, bf16[192,1024]{1,0:T(8,128)(2,1)}, u32[]{:S(2)}, u32[]{:S(2)}) collective-permute-start(bf16[192,1024]{1,0:T(8,128)(2,1)S(1)} %collective-permute-done.1.refs_1_), channel_id=1, source_target_pairs={{1,0},{2,1},{3,2},{0,3},{5,4},{6,5},{7,6},{4,7},{9,8},{10,9},{11,1... | collective-permute-start | bytes 1179656 | tf_op jit(solution)/shard_map/ppermute | solution.py:245
  74.5 16.2 %collective-permute-start.10 = (bf16[192,1024]{1,0:T(8,128)(2,1)}, bf16[192,1024]{1,0:T(8,128)(2,1)}, u32[]{:S(2)}, u32[]{:S(2)}) collective-permute-start(bf16[192,1024]{1,0:T(8,128)(2,1)} %collective-permute-done.7.refs_7_), channel_id=1, source_target_pairs={{3,0},{0,1},{1,2},{2,3},{7,4},{4,5},{5,6},{6,7},{11,8},{8,9},{9,10... | collective-permute-start | bytes 1179656 | tf_op jit(solution)/shard_map/ppermute | solution.py:245
  76.4 14.3 %collective-permute-start.15 = (bf16[192,1024]{1,0:T(8,128)(2,1)}, bf16[192,1024]{1,0:T(8,128)(2,1)}, u32[]{:S(2)}, u32[]{:S(2)}) collective-permute-start(bf16[192,1024]{1,0:T(8,128)(2,1)} %collective-permute-done.7.refs_7_), channel_id=1, source_target_pairs={{4,0},{5,1},{6,2},{7,3},{8,4},{9,5},{10,6},{11,7},{12,8},{13,9},{1... | collective-permute-start | bytes 1179656 | tf_op jit(solution)/shard_map/ppermute | solution.py:245
  80.8 14.6 %collective-permute-start.14 = (bf16[192,1024]{1,0:T(8,128)(2,1)}, bf16[192,1024]{1,0:T(8,128)(2,1)}, u32[]{:S(2)}, u32[]{:S(2)}) collective-permute-start(bf16[192,1024]{1,0:T(8,128)(2,1)} %collective-permute-done.6.refs_6_), channel_id=1, source_target_pairs={{3,0},{0,1},{1,2},{2,3},{7,4},{4,5},{5,6},{6,7},{11,8},{8,9},{9,10... | collective-permute-start | bytes 1179656 | tf_op jit(solution)/shard_map/ppermute | solution.py:245
  83.0 12.5 %collective-permute-start.13 = (bf16[192,1024]{1,0:T(8,128)(2,1)}, bf16[192,1024]{1,0:T(8,128)(2,1)}, u32[]{:S(2)}, u32[]{:S(2)}) collective-permute-start(bf16[192,1024]{1,0:T(8,128)(2,1)} %collective-permute-done.12.refs_12_), channel_id=1, source_target_pairs={{1,0},{2,1},{3,2},{0,3},{5,4},{6,5},{7,6},{4,7},{9,8},{10,9},{11,1... | collective-permute-start | bytes 1179656 | tf_op jit(solution)/shard_map/ppermute | solution.py:245
  127.2 10.0 %collective-permute-start.16 = (bf16[16,48,128]{2,1,0:T(8,128)(2,1)S(1)}, bf16[16,48,128]{2,1,0:T(8,128)(2,1)S(1)}, u32[]{:S(2)}, u32[]{:S(2)}) collective-permute-start(bf16[16,48,128]{2,1,0:T(8,128)(2,1)S(1)} %dynamic-slice_bitcast_fusion), channel_id=1, source_target_pairs={{0,16},{16,0},{32,48},{48,32},{64,80},{80,64},{96,112},{112,96},{1... | collective-permute-start | bytes 589832 | tf_op jit(solution)/shard_map/ppermute | solution.py:226
  132.3 30.6 %all-to-all-start.2 = ((bf16[16,192,256]{2,1,0:T(8,128)(2,1)}), bf16[16,192,256]{2,1,0:T(8,128)(2,1)S(1)}, u32[]{:S(2)}, u32[]{:S(2)}) async-start(bf16[16,192,256]{2,1,0:T(8,128)(2,1)} %bitcast.88), calls=%async_computation.2 | async-start | bytes 3145728 | tf_op jit(solution)/shard_map/all_to_all | solution.py:284
  137.3 6.5 %collective-permute-start.17 = (bf16[8,48,128]{2,1,0:T(8,128)(2,1)S(1)}, bf16[8,48,128]{2,1,0:T(8,128)(2,1)S(1)}, u32[]{:S(2)}, u32[]{:S(2)}) collective-permute-start(bf16[8,48,128]{2,1,0:T(8,128)(2,1)S(1)} %dynamic-slice_bitcast_fusion.1), channel_id=1, source_target_pairs={{0,32},{16,48},{32,0},{48,16},{64,96},{80,112},{96,64},{112,80},{1... | collective-permute-start | bytes 294920 | tf_op jit(solution)/shard_map/ppermute | solution.py:226
  149.9 8.5 %collective-permute-start.19 = (bf16[2,48,128]{2,1,0:T(8,128)(2,1)S(1)}, bf16[2,48,128]{2,1,0:T(8,128)(2,1)S(1)}, u32[]{:S(2)}, u32[]{:S(2)}) collective-permute-start(bf16[2,48,128]{2,1,0:T(8,128)(2,1)S(1)} %dynamic-slice_bitcast_fusion.3), channel_id=1, source_target_pairs={{0,128},{16,144},{32,160},{48,176},{64,192},{80,208},{96,224},{112... | collective-permute-start | bytes 73736 | tf_op jit(solution)/shard_map/ppermute | solution.py:226
  162.9 18.2 %collective-permute-start.20 = (bf16[1,48,128]{2,1,0:T(8,128)(2,1)S(1)}, bf16[1,48,128]{2,1,0:T(8,128)(2,1)S(1)}, u32[]{:S(2)}, u32[]{:S(2)}) collective-permute-start(bf16[1,48,128]{2,1,0:T(8,128)(2,1)S(1)} %constant_dynamic-slice_fusion), channel_id=1, source_target_pairs={{0,256},{16,272},{32,288},{48,304},{64,320},{80,336},{96,352},{112... | collective-permute-start | bytes 36872 | tf_op jit(solution)/shard_map/ppermute | solution.py:226
  (12 other events, 395.3 us)
Sparse Core Ops, SparseCore 0:
  19.7 95.7 all-gather.1

commit v6 on v5

--- a/solution.py
+++ b/solution.py
@@ -25,7 +25,7 @@
 
 
 def attend_kernel(
-    blocks_ref, counts_ref, owner_ref, ids_ref, w_ref, cot_ref, ocol_ref, orow_ref, *refs
+    blocks_ref, counts_ref, owner_ref, ids_ref, w_ref, cot_ref, ocol_ref, orow_ref, rest_ref, *refs
 ):
     members = owner_ref.shape[0]
     parts_refs, refs = refs[:members], refs[members:]
@@ -36,10 +36,21 @@
     keys = slots * rows
     tiles = nodes // ROWS
     local = nodes // members
-    loads = [
-        pltpu.make_async_copy(part, feat_ref.at[pl.ds(k * local, local), :], sem.at[k])
-        for k, part in enumerate(parts_refs)
-    ]
+    near = parts_refs[0].shape[1]
+    far = rest_ref.shape[1]
+
+    def at_owner(k):
+        return pl.ds(pl.multiple_of(owner_ref[k] * local, local), local)
+
+    loads = []
+    for k, part in enumerate(parts_refs):
+        to = pl.ds(k * local, local)
+        loads += [
+            pltpu.make_async_copy(part, feat_ref.at[to, pl.ds(0, near)], sem.at[2 * k]),
+            pltpu.make_async_copy(
+                rest_ref.at[at_owner(k), :], feat_ref.at[to, pl.ds(near, far)], sem.at[2 * k + 1]
+            ),
+        ]
     for load in loads:
         load.start()
 
@@ -55,12 +66,9 @@
         == lax.broadcasted_iota(jnp.int32, (HD, 4 * HD), 1)
     ).astype(F32).astype(BF)
 
-    def at_owner(k):
-        return pl.ds(pl.multiple_of(owner_ref[k] * local, local), local)
-
     batch = 4
     for b in range(0, members, batch):
-        for load in loads[b : b + batch]:
+        for load in loads[2 * b : 2 * (b + batch)]:
             load.wait()
         r = slice(b * local, (b + batch) * local)
         cot = jnp.concatenate([cot_ref[at_owner(b + k), :] for k in range(batch)], axis=0)
@@ -144,8 +152,8 @@
     gw_ref[:, deep:, :] = jnp.where(left, low, pltpu.roll(high, HD, 2)).astype(BF)
 
 
-def attend(blocks_of, owner, w_head, cot, order, blocks, counts, parts):
-    local, width = blocks_of[0].shape
+def attend(blocks_of, rest, owner, w_head, cot, order, blocks, counts, parts):
+    local, width = blocks_of[0].shape[0], blocks_of[0].shape[1] + rest.shape[1]
     nodes = len(blocks_of) * local
     tall, lanes = width // parts * 3 // 2, 2 * HD
     ids = (owner[:, None] * local + jnp.arange(local, dtype=jnp.int32)).reshape(1, nodes)
@@ -158,7 +166,7 @@
             jax.ShapeDtypeStruct((nodes, 4 * HD), BF),
             jax.ShapeDtypeStruct((parts, tall, lanes), BF),
         ],
-        in_specs=[smem] * 3 + [vmem] * 5 + [pl.BlockSpec(memory_space=pl.ANY)] * len(blocks_of),
+        in_specs=[smem] * 3 + [vmem] * 5 + [pl.BlockSpec(memory_space=pl.ANY)] * (1 + len(blocks_of)),
         out_specs=[vmem, vmem],
         scratch_shapes=[
             pltpu.VMEM((nodes, width), BF),
@@ -169,12 +177,12 @@
             pltpu.VMEM((nodes, 2 * HD), F32),
             pltpu.VMEM((nodes, 4 * HD), BF),
             pltpu.VMEM((width, 4 * HD), F32),
-            pltpu.SemaphoreType.DMA((len(blocks_of),)),
+            pltpu.SemaphoreType.DMA((2 * len(blocks_of),)),
         ],
         compiler_params=pltpu.CompilerParams(vmem_limit_bytes=52 << 20),
     )(
         blocks, counts, owner, ids, w_head, cot,
-        order.reshape(nodes, 1), order.reshape(1, nodes), *blocks_of,
+        order.reshape(nodes, 1), order.reshape(1, nodes), rest, *blocks_of,
     )
 
 
@@ -274,12 +282,14 @@
     )
     copies = jnp.broadcast_to(own[None], (size // 2, *own.shape))
     w_head = lax.all_to_all(copies, "dp", 0, 0, tiled=True, axis_index_groups=groups)
-    blocks_of, owner = gather_round(feats, "seq")
+    half = model_width // 2
+    rest = lax.all_gather(feats[:, half:], "seq", axis=0, tiled=True)
+    blocks_of, owner = gather_round(feats[:, :half], "seq")
     by_owner = cotangent[0].reshape(local_rows, HEADS, HD).transpose(1, 0, 2)
     by_owner, w_head = lax.optimization_barrier((by_owner, w_head))
     cot = lax.all_to_all(by_owner, "seq", 0, 0, tiled=True).reshape(HEADS * local_rows, HD)
     grads, part = attend(
-        blocks_of, owner, w_head, cot, node_order[0], blocks[0], counts[0], size
+        blocks_of, rest, owner, w_head, cot, node_order[0], blocks[0], counts[0], size
     )
     got = lax.all_to_all(grads.reshape(HEADS, local_rows, 4 * HD), "seq", 0, 0, tiled=True)
     total, (attended, grad_feats) = reduce_scatter(part, "dp", got, weights)

time: 190 us -> 198 us (1.042); the launches traced: 189 us -> 195 us
  local copies, waits for them, and re-layouts: 10.1 us -> 12.8 us
    ppermute x5, waiting for transfers between devices: 6.35 us -> 11.1 us  [reduce_scatter(): came = lax.ppermute(send, axis, [(i, i ^ bit) for i in range(size)])]
    all_to_all x1, waiting for transfers between devices: 4.45 us -> 0.37 us  [per_device(): lax.all_to_all(grads.reshape(HEADS, local_rows, 4 * HD), 'seq', 0, 0, til...]
    all_gather x1, waiting for transfers between devices: 0.02 us -> 3.39 us  [per_device(): lax.all_gather(chip, 'dp', axis=0, tiled=True, axis_index_groups=groups)]
    ppermute x15, waiting for transfers between devices: 6.67 us -> 4.1 us  [gather_round(): held[(hy + dy) % SIDE, (hx + dx) % SIDE] = lax.ppermute(source, axis, pairs)]
    unnamed x25 -> x27, local copies, waits for them, and re-layouts: 3.96 us -> 3.95 us
  transfers between devices with their start and end apart: 25 -> 26, of which waited for: 7 -> 8; matrix products, arithmetic and copies ran while one was open for 4% -> 5% of each run, Pallas kernels for 18% -> 18%
where the time goes in v6:
time: 198 us; the launch traced here: 195 us
  starting transfers between devices  109 us (55%)
  Pallas kernels  35.4 us (18%)
  waiting for transfers between devices  20.1 us (10%)
  between operations  14.7 us (7%)
  local copies, waits for them, and re-layouts  12.8 us (6%)
  other arithmetic  2.59 us (1%)
    ppermute x15, starting transfers between devices, gather_round(): held[(hy + dy) % SIDE, (hx + dx) % SIDE] = lax.ppermute(source, axis, pairs)  48.4 us
    pallas_call x1, Pallas kernels, attend(): pl.pallas_call(attend_kernel, name='attend', out_shape=[jax.ShapeDtypeStr...  32.3 us
    ppermute x5, starting transfers between devices, reduce_scatter(): came = lax.ppermute(send, axis, [(i, i ^ bit) for i in range(size)])  31.7 us
    ppermute x5, waiting for transfers between devices, reduce_scatter(): came = lax.ppermute(send, axis, [(i, i ^ bit) for i in range(size)])  11.1 us
    all_to_all x1, starting transfers between devices, per_device(): lax.all_to_all(copies, 'dp', 0, 0, tiled=True, axis_index_groups=groups)  9.54 us
    ppermute x1, starting transfers between devices, per_device(): other = lax.ppermute(ordered, 'dp', [(i, i ^ 1) for i in range(size)])  8.79 us
    all_to_all x1, starting transfers between devices, per_device(): lax.all_to_all(grads.reshape(HEADS, local_rows, 4 * HD), 'seq', 0, 0, til...  5.43 us
    all_to_all x1, starting transfers between devices, per_device(): lax.all_to_all(by_owner, 'seq', 0, 0, tiled=True)  5.16 us
  transfers between devices with their start and end apart: 26, of which 8 were waited for; matrix products, arithmetic and copies ran while one was open for 5% of the time, Pallas kernels for 18%

profile of v6, /device:TPU:1, one launch (start us, length us, event | category | flops | bytes accessed | tf_op | source)
XLA Modules:
  0.0 194.7 jit_solution(17471864154790090997)
XLA Ops:
  10.6 8.8 %collective-permute-start = (bf16[32,3072]{1,0:T(8,128)(2,1)S(1)}, bf16[32,3072]{1,0:T(8,128)(2,1)S(1)}, u32[]{:S(2)}, u32[]{:S(2)}) collective-permute-start(bf16[32,3072]{1,0:T(8,128)(2,1)S(1)} %constant_dynamic-update-slice_fusion), channel_id=1, source_target_pairs={{0,16},{16,0},{32,48},{48,32},{64,80},{80,64},{96,112},{112,96},{1... | collective-permute-start | bytes 589832 | tf_op jit(solution)/shard_map/ppermute | solution.py:271
  23.7 9.5 %all-to-all-start = ((bf16[16,96,128]{2,1,0:T(8,128)(2,1)}), bf16[16,96,128]{2,1,0:T(8,128)(2,1)S(1)}, u32[]{:S(2)}, u32[]{:S(2)}) async-start(bf16[16,96,128]{2,1,0:T(8,128)(2,1)} %broadcast_in_dim.2), calls=%async_computation | async-start | bytes 786432 | tf_op jit(solution)/shard_map/all_to_all | solution.py:284
  33.3 4.4 %collective-permute-start.1 = (bf16[192,512]{1,0:T(8,128)(2,1)S(1)}, bf16[192,512]{1,0:T(8,128)(2,1)S(1)}, u32[]{:S(2)}, u32[]{:S(2)}) collective-permute-start(bf16[192,512]{1,0:T(8,128)(2,1)S(1)} %get-tuple-element.25.refs_0_), channel_id=1, source_target_pairs={{1,0},{2,1},{3,2},{0,3},{5,4},{6,5},{7,6},{4,7},{9,8},{10,9},{11,1... | collective-permute-start | bytes 589832 | tf_op jit(solution)/shard_map/ppermute | solution.py:253
  39.6 3.2 %collective-permute-start.4 = (bf16[192,512]{1,0:T(8,128)(2,1)S(1)}, bf16[192,512]{1,0:T(8,128)(2,1)S(1)}, u32[]{:S(2)}, u32[]{:S(2)}) collective-permute-start(bf16[192,512]{1,0:T(8,128)(2,1)S(1)} %get-tuple-element.25.refs_0_), channel_id=1, source_target_pairs={{12,0},{13,1},{14,2},{15,3},{0,4},{1,5},{2,6},{3,7},{4,8},{5,9},{6... | collective-permute-start | bytes 589832 | tf_op jit(solution)/shard_map/ppermute | solution.py:253
  42.8 3.4 %collective-permute-start.3 = (bf16[192,512]{1,0:T(8,128)(2,1)S(1)}, bf16[192,512]{1,0:T(8,128)(2,1)S(1)}, u32[]{:S(2)}, u32[]{:S(2)}) collective-permute-start(bf16[192,512]{1,0:T(8,128)(2,1)S(1)} %get-tuple-element.25.refs_0_), channel_id=1, source_target_pairs={{4,0},{5,1},{6,2},{7,3},{8,4},{9,5},{10,6},{11,7},{12,8},{13,9},{1... | collective-permute-start | bytes 589832 | tf_op jit(solution)/shard_map/ppermute | solution.py:253
  49.9 4.6 %collective-permute-start.11 = (bf16[192,512]{1,0:T(8,128)(2,1)S(1)}, bf16[192,512]{1,0:T(8,128)(2,1)S(1)}, u32[]{:S(2)}, u32[]{:S(2)}) collective-permute-start(bf16[192,512]{1,0:T(8,128)(2,1)S(1)} %collective-permute-done.3.refs_3_), channel_id=1, source_target_pairs={{4,0},{5,1},{6,2},{7,3},{8,4},{9,5},{10,6},{11,7},{12,8},{13,9},{1... | collective-permute-start | bytes 589832 | tf_op jit(solution)/shard_map/ppermute | solution.py:253
  54.5 4.3 %collective-permute-start.5 = (bf16[192,512]{1,0:T(8,128)(2,1)S(1)}, bf16[192,512]{1,0:T(8,128)(2,1)S(1)}, u32[]{:S(2)}, u32[]{:S(2)}) collective-permute-start(bf16[192,512]{1,0:T(8,128)(2,1)S(1)} %collective-permute-done.3.refs_3_), channel_id=1, source_target_pairs={{1,0},{2,1},{3,2},{0,3},{5,4},{6,5},{7,6},{4,7},{9,8},{10,9},{11,1... | collective-permute-start | bytes 589832 | tf_op jit(solution)/shard_map/ppermute | solution.py:253
  62.9 3.2 %collective-permute-start.12 = (bf16[192,512]{1,0:T(8,128)(2,1)S(1)}, bf16[192,512]{1,0:T(8,128)(2,1)S(1)}, u32[]{:S(2)}, u32[]{:S(2)}) collective-permute-start(bf16[192,512]{1,0:T(8,128)(2,1)S(1)} %collective-permute-done.8.refs_8_), channel_id=1, source_target_pairs={{12,0},{13,1},{14,2},{15,3},{0,4},{1,5},{2,6},{3,7},{4,8},{5,9},{6... | collective-permute-start | bytes 589832 | tf_op jit(solution)/shard_map/ppermute | solution.py:253
  66.1 5.2 %all-to-all-start.1 = ((bf16[16,192,64]{1,2,0:T(8,128)(2,1)}), bf16[16,192,64]{1,2,0:T(8,128)(2,1)S(1)}, u32[]{:S(2)}, u32[]{:S(2)}) async-start(bf16[16,192,64]{1,2,0:T(8,128)(2,1)} %bitcast.6), calls=%async_computation.1 | async-start | bytes 1048576 | tf_op jit(solution)/shard_map/all_to_all | solution.py:290
  73.2 4.5 %collective-permute-start.9 = (bf16[192,512]{1,0:T(8,128)(2,1)S(1)}, bf16[192,512]{1,0:T(8,128)(2,1)S(1)}, u32[]{:S(2)}, u32[]{:S(2)}) collective-permute-start(bf16[192,512]{1,0:T(8,128)(2,1)S(1)} %collective-permute-done.1.refs_1_), channel_id=1, source_target_pairs={{1,0},{2,1},{3,2},{0,3},{5,4},{6,5},{7,6},{4,7},{9,8},{10,9},{11,1... | collective-permute-start | bytes 589832 | tf_op jit(solution)/shard_map/ppermute | solution.py:253
  79.6 4.3 %collective-permute-start.15 = (bf16[192,512]{1,0:T(8,128)(2,1)S(1)}, bf16[192,512]{1,0:T(8,128)(2,1)}, u32[]{:S(2)}, u32[]{:S(2)}) collective-permute-start(bf16[192,512]{1,0:T(8,128)(2,1)S(1)} %collective-permute-done.7.refs_7_), channel_id=1, source_target_pairs={{4,0},{5,1},{6,2},{7,3},{8,4},{9,5},{10,6},{11,7},{12,8},{13,9},{1... | collective-permute-start | bytes 589832 | tf_op jit(solution)/shard_map/ppermute | solution.py:253
  86.1 4.5 %collective-permute-start.13 = (bf16[192,512]{1,0:T(8,128)(2,1)S(1)}, bf16[192,512]{1,0:T(8,128)(2,1)}, u32[]{:S(2)}, u32[]{:S(2)}) collective-permute-start(bf16[192,512]{1,0:T(8,128)(2,1)S(1)} %collective-permute-done.12.refs_12_), channel_id=1, source_target_pairs={{1,0},{2,1},{3,2},{0,3},{5,4},{6,5},{7,6},{4,7},{9,8},{10,9},{11,1... | collective-permute-start | bytes 589832 | tf_op jit(solution)/shard_map/ppermute | solution.py:253
  91.9 3.5 %collective-permute-done.14.refs_14_ = bf16[192,512]{1,0:T(8,128)(2,1)} collective-permute-done((bf16[192,512]{1,0:T(8,128)(2,1)S(1)}, bf16[192,512]{1,0:T(8,128)(2,1)}, u32[]{:S(2)}, u32[]{:S(2)}) %collective-permute-start.14) | collective-permute-done | bytes 196640 | tf_op jit(solution)/shard_map/ppermute | solution.py:253
  95.4 32.3 %attend.1 = (bf16[3072,256]{1,0:T(8,128)(2,1)}, bf16[32,48,128]{2,1,0:T(8,128)(2,1)}) custom-call(s32[48,8]{1,0:T(8,128)S(1)} %bitcast.74, s32[48]{0:T(128)S(1)} %bitcast.76, s32[16]{0:T(128)S(1)} %fusion.6.owner_ref, s32[1,3072]{1,0:T(1,128)S(1)} %add.129.ids_ref, bf16[16,96,128]{2,1,0:T(8,128)(2,1)} %copy-done.3, bf16[3072,64]{1,0:T(8,128)(2,1)} %bitcast.77, ...), custom_call_target="tpu_custom_call" | custom-call | tf_op jit(solution)/shard_map/attend/pallas_call | solution.py:162
  128.7 5.8 %collective-permute-start.16 = (bf16[16,48,128]{2,1,0:T(8,128)(2,1)S(1)}, bf16[16,48,128]{2,1,0:T(8,128)(2,1)S(1)}, u32[]{:S(2)}, u32[]{:S(2)}) collective-permute-start(bf16[16,48,128]{2,1,0:T(8,128)(2,1)S(1)} %dynamic-slice_bitcast_fusion), channel_id=1, source_target_pairs={{0,16},{16,0},{32,48},{48,32},{64,80},{80,64},{96,112},{112,96},{1... | collective-permute-start | bytes 589832 | tf_op jit(solution)/shard_map/ppermute | solution.py:234
  134.6 5.4 %all-to-all-start.2 = ((bf16[16,192,256]{2,1,0:T(8,128)(2,1)}), bf16[16,192,256]{2,1,0:T(8,128)(2,1)S(1)}, u32[]{:S(2)}, u32[]{:S(2)}) async-start(bf16[16,192,256]{2,1,0:T(8,128)(2,1)} %bitcast.81), calls=%async_computation.2 | async-start | bytes 3145728 | tf_op jit(solution)/shard_map/all_to_all | solution.py:294
  140.1 3.4 %collective-permute-start.17 = (bf16[8,48,128]{2,1,0:T(8,128)(2,1)S(1)}, bf16[8,48,128]{2,1,0:T(8,128)(2,1)S(1)}, u32[]{:S(2)}, u32[]{:S(2)}) collective-permute-start(bf16[8,48,128]{2,1,0:T(8,128)(2,1)S(1)} %dynamic-slice_bitcast_fusion.1), channel_id=1, source_target_pairs={{0,32},{16,48},{32,0},{48,16},{64,96},{80,112},{96,64},{112,80},{1... | collective-permute-start | bytes 294920 | tf_op jit(solution)/shard_map/ppermute | solution.py:234
  143.5 5.4 %collective-permute-done.17 = bf16[8,48,128]{2,1,0:T(8,128)(2,1)S(1)} collective-permute-done((bf16[8,48,128]{2,1,0:T(8,128)(2,1)S(1)}, bf16[8,48,128]{2,1,0:T(8,128)(2,1)S(1)}, u32[]{:S(2)}, u32[]{:S(2)}) %collective-permute-start.17) | collective-permute-done | bytes 98336 | tf_op jit(solution)/shard_map/ppermute | solution.py:234
  149.0 4.0 %collective-permute-start.18 = (bf16[4,48,128]{2,1,0:T(8,128)(2,1)S(1)}, bf16[4,48,128]{2,1,0:T(8,128)(2,1)S(1)}, u32[]{:S(2)}, u32[]{:S(2)}) collective-permute-start(bf16[4,48,128]{2,1,0:T(8,128)(2,1)S(1)} %dynamic-slice_bitcast_fusion.2), channel_id=1, source_target_pairs={{0,64},{16,80},{32,96},{48,112},{64,0},{80,16},{96,32},{112,48},{1... | collective-permute-start | bytes 147464 | tf_op jit(solution)/shard_map/ppermute | solution.py:234
  153.0 3.2 %collective-permute-done.18 = bf16[4,48,128]{2,1,0:T(8,128)(2,1)S(1)} collective-permute-done((bf16[4,48,128]{2,1,0:T(8,128)(2,1)S(1)}, bf16[4,48,128]{2,1,0:T(8,128)(2,1)S(1)}, u32[]{:S(2)}, u32[]{:S(2)}) %collective-permute-start.18) | collective-permute-done | bytes 49184 | tf_op jit(solution)/shard_map/ppermute | solution.py:234
  156.3 6.5 %collective-permute-start.19 = (bf16[2,48,128]{2,1,0:T(8,128)(2,1)S(1)}, bf16[2,48,128]{2,1,0:T(8,128)(2,1)S(1)}, u32[]{:S(2)}, u32[]{:S(2)}) collective-permute-start(bf16[2,48,128]{2,1,0:T(8,128)(2,1)S(1)} %dynamic-slice_bitcast_fusion.3), channel_id=1, source_target_pairs={{0,128},{16,144},{32,160},{48,176},{64,192},{80,208},{96,224},{112... | collective-permute-start | bytes 73736 | tf_op jit(solution)/shard_map/ppermute | solution.py:234
  165.7 12.1 %collective-permute-start.20 = (bf16[1,48,128]{2,1,0:T(8,128)(2,1)S(1)}, bf16[1,48,128]{2,1,0:T(8,128)(2,1)S(1)}, u32[]{:S(2)}, u32[]{:S(2)}) collective-permute-start(bf16[1,48,128]{2,1,0:T(8,128)(2,1)S(1)} %constant_dynamic-slice_fusion), channel_id=1, source_target_pairs={{0,256},{16,272},{32,288},{48,304},{64,320},{80,336},{96,352},{112... | collective-permute-start | bytes 36872 | tf_op jit(solution)/shard_map/ppermute | solution.py:234
  177.8 3.4 %all-gather.5.cloned.1.call-done.w_ref = bf16[1024,3072]{1,0:T(8,128)(2,1)} async-done(((bf16[64,3072]{1,0:T(8,128)(2,1)}), bf16[1024,3072]{1,0:T(8,128)(2,1)}) %all-gather.5.cloned.1.call-update) | async-done | bytes 6291472 | tf_op jit(solution)/shard_map/all_gather | solution.py:276
  184.0 3.1 %finish.1 = (bf16[192,1024]{1,0:T(8,128)(2,1)}, bf16[192,1024]{1,0:T(8,128)(2,1)}) custom-call(bf16[16,192,256]{2,1,0:T(8,128)(2,1)S(1)} %all-to-all-done.2.g_ref, bf16[1024,3072]{1,0:T(8,128)(2,1)S(1)} %copy-done), custom_call_target="tpu_custom_call" | custom-call | tf_op jit(solution)/shard_map/finish/pallas_call | solution.py:209
  (90 shorter events, 32.1 us)
Async XLA Ops:
  7.2 88.2 %all-gather.3.cloned.1.call-start = ((), (), s32[]{:S(2)}) async-start(), calls=%async_computation.3 | async-start | bytes 3342336 | tf_op jit(solution)/shard_map/all_gather | solution.py:286
  9.0 172.3 %all-gather.5.cloned.1.call-start = ((), (), s32[]{:S(2)}) async-start(), calls=%async_computation.4 | async-start | bytes 6684672 | tf_op jit(solution)/shard_map/all_gather | solution.py:276
  10.6 9.8 %collective-permute-start = (bf16[32,3072]{1,0:T(8,128)(2,1)S(1)}, bf16[32,3072]{1,0:T(8,128)(2,1)S(1)}, u32[]{:S(2)}, u32[]{:S(2)}) collective-permute-start(bf16[32,3072]{1,0:T(8,128)(2,1)S(1)} %constant_dynamic-update-slice_fusion), channel_id=1, source_target_pairs={{0,16},{16,0},{32,48},{48,32},{64,80},{80,64},{96,112},{112,96},{1... | collective-permute-start | bytes 589832 | tf_op jit(solution)/shard_map/ppermute | solution.py:271
  23.7 42.4 %all-to-all-start = ((bf16[16,96,128]{2,1,0:T(8,128)(2,1)}), bf16[16,96,128]{2,1,0:T(8,128)(2,1)S(1)}, u32[]{:S(2)}, u32[]{:S(2)}) async-start(bf16[16,96,128]{2,1,0:T(8,128)(2,1)} %broadcast_in_dim.2), calls=%async_computation | async-start | bytes 786432 | tf_op jit(solution)/shard_map/all_to_all | solution.py:284
  33.3 13.9 %collective-permute-start.1 = (bf16[192,512]{1,0:T(8,128)(2,1)S(1)}, bf16[192,512]{1,0:T(8,128)(2,1)S(1)}, u32[]{:S(2)}, u32[]{:S(2)}) collective-permute-start(bf16[192,512]{1,0:T(8,128)(2,1)S(1)} %get-tuple-element.25.refs_0_), channel_id=1, source_target_pairs={{1,0},{2,1},{3,2},{0,3},{5,4},{6,5},{7,6},{4,7},{9,8},{10,9},{11,1... | collective-permute-start | bytes 589832 | tf_op jit(solution)/shard_map/ppermute | solution.py:253
  37.6 21.2 %collective-permute-start.2 = (bf16[192,512]{1,0:T(8,128)(2,1)S(1)}, bf16[192,512]{1,0:T(8,128)(2,1)S(1)}, u32[]{:S(2)}, u32[]{:S(2)}) collective-permute-start(bf16[192,512]{1,0:T(8,128)(2,1)S(1)} %get-tuple-element.25.refs_0_), channel_id=1, source_target_pairs={{3,0},{0,1},{1,2},{2,3},{7,4},{4,5},{5,6},{6,7},{11,8},{8,9},{9,10... | collective-permute-start | bytes 589832 | tf_op jit(solution)/shard_map/ppermute | solution.py:253
  39.6 21.3 %collective-permute-start.4 = (bf16[192,512]{1,0:T(8,128)(2,1)S(1)}, bf16[192,512]{1,0:T(8,128)(2,1)S(1)}, u32[]{:S(2)}, u32[]{:S(2)}) collective-permute-start(bf16[192,512]{1,0:T(8,128)(2,1)S(1)} %get-tuple-element.25.refs_0_), channel_id=1, source_target_pairs={{12,0},{13,1},{14,2},{15,3},{0,4},{1,5},{2,6},{3,7},{4,8},{5,9},{6... | collective-permute-start | bytes 589832 | tf_op jit(solution)/shard_map/ppermute | solution.py:253
  47.2 15.7 %collective-permute-start.8 = (bf16[192,512]{1,0:T(8,128)(2,1)S(1)}, bf16[192,512]{1,0:T(8,128)(2,1)S(1)}, u32[]{:S(2)}, u32[]{:S(2)}) collective-permute-start(bf16[192,512]{1,0:T(8,128)(2,1)S(1)} %collective-permute-done.1.refs_1_), channel_id=1, source_target_pairs={{12,0},{13,1},{14,2},{15,3},{0,4},{1,5},{2,6},{3,7},{4,8},{5,9},{6... | collective-permute-start | bytes 589832 | tf_op jit(solution)/shard_map/ppermute | solution.py:253
  49.9 29.7 %collective-permute-start.11 = (bf16[192,512]{1,0:T(8,128)(2,1)S(1)}, bf16[192,512]{1,0:T(8,128)(2,1)S(1)}, u32[]{:S(2)}, u32[]{:S(2)}) collective-permute-start(bf16[192,512]{1,0:T(8,128)(2,1)S(1)} %collective-permute-done.3.refs_3_), channel_id=1, source_target_pairs={{4,0},{5,1},{6,2},{7,3},{8,4},{9,5},{10,6},{11,7},{12,8},{13,9},{1... | collective-permute-start | bytes 589832 | tf_op jit(solution)/shard_map/ppermute | solution.py:253
  54.5 29.4 %collective-permute-start.5 = (bf16[192,512]{1,0:T(8,128)(2,1)S(1)}, bf16[192,512]{1,0:T(8,128)(2,1)S(1)}, u32[]{:S(2)}, u32[]{:S(2)}) collective-permute-start(bf16[192,512]{1,0:T(8,128)(2,1)S(1)} %collective-permute-done.3.refs_3_), channel_id=1, source_target_pairs={{1,0},{2,1},{3,2},{0,3},{5,4},{6,5},{7,6},{4,7},{9,8},{10,9},{11,1... | collective-permute-start | bytes 589832 | tf_op jit(solution)/shard_map/ppermute | solution.py:253
  58.8 14.4 %collective-permute-start.7 = (bf16[192,512]{1,0:T(8,128)(2,1)S(1)}, bf16[192,512]{1,0:T(8,128)(2,1)S(1)}, u32[]{:S(2)}, u32[]{:S(2)}) collective-permute-start(bf16[192,512]{1,0:T(8,128)(2,1)S(1)} %collective-permute-done.2.refs_2_), channel_id=1, source_target_pairs={{4,0},{5,1},{6,2},{7,3},{8,4},{9,5},{10,6},{11,7},{12,8},{13,9},{1... | collective-permute-start | bytes 589832 | tf_op jit(solution)/shard_map/ppermute | solution.py:253
  60.9 16.8 %collective-permute-start.6 = (bf16[192,512]{1,0:T(8,128)(2,1)S(1)}, bf16[192,512]{1,0:T(8,128)(2,1)S(1)}, u32[]{:S(2)}, u32[]{:S(2)}) collective-permute-start(bf16[192,512]{1,0:T(8,128)(2,1)S(1)} %collective-permute-done.4.refs_4_), channel_id=1, source_target_pairs={{3,0},{0,1},{1,2},{2,3},{7,4},{4,5},{5,6},{6,7},{11,8},{8,9},{9,10... | collective-permute-start | bytes 589832 | tf_op jit(solution)/shard_map/ppermute | solution.py:253
  62.9 23.3 %collective-permute-start.12 = (bf16[192,512]{1,0:T(8,128)(2,1)S(1)}, bf16[192,512]{1,0:T(8,128)(2,1)S(1)}, u32[]{:S(2)}, u32[]{:S(2)}) collective-permute-start(bf16[192,512]{1,0:T(8,128)(2,1)S(1)} %collective-permute-done.8.refs_8_), channel_id=1, source_target_pairs={{12,0},{13,1},{14,2},{15,3},{0,4},{1,5},{2,6},{3,7},{4,8},{5,9},{6... | collective-permute-start | bytes 589832 | tf_op jit(solution)/shard_map/ppermute | solution.py:253
  66.1 24.6 %all-to-all-start.1 = ((bf16[16,192,64]{1,2,0:T(8,128)(2,1)}), bf16[16,192,64]{1,2,0:T(8,128)(2,1)S(1)}, u32[]{:S(2)}, u32[]{:S(2)}) async-start(bf16[16,192,64]{1,2,0:T(8,128)(2,1)} %bitcast.6), calls=%async_computation.1 | async-start | bytes 1048576 | tf_op jit(solution)/shard_map/all_to_all | solution.py:290
  73.2 18.7 %collective-permute-start.9 = (bf16[192,512]{1,0:T(8,128)(2,1)S(1)}, bf16[192,512]{1,0:T(8,128)(2,1)S(1)}, u32[]{:S(2)}, u32[]{:S(2)}) collective-permute-start(bf16[192,512]{1,0:T(8,128)(2,1)S(1)} %collective-permute-done.1.refs_1_), channel_id=1, source_target_pairs={{1,0},{2,1},{3,2},{0,3},{5,4},{6,5},{7,6},{4,7},{9,8},{10,9},{11,1... | collective-permute-start | bytes 589832 | tf_op jit(solution)/shard_map/ppermute | solution.py:253
  77.7 14.2 %collective-permute-start.10 = (bf16[192,512]{1,0:T(8,128)(2,1)S(1)}, bf16[192,512]{1,0:T(8,128)(2,1)S(1)}, u32[]{:S(2)}, u32[]{:S(2)}) collective-permute-start(bf16[192,512]{1,0:T(8,128)(2,1)S(1)} %collective-permute-done.7.refs_7_), channel_id=1, source_target_pairs={{3,0},{0,1},{1,2},{2,3},{7,4},{4,5},{5,6},{6,7},{11,8},{8,9},{9,10... | collective-permute-start | bytes 589832 | tf_op jit(solution)/shard_map/ppermute | solution.py:253
  79.6 12.3 %collective-permute-start.15 = (bf16[192,512]{1,0:T(8,128)(2,1)S(1)}, bf16[192,512]{1,0:T(8,128)(2,1)}, u32[]{:S(2)}, u32[]{:S(2)}) collective-permute-start(bf16[192,512]{1,0:T(8,128)(2,1)S(1)} %collective-permute-done.7.refs_7_), channel_id=1, source_target_pairs={{4,0},{5,1},{6,2},{7,3},{8,4},{9,5},{10,6},{11,7},{12,8},{13,9},{1... | collective-permute-start | bytes 589832 | tf_op jit(solution)/shard_map/ppermute | solution.py:253
  84.0 11.4 %collective-permute-start.14 = (bf16[192,512]{1,0:T(8,128)(2,1)S(1)}, bf16[192,512]{1,0:T(8,128)(2,1)}, u32[]{:S(2)}, u32[]{:S(2)}) collective-permute-start(bf16[192,512]{1,0:T(8,128)(2,1)S(1)} %collective-permute-done.6.refs_6_), channel_id=1, source_target_pairs={{3,0},{0,1},{1,2},{2,3},{7,4},{4,5},{5,6},{6,7},{11,8},{8,9},{9,10... | collective-permute-start | bytes 589832 | tf_op jit(solution)/shard_map/ppermute | solution.py:253
  86.1 9.3 %collective-permute-start.13 = (bf16[192,512]{1,0:T(8,128)(2,1)S(1)}, bf16[192,512]{1,0:T(8,128)(2,1)}, u32[]{:S(2)}, u32[]{:S(2)}) collective-permute-start(bf16[192,512]{1,0:T(8,128)(2,1)S(1)} %collective-permute-done.12.refs_12_), channel_id=1, source_target_pairs={{1,0},{2,1},{3,2},{0,3},{5,4},{6,5},{7,6},{4,7},{9,8},{10,9},{11,1... | collective-permute-start | bytes 589832 | tf_op jit(solution)/shard_map/ppermute | solution.py:253
  128.7 11.3 %collective-permute-start.16 = (bf16[16,48,128]{2,1,0:T(8,128)(2,1)S(1)}, bf16[16,48,128]{2,1,0:T(8,128)(2,1)S(1)}, u32[]{:S(2)}, u32[]{:S(2)}) collective-permute-start(bf16[16,48,128]{2,1,0:T(8,128)(2,1)S(1)} %dynamic-slice_bitcast_fusion), channel_id=1, source_target_pairs={{0,16},{16,0},{32,48},{48,32},{64,80},{80,64},{96,112},{112,96},{1... | collective-permute-start | bytes 589832 | tf_op jit(solution)/shard_map/ppermute | solution.py:234
  134.6 31.1 %all-to-all-start.2 = ((bf16[16,192,256]{2,1,0:T(8,128)(2,1)}), bf16[16,192,256]{2,1,0:T(8,128)(2,1)S(1)}, u32[]{:S(2)}, u32[]{:S(2)}) async-start(bf16[16,192,256]{2,1,0:T(8,128)(2,1)} %bitcast.81), calls=%async_computation.2 | async-start | bytes 3145728 | tf_op jit(solution)/shard_map/all_to_all | solution.py:294
  140.1 8.9 %collective-permute-start.17 = (bf16[8,48,128]{2,1,0:T(8,128)(2,1)S(1)}, bf16[8,48,128]{2,1,0:T(8,128)(2,1)S(1)}, u32[]{:S(2)}, u32[]{:S(2)}) collective-permute-start(bf16[8,48,128]{2,1,0:T(8,128)(2,1)S(1)} %dynamic-slice_bitcast_fusion.1), channel_id=1, source_target_pairs={{0,32},{16,48},{32,0},{48,16},{64,96},{80,112},{96,64},{112,80},{1... | collective-permute-start | bytes 294920 | tf_op jit(solution)/shard_map/ppermute | solution.py:234
  156.3 9.0 %collective-permute-start.19 = (bf16[2,48,128]{2,1,0:T(8,128)(2,1)S(1)}, bf16[2,48,128]{2,1,0:T(8,128)(2,1)S(1)}, u32[]{:S(2)}, u32[]{:S(2)}) collective-permute-start(bf16[2,48,128]{2,1,0:T(8,128)(2,1)S(1)} %dynamic-slice_bitcast_fusion.3), channel_id=1, source_target_pairs={{0,128},{16,144},{32,160},{48,176},{64,192},{80,208},{96,224},{112... | collective-permute-start | bytes 73736 | tf_op jit(solution)/shard_map/ppermute | solution.py:234
  165.7 21.3 %collective-permute-start.20 = (bf16[1,48,128]{2,1,0:T(8,128)(2,1)S(1)}, bf16[1,48,128]{2,1,0:T(8,128)(2,1)S(1)}, u32[]{:S(2)}, u32[]{:S(2)}) collective-permute-start(bf16[1,48,128]{2,1,0:T(8,128)(2,1)S(1)} %constant_dynamic-slice_fusion), channel_id=1, source_target_pairs={{0,256},{16,272},{32,288},{48,304},{64,320},{80,336},{96,352},{112... | collective-permute-start | bytes 36872 | tf_op jit(solution)/shard_map/ppermute | solution.py:234
  (14 other events, 268.8 us)
Sparse Core Ops, SparseCore 0:
  11.0 81.1 all-gather.2
  94.9 86.2 all-gather.4

commit v7 on v5

--- a/solution.py
+++ b/solution.py
@@ -10,7 +10,7 @@
 BF = jnp.bfloat16
 F32 = jnp.float32
 ROWS = 1024
-GROUP = 12
+GROUP = 24
 SIDE = 4
 HOPS = (
     ((0, 0), (0, 1)), ((0, 0), (0, -1)), ((0, 0), (1, 0)), ((0, 0), (-1, 0)),
@@ -178,7 +178,16 @@
     )
 
 
-def finish_kernel(g_ref, w_ref, att_ref, gf_ref, lhs_ref):
+def finish_kernel(g_ref, w_ref, att_ref, gf_ref, lhs_ref, have_ref, sem):
+    bands = sem.shape[0]
+    band = w_ref.shape[0] // bands
+    cuts = [slice(i * band, (i + 1) * band) for i in range(bands)]
+    loads = [
+        pltpu.make_async_copy(w_ref.at[cut, :], have_ref.at[cut, :], sem.at[i])
+        for i, cut in enumerate(cuts)
+    ]
+    for load in loads:
+        load.start()
     heads = g_ref.shape[0]
     wide = heads * 2 * HD
     first = lax.broadcasted_iota(jnp.int32, (g_ref.shape[1], 2 * HD), 1) < HD
@@ -192,7 +201,9 @@
             first, even, pltpu.roll(odd, HD, 1)
         ).astype(BF)
         att_ref[:, to] = jnp.where(first, pltpu.roll(even, HD, 1), odd).astype(BF)
-    gf_ref[...] = dot(lhs_ref[...], w_ref[...], 1, 1).astype(BF)
+    for cut, load in zip(cuts, loads):
+        load.wait()
+        gf_ref[:, cut] = dot(lhs_ref[...], have_ref[cut, :], 1, 1).astype(BF)
 
 
 def finish(got, weights):
@@ -205,10 +216,14 @@
             jax.ShapeDtypeStruct((rows, HEADS * HD), BF),
             jax.ShapeDtypeStruct((rows, width), BF),
         ],
-        in_specs=[vmem, vmem],
+        in_specs=[vmem, pl.BlockSpec(memory_space=pl.ANY)],
         out_specs=[vmem, vmem],
-        scratch_shapes=[pltpu.VMEM((rows, weights.shape[1]), BF)],
-        compiler_params=pltpu.CompilerParams(vmem_limit_bytes=40 << 20),
+        scratch_shapes=[
+            pltpu.VMEM((rows, weights.shape[1]), BF),
+            pltpu.VMEM(weights.shape, BF),
+            pltpu.SemaphoreType.DMA((4,)),
+        ],
+        compiler_params=pltpu.CompilerParams(vmem_limit_bytes=57 << 20),
     )(got, weights)
 
 

time: 190 us -> 191 us (level)
  Pallas kernels: 34.7 us -> 39.1 us
  local copies, waits for them, and re-layouts: 10.1 us -> 7.37 us
    pallas_call x1, Pallas kernels: 3.05 us -> 7.82 us  [finish(): pl.pallas_call(finish_kernel, name='finish', out_shape=[jax.ShapeDtypeStr...]
    unnamed x25, local copies, waits for them, and re-layouts: 3.96 us -> 1.19 us
  transfers between devices with their start and end apart: 25 -> 25, of which waited for: 7 -> 7; matrix products, arithmetic and copies ran while one was open for 4% -> 4% of each run, Pallas kernels for 18% -> 21%
where the time goes in v7:
time: 191 us; the launch traced here: 190 us
  starting transfers between devices  108 us (57%)
  Pallas kernels  39.1 us (20%)
  waiting for transfers between devices  18.5 us (10%)
  between operations  14.7 us (8%)
  local copies, waits for them, and re-layouts  7.37 us (4%)
  other arithmetic  2.59 us (1%)
    ppermute x15, starting transfers between devices, gather_round(): held[(hy + dy) % SIDE, (hx + dx) % SIDE] = lax.ppermute(source, axis, pairs)  48.9 us
    ppermute x5, starting transfers between devices, reduce_scatter(): came = lax.ppermute(send, axis, [(i, i ^ bit) for i in range(size)])  32.1 us
    pallas_call x1, Pallas kernels, attend(): pl.pallas_call(attend_kernel, name='attend', out_shape=[jax.ShapeDtypeStr...  31.2 us
    all_to_all x1, starting transfers between devices, per_device(): lax.all_to_all(copies, 'dp', 0, 0, tiled=True, axis_index_groups=groups)  9.54 us
    ppermute x1, starting transfers between devices, per_device(): other = lax.ppermute(ordered, 'dp', [(i, i ^ 1) for i in range(size)])  8.92 us
    pallas_call x1, Pallas kernels, finish(): pl.pallas_call(finish_kernel, name='finish', out_shape=[jax.ShapeDtypeStr...  7.82 us
    ppermute x15, waiting for transfers between devices, gather_round(): held[(hy + dy) % SIDE, (hx + dx) % SIDE] = lax.ppermute(source, axis, pairs)  6.85 us
    ppermute x5, waiting for transfers between devices, reduce_scatter(): came = lax.ppermute(send, axis, [(i, i ^ bit) for i in range(size)])  6.22 us
  transfers between devices with their start and end apart: 25, of which 7 were waited for; matrix products, arithmetic and copies ran while one was open for 4% of the time, Pallas kernels for 21%

profile of v7, /device:TPU:1, one launch (start us, length us, event | category | flops | bytes accessed | tf_op | source)
XLA Modules:
  0.0 190.3 jit_solution(12796960168572098932)
XLA Ops:
  8.8 8.9 %collective-permute-start = (bf16[32,3072]{1,0:T(8,128)(2,1)S(1)}, bf16[32,3072]{1,0:T(8,128)(2,1)S(1)}, u32[]{:S(2)}, u32[]{:S(2)}) collective-permute-start(bf16[32,3072]{1,0:T(8,128)(2,1)S(1)} %constant_dynamic-update-slice_fusion), channel_id=1, source_target_pairs={{0,16},{16,0},{32,48},{48,32},{64,80},{80,64},{96,112},{112,96},{1... | collective-permute-start | bytes 589832 | tf_op jit(solution)/shard_map/ppermute | solution.py:278
  22.0 9.5 %all-to-all-start = ((bf16[16,96,128]{2,1,0:T(8,128)(2,1)}), bf16[16,96,128]{2,1,0:T(8,128)(2,1)S(1)}, u32[]{:S(2)}, u32[]{:S(2)}) async-start(bf16[16,96,128]{2,1,0:T(8,128)(2,1)} %broadcast_in_dim.2), calls=%async_computation | async-start | bytes 786432 | tf_op jit(solution)/shard_map/all_to_all | solution.py:291
  31.6 4.4 %collective-permute-start.1 = (bf16[192,1024]{1,0:T(8,128)(2,1)S(1)}, bf16[192,1024]{1,0:T(8,128)(2,1)S(1)}, u32[]{:S(2)}, u32[]{:S(2)}) collective-permute-start(bf16[192,1024]{1,0:T(8,128)(2,1)S(1)} %bitcast.74), channel_id=1, source_target_pairs={{1,0},{2,1},{3,2},{0,3},{5,4},{6,5},{7,6},{4,7},{9,8},{10,9},{11,1... | collective-permute-start | bytes 1179656 | tf_op jit(solution)/shard_map/ppermute | solution.py:260
  37.9 3.2 %collective-permute-start.4 = (bf16[192,1024]{1,0:T(8,128)(2,1)S(1)}, bf16[192,1024]{1,0:T(8,128)(2,1)S(1)}, u32[]{:S(2)}, u32[]{:S(2)}) collective-permute-start(bf16[192,1024]{1,0:T(8,128)(2,1)S(1)} %bitcast.76), channel_id=1, source_target_pairs={{12,0},{13,1},{14,2},{15,3},{0,4},{1,5},{2,6},{3,7},{4,8},{5,9},{6... | collective-permute-start | bytes 1179656 | tf_op jit(solution)/shard_map/ppermute | solution.py:260
  41.1 3.4 %collective-permute-start.3 = (bf16[192,1024]{1,0:T(8,128)(2,1)S(1)}, bf16[192,1024]{1,0:T(8,128)(2,1)S(1)}, u32[]{:S(2)}, u32[]{:S(2)}) collective-permute-start(bf16[192,1024]{1,0:T(8,128)(2,1)S(1)} %bitcast.77), channel_id=1, source_target_pairs={{4,0},{5,1},{6,2},{7,3},{8,4},{9,5},{10,6},{11,7},{12,8},{13,9},{1... | collective-permute-start | bytes 1179656 | tf_op jit(solution)/shard_map/ppermute | solution.py:260
  44.5 2.5 %collective-permute-start.8 = (bf16[192,1024]{1,0:T(8,128)(2,1)S(1)}, bf16[192,1024]{1,0:T(8,128)(2,1)S(1)}, u32[]{:S(2)}, u32[]{:S(2)}) collective-permute-start(bf16[192,1024]{1,0:T(8,128)(2,1)S(1)} %collective-permute-done.1.refs_1_), channel_id=1, source_target_pairs={{12,0},{13,1},{14,2},{15,3},{0,4},{1,5},{2,6},{3,7},{4,8},{5,9},{6... | collective-permute-start | bytes 1179656 | tf_op jit(solution)/shard_map/ppermute | solution.py:260
  48.9 4.6 %collective-permute-start.7 = (bf16[192,1024]{1,0:T(8,128)(2,1)S(1)}, bf16[192,1024]{1,0:T(8,128)(2,1)}, u32[]{:S(2)}, u32[]{:S(2)}) collective-permute-start(bf16[192,1024]{1,0:T(8,128)(2,1)S(1)} %collective-permute-done.2.refs_2_), channel_id=1, source_target_pairs={{4,0},{5,1},{6,2},{7,3},{8,4},{9,5},{10,6},{11,7},{12,8},{13,9},{1... | collective-permute-start | bytes 1179656 | tf_op jit(solution)/shard_map/ppermute | solution.py:260
  57.9 4.6 %collective-permute-start.5 = (bf16[192,1024]{1,0:T(8,128)(2,1)S(1)}, bf16[192,1024]{1,0:T(8,128)(2,1)}, u32[]{:S(2)}, u32[]{:S(2)}) collective-permute-start(bf16[192,1024]{1,0:T(8,128)(2,1)S(1)} %collective-permute-done.3.refs_3_), channel_id=1, source_target_pairs={{1,0},{2,1},{3,2},{0,3},{5,4},{6,5},{7,6},{4,7},{9,8},{10,9},{11,1... | collective-permute-start | bytes 1179656 | tf_op jit(solution)/shard_map/ppermute | solution.py:260
  62.5 2.9 %collective-permute-start.12 = (bf16[192,1024]{1,0:T(8,128)(2,1)S(1)}, bf16[192,1024]{1,0:T(8,128)(2,1)}, u32[]{:S(2)}, u32[]{:S(2)}) collective-permute-start(bf16[192,1024]{1,0:T(8,128)(2,1)S(1)} %collective-permute-done.8.refs_8_), channel_id=1, source_target_pairs={{12,0},{13,1},{14,2},{15,3},{0,4},{1,5},{2,6},{3,7},{4,8},{5,9},{6... | collective-permute-start | bytes 1179656 | tf_op jit(solution)/shard_map/ppermute | solution.py:260
  66.5 3.6 %all-to-all-start.1 = ((bf16[16,192,64]{1,2,0:T(8,128)(2,1)}), bf16[16,192,64]{1,2,0:T(8,128)(2,1)S(1)}, u32[]{:S(2)}, u32[]{:S(2)}) async-start(bf16[16,192,64]{1,2,0:T(8,128)(2,1)} %bitcast.6), calls=%async_computation.1 | async-start | bytes 1048576 | tf_op jit(solution)/shard_map/all_to_all | solution.py:295
  70.1 4.4 %collective-permute-start.9 = (bf16[192,1024]{1,0:T(8,128)(2,1)S(1)}, bf16[192,1024]{1,0:T(8,128)(2,1)}, u32[]{:S(2)}, u32[]{:S(2)}) collective-permute-start(bf16[192,1024]{1,0:T(8,128)(2,1)S(1)} %collective-permute-done.1.refs_1_), channel_id=1, source_target_pairs={{1,0},{2,1},{3,2},{0,3},{5,4},{6,5},{7,6},{4,7},{9,8},{10,9},{11,1... | collective-permute-start | bytes 1179656 | tf_op jit(solution)/shard_map/ppermute | solution.py:260
  76.4 4.4 %collective-permute-start.15 = (bf16[192,1024]{1,0:T(8,128)(2,1)}, bf16[192,1024]{1,0:T(8,128)(2,1)}, u32[]{:S(2)}, u32[]{:S(2)}) collective-permute-start(bf16[192,1024]{1,0:T(8,128)(2,1)} %collective-permute-done.7.refs_7_), channel_id=1, source_target_pairs={{4,0},{5,1},{6,2},{7,3},{8,4},{9,5},{10,6},{11,7},{12,8},{13,9},{1... | collective-permute-start | bytes 1179656 | tf_op jit(solution)/shard_map/ppermute | solution.py:260
  83.0 4.4 %collective-permute-start.13 = (bf16[192,1024]{1,0:T(8,128)(2,1)}, bf16[192,1024]{1,0:T(8,128)(2,1)}, u32[]{:S(2)}, u32[]{:S(2)}) collective-permute-start(bf16[192,1024]{1,0:T(8,128)(2,1)} %collective-permute-done.12.refs_12_), channel_id=1, source_target_pairs={{1,0},{2,1},{3,2},{0,3},{5,4},{6,5},{7,6},{4,7},{9,8},{10,9},{11,1... | collective-permute-start | bytes 1179656 | tf_op jit(solution)/shard_map/ppermute | solution.py:260
  90.5 4.9 %collective-permute-done.14.refs_14_ = bf16[192,1024]{1,0:T(8,128)(2,1)} collective-permute-done((bf16[192,1024]{1,0:T(8,128)(2,1)}, bf16[192,1024]{1,0:T(8,128)(2,1)}, u32[]{:S(2)}, u32[]{:S(2)}) %collective-permute-start.14) | collective-permute-done | bytes 393248 | tf_op jit(solution)/shard_map/ppermute | solution.py:260
  95.4 31.2 %attend.1 = (bf16[3072,256]{1,0:T(8,128)(2,1)}, bf16[32,48,128]{2,1,0:T(8,128)(2,1)S(1)}) custom-call(s32[48,8]{1,0:T(8,128)S(1)} %bitcast.81, s32[48]{0:T(128)S(1)} %bitcast.83, s32[16]{0:T(128)S(1)} %fusion.6.owner_ref, s32[1,3072]{1,0:T(1,128)S(1)} %add.129.ids_ref, bf16[16,96,128]{2,1,0:T(8,128)(2,1)S(1)} %all-to-all-done.w_ref, ...), custom_call_target="tpu_custom_call" | custom-call | tf_op jit(solution)/shard_map/attend/pallas_call | solution.py:154
  126.7 5.0 %collective-permute-start.16 = (bf16[16,48,128]{2,1,0:T(8,128)(2,1)S(1)}, bf16[16,48,128]{2,1,0:T(8,128)(2,1)S(1)}, u32[]{:S(2)}, u32[]{:S(2)}) collective-permute-start(bf16[16,48,128]{2,1,0:T(8,128)(2,1)S(1)} %dynamic-slice_bitcast_fusion), channel_id=1, source_target_pairs={{0,16},{16,0},{32,48},{48,32},{64,80},{80,64},{96,112},{112,96},{1... | collective-permute-start | bytes 589832 | tf_op jit(solution)/shard_map/ppermute | solution.py:241
  131.8 4.9 %all-to-all-start.2 = ((bf16[16,192,256]{2,1,0:T(8,128)(2,1)}), bf16[16,192,256]{2,1,0:T(8,128)(2,1)S(1)}, u32[]{:S(2)}, u32[]{:S(2)}) async-start(bf16[16,192,256]{2,1,0:T(8,128)(2,1)} %bitcast.88), calls=%async_computation.2 | async-start | bytes 3145728 | tf_op jit(solution)/shard_map/all_to_all | solution.py:299
  136.8 3.9 %collective-permute-start.17 = (bf16[8,48,128]{2,1,0:T(8,128)(2,1)S(1)}, bf16[8,48,128]{2,1,0:T(8,128)(2,1)S(1)}, u32[]{:S(2)}, u32[]{:S(2)}) collective-permute-start(bf16[8,48,128]{2,1,0:T(8,128)(2,1)S(1)} %dynamic-slice_bitcast_fusion.1), channel_id=1, source_target_pairs={{0,32},{16,48},{32,0},{48,16},{64,96},{80,112},{96,64},{112,80},{1... | collective-permute-start | bytes 294920 | tf_op jit(solution)/shard_map/ppermute | solution.py:241
  140.7 2.7 %collective-permute-done.17 = bf16[8,48,128]{2,1,0:T(8,128)(2,1)S(1)} collective-permute-done((bf16[8,48,128]{2,1,0:T(8,128)(2,1)S(1)}, bf16[8,48,128]{2,1,0:T(8,128)(2,1)S(1)}, u32[]{:S(2)}, u32[]{:S(2)}) %collective-permute-start.17) | collective-permute-done | bytes 98336 | tf_op jit(solution)/shard_map/ppermute | solution.py:241
  143.4 4.0 %collective-permute-start.18 = (bf16[4,48,128]{2,1,0:T(8,128)(2,1)S(1)}, bf16[4,48,128]{2,1,0:T(8,128)(2,1)S(1)}, u32[]{:S(2)}, u32[]{:S(2)}) collective-permute-start(bf16[4,48,128]{2,1,0:T(8,128)(2,1)S(1)} %dynamic-slice_bitcast_fusion.2), channel_id=1, source_target_pairs={{0,64},{16,80},{32,96},{48,112},{64,0},{80,16},{96,32},{112,48},{1... | collective-permute-start | bytes 147464 | tf_op jit(solution)/shard_map/ppermute | solution.py:241
  149.5 7.0 %collective-permute-start.19 = (bf16[2,48,128]{2,1,0:T(8,128)(2,1)S(1)}, bf16[2,48,128]{2,1,0:T(8,128)(2,1)S(1)}, u32[]{:S(2)}, u32[]{:S(2)}) collective-permute-start(bf16[2,48,128]{2,1,0:T(8,128)(2,1)S(1)} %dynamic-slice_bitcast_fusion.3), channel_id=1, source_target_pairs={{0,128},{16,144},{32,160},{48,176},{64,192},{80,208},{96,224},{112... | collective-permute-start | bytes 73736 | tf_op jit(solution)/shard_map/ppermute | solution.py:241
  158.0 4.4 %all-to-all-done.2.g_ref = bf16[16,192,256]{2,1,0:T(8,128)(2,1)S(1)} async-done(((bf16[16,192,256]{2,1,0:T(8,128)(2,1)}), bf16[16,192,256]{2,1,0:T(8,128)(2,1)S(1)}, u32[]{:S(2)}, u32[]{:S(2)}) %all-to-all-start.2) | async-done | bytes 1572896 | tf_op jit(solution)/shard_map/all_to_all | solution.py:299
  162.4 12.3 %collective-permute-start.20 = (bf16[1,48,128]{2,1,0:T(8,128)(2,1)S(1)}, bf16[1,48,128]{2,1,0:T(8,128)(2,1)S(1)}, u32[]{:S(2)}, u32[]{:S(2)}) collective-permute-start(bf16[1,48,128]{2,1,0:T(8,128)(2,1)S(1)} %constant_dynamic-slice_fusion), channel_id=1, source_target_pairs={{0,256},{16,272},{32,288},{48,304},{64,320},{80,336},{96,352},{112... | collective-permute-start | bytes 36872 | tf_op jit(solution)/shard_map/ppermute | solution.py:241
  174.8 7.8 %finish.1 = (bf16[192,1024]{1,0:T(8,128)(2,1)}, bf16[192,1024]{1,0:T(8,128)(2,1)}) custom-call(bf16[16,192,256]{2,1,0:T(8,128)(2,1)} %copy-done.3, bf16[1024,3072]{1,0:T(8,128)(2,1)} %all-gather.2.cloned.1.call-done.w_ref), custom_call_target="tpu_custom_call" | custom-call | tf_op jit(solution)/shard_map/finish/pallas_call | solution.py:212
  (84 shorter events, 26.8 us)
Async XLA Ops:
  7.2 167.6 %all-gather.2.cloned.1.call-start = ((), (), s32[]{:S(2)}) async-start(), calls=%async_computation.3 | async-start | bytes 6684672 | tf_op jit(solution)/shard_map/all_gather | solution.py:283
  8.8 10.0 %collective-permute-start = (bf16[32,3072]{1,0:T(8,128)(2,1)S(1)}, bf16[32,3072]{1,0:T(8,128)(2,1)S(1)}, u32[]{:S(2)}, u32[]{:S(2)}) collective-permute-start(bf16[32,3072]{1,0:T(8,128)(2,1)S(1)} %constant_dynamic-update-slice_fusion), channel_id=1, source_target_pairs={{0,16},{16,0},{32,48},{48,32},{64,80},{80,64},{96,112},{112,96},{1... | collective-permute-start | bytes 589832 | tf_op jit(solution)/shard_map/ppermute | solution.py:278
  22.0 44.4 %all-to-all-start = ((bf16[16,96,128]{2,1,0:T(8,128)(2,1)}), bf16[16,96,128]{2,1,0:T(8,128)(2,1)S(1)}, u32[]{:S(2)}, u32[]{:S(2)}) async-start(bf16[16,96,128]{2,1,0:T(8,128)(2,1)} %broadcast_in_dim.2), calls=%async_computation | async-start | bytes 786432 | tf_op jit(solution)/shard_map/all_to_all | solution.py:291
  31.6 12.9 %collective-permute-start.1 = (bf16[192,1024]{1,0:T(8,128)(2,1)S(1)}, bf16[192,1024]{1,0:T(8,128)(2,1)S(1)}, u32[]{:S(2)}, u32[]{:S(2)}) collective-permute-start(bf16[192,1024]{1,0:T(8,128)(2,1)S(1)} %bitcast.74), channel_id=1, source_target_pairs={{1,0},{2,1},{3,2},{0,3},{5,4},{6,5},{7,6},{4,7},{9,8},{10,9},{11,1... | collective-permute-start | bytes 1179656 | tf_op jit(solution)/shard_map/ppermute | solution.py:260
  36.0 12.9 %collective-permute-start.2 = (bf16[192,1024]{1,0:T(8,128)(2,1)S(1)}, bf16[192,1024]{1,0:T(8,128)(2,1)S(1)}, u32[]{:S(2)}, u32[]{:S(2)}) collective-permute-start(bf16[192,1024]{1,0:T(8,128)(2,1)S(1)} %bitcast.75), channel_id=1, source_target_pairs={{3,0},{0,1},{1,2},{2,3},{7,4},{4,5},{5,6},{6,7},{11,8},{8,9},{9,10... | collective-permute-start | bytes 1179656 | tf_op jit(solution)/shard_map/ppermute | solution.py:260
  37.9 15.6 %collective-permute-start.4 = (bf16[192,1024]{1,0:T(8,128)(2,1)S(1)}, bf16[192,1024]{1,0:T(8,128)(2,1)S(1)}, u32[]{:S(2)}, u32[]{:S(2)}) collective-permute-start(bf16[192,1024]{1,0:T(8,128)(2,1)S(1)} %bitcast.76), channel_id=1, source_target_pairs={{12,0},{13,1},{14,2},{15,3},{0,4},{1,5},{2,6},{3,7},{4,8},{5,9},{6... | collective-permute-start | bytes 1179656 | tf_op jit(solution)/shard_map/ppermute | solution.py:260
  41.1 14.4 %collective-permute-start.3 = (bf16[192,1024]{1,0:T(8,128)(2,1)S(1)}, bf16[192,1024]{1,0:T(8,128)(2,1)S(1)}, u32[]{:S(2)}, u32[]{:S(2)}) collective-permute-start(bf16[192,1024]{1,0:T(8,128)(2,1)S(1)} %bitcast.77), channel_id=1, source_target_pairs={{4,0},{5,1},{6,2},{7,3},{8,4},{9,5},{10,6},{11,7},{12,8},{13,9},{1... | collective-permute-start | bytes 1179656 | tf_op jit(solution)/shard_map/ppermute | solution.py:260
  44.5 18.0 %collective-permute-start.8 = (bf16[192,1024]{1,0:T(8,128)(2,1)S(1)}, bf16[192,1024]{1,0:T(8,128)(2,1)S(1)}, u32[]{:S(2)}, u32[]{:S(2)}) collective-permute-start(bf16[192,1024]{1,0:T(8,128)(2,1)S(1)} %collective-permute-done.1.refs_1_), channel_id=1, source_target_pairs={{12,0},{13,1},{14,2},{15,3},{0,4},{1,5},{2,6},{3,7},{4,8},{5,9},{6... | collective-permute-start | bytes 1179656 | tf_op jit(solution)/shard_map/ppermute | solution.py:260
  48.9 21.2 %collective-permute-start.7 = (bf16[192,1024]{1,0:T(8,128)(2,1)S(1)}, bf16[192,1024]{1,0:T(8,128)(2,1)}, u32[]{:S(2)}, u32[]{:S(2)}) collective-permute-start(bf16[192,1024]{1,0:T(8,128)(2,1)S(1)} %collective-permute-done.2.refs_2_), channel_id=1, source_target_pairs={{4,0},{5,1},{6,2},{7,3},{8,4},{9,5},{10,6},{11,7},{12,8},{13,9},{1... | collective-permute-start | bytes 1179656 | tf_op jit(solution)/shard_map/ppermute | solution.py:260
  53.5 20.9 %collective-permute-start.6 = (bf16[192,1024]{1,0:T(8,128)(2,1)S(1)}, bf16[192,1024]{1,0:T(8,128)(2,1)}, u32[]{:S(2)}, u32[]{:S(2)}) collective-permute-start(bf16[192,1024]{1,0:T(8,128)(2,1)S(1)} %collective-permute-done.4.refs_4_), channel_id=1, source_target_pairs={{3,0},{0,1},{1,2},{2,3},{7,4},{4,5},{5,6},{6,7},{11,8},{8,9},{9,10... | collective-permute-start | bytes 1179656 | tf_op jit(solution)/shard_map/ppermute | solution.py:260
  55.5 20.9 %collective-permute-start.11 = (bf16[192,1024]{1,0:T(8,128)(2,1)S(1)}, bf16[192,1024]{1,0:T(8,128)(2,1)}, u32[]{:S(2)}, u32[]{:S(2)}) collective-permute-start(bf16[192,1024]{1,0:T(8,128)(2,1)S(1)} %collective-permute-done.3.refs_3_), channel_id=1, source_target_pairs={{4,0},{5,1},{6,2},{7,3},{8,4},{9,5},{10,6},{11,7},{12,8},{13,9},{1... | collective-permute-start | bytes 1179656 | tf_op jit(solution)/shard_map/ppermute | solution.py:260
  57.9 22.9 %collective-permute-start.5 = (bf16[192,1024]{1,0:T(8,128)(2,1)S(1)}, bf16[192,1024]{1,0:T(8,128)(2,1)}, u32[]{:S(2)}, u32[]{:S(2)}) collective-permute-start(bf16[192,1024]{1,0:T(8,128)(2,1)S(1)} %collective-permute-done.3.refs_3_), channel_id=1, source_target_pairs={{1,0},{2,1},{3,2},{0,3},{5,4},{6,5},{7,6},{4,7},{9,8},{10,9},{11,1... | collective-permute-start | bytes 1179656 | tf_op jit(solution)/shard_map/ppermute | solution.py:260
  62.5 20.5 %collective-permute-start.12 = (bf16[192,1024]{1,0:T(8,128)(2,1)S(1)}, bf16[192,1024]{1,0:T(8,128)(2,1)}, u32[]{:S(2)}, u32[]{:S(2)}) collective-permute-start(bf16[192,1024]{1,0:T(8,128)(2,1)S(1)} %collective-permute-done.8.refs_8_), channel_id=1, source_target_pairs={{12,0},{13,1},{14,2},{15,3},{0,4},{1,5},{2,6},{3,7},{4,8},{5,9},{6... | collective-permute-start | bytes 1179656 | tf_op jit(solution)/shard_map/ppermute | solution.py:260
  66.5 22.8 %all-to-all-start.1 = ((bf16[16,192,64]{1,2,0:T(8,128)(2,1)}), bf16[16,192,64]{1,2,0:T(8,128)(2,1)S(1)}, u32[]{:S(2)}, u32[]{:S(2)}) async-start(bf16[16,192,64]{1,2,0:T(8,128)(2,1)} %bitcast.6), calls=%async_computation.1 | async-start | bytes 1048576 | tf_op jit(solution)/shard_map/all_to_all | solution.py:295
  70.1 20.4 %collective-permute-start.9 = (bf16[192,1024]{1,0:T(8,128)(2,1)S(1)}, bf16[192,1024]{1,0:T(8,128)(2,1)}, u32[]{:S(2)}, u32[]{:S(2)}) collective-permute-start(bf16[192,1024]{1,0:T(8,128)(2,1)S(1)} %collective-permute-done.1.refs_1_), channel_id=1, source_target_pairs={{1,0},{2,1},{3,2},{0,3},{5,4},{6,5},{7,6},{4,7},{9,8},{10,9},{11,1... | collective-permute-start | bytes 1179656 | tf_op jit(solution)/shard_map/ppermute | solution.py:260
  74.5 16.0 %collective-permute-start.10 = (bf16[192,1024]{1,0:T(8,128)(2,1)}, bf16[192,1024]{1,0:T(8,128)(2,1)}, u32[]{:S(2)}, u32[]{:S(2)}) collective-permute-start(bf16[192,1024]{1,0:T(8,128)(2,1)} %collective-permute-done.7.refs_7_), channel_id=1, source_target_pairs={{3,0},{0,1},{1,2},{2,3},{7,4},{4,5},{5,6},{6,7},{11,8},{8,9},{9,10... | collective-permute-start | bytes 1179656 | tf_op jit(solution)/shard_map/ppermute | solution.py:260
  76.4 14.1 %collective-permute-start.15 = (bf16[192,1024]{1,0:T(8,128)(2,1)}, bf16[192,1024]{1,0:T(8,128)(2,1)}, u32[]{:S(2)}, u32[]{:S(2)}) collective-permute-start(bf16[192,1024]{1,0:T(8,128)(2,1)} %collective-permute-done.7.refs_7_), channel_id=1, source_target_pairs={{4,0},{5,1},{6,2},{7,3},{8,4},{9,5},{10,6},{11,7},{12,8},{13,9},{1... | collective-permute-start | bytes 1179656 | tf_op jit(solution)/shard_map/ppermute | solution.py:260
  80.8 14.6 %collective-permute-start.14 = (bf16[192,1024]{1,0:T(8,128)(2,1)}, bf16[192,1024]{1,0:T(8,128)(2,1)}, u32[]{:S(2)}, u32[]{:S(2)}) collective-permute-start(bf16[192,1024]{1,0:T(8,128)(2,1)} %collective-permute-done.6.refs_6_), channel_id=1, source_target_pairs={{3,0},{0,1},{1,2},{2,3},{7,4},{4,5},{5,6},{6,7},{11,8},{8,9},{9,10... | collective-permute-start | bytes 1179656 | tf_op jit(solution)/shard_map/ppermute | solution.py:260
  83.0 12.5 %collective-permute-start.13 = (bf16[192,1024]{1,0:T(8,128)(2,1)}, bf16[192,1024]{1,0:T(8,128)(2,1)}, u32[]{:S(2)}, u32[]{:S(2)}) collective-permute-start(bf16[192,1024]{1,0:T(8,128)(2,1)} %collective-permute-done.12.refs_12_), channel_id=1, source_target_pairs={{1,0},{2,1},{3,2},{0,3},{5,4},{6,5},{7,6},{4,7},{9,8},{10,9},{11,1... | collective-permute-start | bytes 1179656 | tf_op jit(solution)/shard_map/ppermute | solution.py:260
  126.7 10.0 %collective-permute-start.16 = (bf16[16,48,128]{2,1,0:T(8,128)(2,1)S(1)}, bf16[16,48,128]{2,1,0:T(8,128)(2,1)S(1)}, u32[]{:S(2)}, u32[]{:S(2)}) collective-permute-start(bf16[16,48,128]{2,1,0:T(8,128)(2,1)S(1)} %dynamic-slice_bitcast_fusion), channel_id=1, source_target_pairs={{0,16},{16,0},{32,48},{48,32},{64,80},{80,64},{96,112},{112,96},{1... | collective-permute-start | bytes 589832 | tf_op jit(solution)/shard_map/ppermute | solution.py:241
  131.8 30.6 %all-to-all-start.2 = ((bf16[16,192,256]{2,1,0:T(8,128)(2,1)}), bf16[16,192,256]{2,1,0:T(8,128)(2,1)S(1)}, u32[]{:S(2)}, u32[]{:S(2)}) async-start(bf16[16,192,256]{2,1,0:T(8,128)(2,1)} %bitcast.88), calls=%async_computation.2 | async-start | bytes 3145728 | tf_op jit(solution)/shard_map/all_to_all | solution.py:299
  136.8 6.6 %collective-permute-start.17 = (bf16[8,48,128]{2,1,0:T(8,128)(2,1)S(1)}, bf16[8,48,128]{2,1,0:T(8,128)(2,1)S(1)}, u32[]{:S(2)}, u32[]{:S(2)}) collective-permute-start(bf16[8,48,128]{2,1,0:T(8,128)(2,1)S(1)} %dynamic-slice_bitcast_fusion.1), channel_id=1, source_target_pairs={{0,32},{16,48},{32,0},{48,16},{64,96},{80,112},{96,64},{112,80},{1... | collective-permute-start | bytes 294920 | tf_op jit(solution)/shard_map/ppermute | solution.py:241
  149.5 8.5 %collective-permute-start.19 = (bf16[2,48,128]{2,1,0:T(8,128)(2,1)S(1)}, bf16[2,48,128]{2,1,0:T(8,128)(2,1)S(1)}, u32[]{:S(2)}, u32[]{:S(2)}) collective-permute-start(bf16[2,48,128]{2,1,0:T(8,128)(2,1)S(1)} %dynamic-slice_bitcast_fusion.3), channel_id=1, source_target_pairs={{0,128},{16,144},{32,160},{48,176},{64,192},{80,208},{96,224},{112... | collective-permute-start | bytes 73736 | tf_op jit(solution)/shard_map/ppermute | solution.py:241
  162.4 20.2 %collective-permute-start.20 = (bf16[1,48,128]{2,1,0:T(8,128)(2,1)S(1)}, bf16[1,48,128]{2,1,0:T(8,128)(2,1)S(1)}, u32[]{:S(2)}, u32[]{:S(2)}) collective-permute-start(bf16[1,48,128]{2,1,0:T(8,128)(2,1)S(1)} %constant_dynamic-slice_fusion), channel_id=1, source_target_pairs={{0,256},{16,272},{32,288},{48,304},{64,320},{80,336},{96,352},{112... | collective-permute-start | bytes 36872 | tf_op jit(solution)/shard_map/ppermute | solution.py:241
  (12 other events, 404.0 us)
Sparse Core Ops, SparseCore 0:
  19.7 95.7 all-gather.1
